TPU v7x, 32 devices: a whole 2x2x4 slice. The times are simulated.
32 devices in a mesh: dp: 4 (over z), seq: 8 (over y, x, core).
Axes of the slice: x: 2, y: 2, z: 4, core: 2. Of those that a mesh axis runs over, the one named last changes fastest.
Arguments:
- inputs: bfloat16 [4, 2048, 768], P('dp', 'seq'), may hold values from -6 to 6
- cotangent: float32 [4, 2048, 768], P('dp', 'seq'), may hold values from -6 to 6
- doc_lengths: int32 [4, 8], P('dp'), may hold values from 1 to 1920, 2048 in all within a row
- doc_labels: int32 [4, 8], P('dp'), may hold values from 0 to 2
- query_weight: bfloat16 [768, 768], P('seq'), may hold values from -0.3125 to 0.3125
- query_bias: bfloat16 [768], P('seq'), may hold values from -4 to 4
- key_weight: bfloat16 [768, 768], P('seq'), may hold values from -0.3125 to 0.3125
- value_weight: bfloat16 [768, 768], P('seq'), may hold values from -0.21875 to 0.21875
- value_bias: bfloat16 [768], P('seq'), may hold values from -0.75 to 0.75
- proj_weight: bfloat16 [768, 768], P('seq'), may hold values from -0.625 to 0.625
- proj_bias: bfloat16 [768], P('seq'), may hold values from -4 to 4
- norm_gain: bfloat16 [768], P('seq'), may hold values from 0.099609375 to 1.8984375
- norm_shift: bfloat16 [768], P('seq'), may hold values from -4 to 4
- up_weight: bfloat16 [768, 3072], P('seq'), may hold values from -0.21875 to 0.21875
- up_bias: bfloat16 [3072], P('seq'), may hold values from -4 to 4
- down_weight: bfloat16 [3072, 768], P('seq'), may hold values from -0.109375 to 0.109375
- down_bias: bfloat16 [768], P('seq'), may hold values from -4 to 4
- final_gain: bfloat16 [768], P('seq'), may hold values from 0.099609375 to 1.8984375
- final_shift: bfloat16 [768], P('seq'), may hold values from -4 to 4
- pool_weight: bfloat16 [768, 768], P('seq'), may hold values from -0.21875 to 0.21875
- pool_bias: bfloat16 [768], P('seq'), may hold values from -4 to 4
- class_weight: bfloat16 [768, 3], P('seq'), may hold values from -0.4375 to 0.4375
- class_bias: bfloat16 [3], replicated, may hold values from -6 to 6
Outputs:
- output: bfloat16 [4, 2048, 768], P('dp', 'seq')
- logits: float32 [4, 8, 3], P('dp')
- input_grad: float32 [4, 2048, 768], P('dp', 'seq')
- query_wgrad: float32 [768, 768], P('seq')
- query_bgrad: float32 [768], P('seq')
- key_wgrad: float32 [768, 768], P('seq')
- value_wgrad: float32 [768, 768], P('seq')
- value_bgrad: float32 [768], P('seq')
- proj_wgrad: float32 [768, 768], P('seq')
- proj_bgrad: float32 [768], P('seq')
- norm_ggrad: float32 [768], P('seq')
- norm_sgrad: float32 [768], P('seq')
- up_wgrad: float32 [768, 3072], P('seq')
- up_bgrad: float32 [3072], P('seq')
- down_wgrad: float32 [3072, 768], P('seq')
- down_bgrad: float32 [768], P('seq')
- final_ggrad: float32 [768], P('seq')
- final_sgrad: float32 [768], P('seq')
- pool_wgrad: float32 [768, 768], P('seq')
- pool_bgrad: float32 [768], P('seq')
- class_wgrad: float32 [768, 3], P('seq')
- class_bgrad: float32 [3], replicated
Inputs may be any that keep to these rules, and one draw needn't show every extreme that they name: `doc_lengths`: in each sequence the 8 lengths sum to 2048, and one document has exactly 1920 tokens.
All inputs are finite; a program needn't handle non-finite values.
Results may differ from a plain program's by a relative error of at most 0.025.
Values may be sent and summed in bfloat16 or wider, within the bound.
No kernel may reach another device: no remote copies, remote signals or barrier semaphores. Data moves between devices by JAX's collectives and lax.ppermute only.
A program may use at most 192 MiB of HBM per device.

v0:
```python
import jax
import jax.numpy as jnp
from jax import lax
from jax.sharding import PartitionSpec as P

D = 768
HEADS = 12
HEAD_DIM = 64
CLASSES = 3


epsilon = 1e-06
masked_score = -1e30
param_names = (
    "query_weight",
    "key_weight",
    "value_weight",
    "proj_weight",
    "up_weight",
    "down_weight",
    "pool_weight",
    "class_weight",
    "query_bias",
    "value_bias",
    "proj_bias",
    "norm_gain",
    "norm_shift",
    "up_bias",
    "down_bias",
    "final_gain",
    "final_shift",
    "pool_bias",
)


def layer_norm(value, gain, shift):
    centre = jnp.mean(value, axis=-1, keepdims=True)
    centred = value - centre
    spread = jnp.mean(centred * centred, axis=-1, keepdims=True)
    return centred * lax.rsqrt(spread + epsilon) * gain + shift


def gelu_exact(value):
    return jax.nn.gelu(value, approximate=False)


def segment_of(positions, starts):
    return jnp.sum((positions[:, None] >= starts[None, :]).astype(jnp.int32), axis=1) - 1


def block_size():
    return 512


def block_scores(query_part, query_seg, key_part, key_start, starts):
    key_seg = segment_of(key_start + jnp.arange(key_part.shape[0], dtype=jnp.int32), starts)
    allowed = (query_seg[:, None] == key_seg[None, :])[None]
    scaling = query_part.shape[-1] ** (-0.5)
    scores = (
        jnp.einsum("thd,shd->hts", query_part, key_part, preferred_element_type=jnp.float32)
        * scaling
    )
    return (jnp.where(allowed, scores, masked_score), allowed)


def score_grads(
    query_part,
    query_seg,
    key_part,
    value_part,
    key_start,
    grad_part,
    total_part,
    delta_part,
    starts,
):
    scores, allowed = block_scores(query_part, query_seg, key_part, key_start, starts)
    soft = jnp.where(allowed, jnp.exp(scores - total_part[..., None]), 0.0)
    soft_low = soft.astype(jnp.bfloat16)
    grad_soft = jnp.einsum(
        "thd,shd->hts", grad_part, value_part, preferred_element_type=jnp.float32
    )
    grad_scores = (soft * (grad_soft - delta_part[..., None])).astype(jnp.bfloat16)
    return (soft_low, grad_scores)


def on_device(
    inputs,
    cotangent,
    doc_lengths,
    doc_labels,
    query_weight,
    query_bias,
    key_weight,
    value_weight,
    value_bias,
    proj_weight,
    proj_bias,
    norm_gain,
    norm_shift,
    up_weight,
    up_bias,
    down_weight,
    down_bias,
    final_gain,
    final_shift,
    pool_weight,
    pool_bias,
    class_weight,
    class_bias,
):
    params = dict(
        zip(
            param_names,
            (
                lax.all_gather(query_weight, "seq", axis=0, tiled=True),
                lax.all_gather(key_weight, "seq", axis=0, tiled=True),
                lax.all_gather(value_weight, "seq", axis=0, tiled=True),
                lax.all_gather(proj_weight, "seq", axis=0, tiled=True),
                lax.all_gather(up_weight, "seq", axis=0, tiled=True),
                lax.all_gather(down_weight, "seq", axis=0, tiled=True),
                lax.all_gather(pool_weight, "seq", axis=0, tiled=True),
                lax.all_gather(class_weight, "seq", axis=0, tiled=True),
                lax.all_gather(query_bias, "seq", axis=0, tiled=True),
                lax.all_gather(value_bias, "seq", axis=0, tiled=True),
                lax.all_gather(proj_bias, "seq", axis=0, tiled=True),
                lax.all_gather(norm_gain, "seq", axis=0, tiled=True),
                lax.all_gather(norm_shift, "seq", axis=0, tiled=True),
                lax.all_gather(up_bias, "seq", axis=0, tiled=True),
                lax.all_gather(down_bias, "seq", axis=0, tiled=True),
                lax.all_gather(final_gain, "seq", axis=0, tiled=True),
                lax.all_gather(final_shift, "seq", axis=0, tiled=True),
                lax.all_gather(pool_bias, "seq", axis=0, tiled=True),
            ),
        )
    )
    vectors = {entry: params[entry].astype(jnp.float32) for entry in param_names[8:]}
    tokens = inputs[0]
    local_rows = tokens.shape[0]
    row_start = lax.axis_index("seq") * local_rows
    lengths = doc_lengths[0]
    starts = jnp.cumsum(lengths) - lengths
    positions = row_start + jnp.arange(local_rows, dtype=jnp.int32)
    query_segs = segment_of(positions, starts)
    head_shape = (HEADS, HEAD_DIM)
    scaling = HEAD_DIM ** (-0.5)
    queries = (
        jnp.dot(tokens, params["query_weight"], preferred_element_type=jnp.float32)
        + vectors["query_bias"]
    ).astype(jnp.bfloat16)
    key_rows = jnp.dot(tokens, params["key_weight"], preferred_element_type=jnp.float32).astype(
        jnp.bfloat16
    )
    value_rows = (
        jnp.dot(tokens, params["value_weight"], preferred_element_type=jnp.float32)
        + vectors["value_bias"]
    ).astype(jnp.bfloat16)
    every_key, every_value = (
        lax.all_gather(key_rows, "seq", axis=0, tiled=True),
        lax.all_gather(value_rows, "seq", axis=0, tiled=True),
    )
    all_rows = every_key.shape[0]
    block_rows = block_size()
    blocks = all_rows // block_rows
    key_blocks = every_key.reshape((blocks, block_rows) + head_shape)
    value_blocks = every_value.reshape((blocks, block_rows) + head_shape)
    block_ids = jnp.arange(blocks, dtype=jnp.int32)
    query_heads = queries.reshape((local_rows,) + head_shape)

    def max_step(running, step_in):
        key_part, number = step_in
        scores, allowed = block_scores(
            query_heads, query_segs, key_part, number * block_rows, starts
        )
        new_max = jnp.maximum(running[0], jnp.max(scores, axis=-1))
        weights = jnp.where(allowed, jnp.exp(scores - new_max[..., None]), 0.0)
        return (
            (new_max, running[1] * jnp.exp(running[0] - new_max) + jnp.sum(weights, axis=-1)),
            None,
        )

    first_state = (
        jnp.full((HEADS, local_rows), masked_score, jnp.float32),
        jnp.zeros((HEADS, local_rows), jnp.float32),
    )
    (row_max, row_sum), unused = lax.scan(max_step, first_state, (key_blocks, block_ids))
    log_total = row_max + jnp.log(row_sum)

    def value_step(running, step_in):
        key_part, value_part, number = step_in
        scores, allowed = block_scores(
            query_heads, query_segs, key_part, number * block_rows, starts
        )
        soft_low = jnp.where(allowed, jnp.exp(scores - log_total[..., None]), 0.0).astype(
            jnp.bfloat16
        )
        return (
            running
            + jnp.einsum("hts,shd->thd", soft_low, value_part, preferred_element_type=jnp.float32),
            None,
        )

    attended_sum, unused = lax.scan(
        value_step,
        jnp.zeros((local_rows,) + head_shape, jnp.float32),
        (key_blocks, value_blocks, block_ids),
    )
    attended_sum = attended_sum.reshape(local_rows, D)
    attended = attended_sum.astype(jnp.bfloat16)
    first_residual = (
        tokens.astype(jnp.float32)
        + jnp.dot(attended, params["proj_weight"], preferred_element_type=jnp.float32)
        + vectors["proj_bias"]
    )
    normed, norm_pull = jax.vjp(
        layer_norm, first_residual, vectors["norm_gain"], vectors["norm_shift"]
    )
    normed_low = normed.astype(jnp.bfloat16)
    upward = (
        jnp.dot(normed_low, params["up_weight"], preferred_element_type=jnp.float32)
        + vectors["up_bias"]
    )
    activation_f, gelu_pull = jax.vjp(gelu_exact, upward)
    activation = activation_f.astype(jnp.bfloat16)
    second_residual = (
        normed
        + jnp.dot(activation, params["down_weight"], preferred_element_type=jnp.float32)
        + vectors["down_bias"]
    )
    outcome, final_pull = jax.vjp(
        layer_norm, second_residual, vectors["final_gain"], vectors["final_shift"]
    )
    picker = (starts[:, None] == positions[None, :]).astype(jnp.float32)
    first_rows = lax.psum(jnp.dot(picker, outcome, precision=lax.Precision.HIGHEST), "seq")
    first_low = first_rows.astype(jnp.bfloat16)
    pooled = jnp.tanh(
        jnp.dot(first_low, params["pool_weight"], preferred_element_type=jnp.float32)
        + vectors["pool_bias"]
    )
    pooled_low = pooled.astype(jnp.bfloat16)
    logits = jnp.dot(
        pooled_low, params["class_weight"], preferred_element_type=jnp.float32
    ) + class_bias.astype(jnp.float32)
    onehot = (doc_labels[0][:, None] == jnp.arange(CLASSES, dtype=jnp.int32)[None, :]).astype(
        jnp.float32
    )
    grad_logits = jax.nn.softmax(logits, axis=-1) - onehot
    grad_pooled = jnp.dot(
        grad_logits, params["class_weight"].astype(jnp.float32).T, precision=lax.Precision.HIGHEST
    )
    grad_pre = grad_pooled * (1.0 - pooled * pooled)
    grad_first = jnp.dot(
        grad_pre, params["pool_weight"].astype(jnp.float32).T, precision=lax.Precision.HIGHEST
    )
    pool_wpart = jnp.dot(first_low.astype(jnp.float32).T, grad_pre, precision=lax.Precision.HIGHEST)
    pool_bpart = jnp.sum(grad_pre, axis=0)
    class_wpart = jnp.dot(
        pooled_low.astype(jnp.float32).T, grad_logits, precision=lax.Precision.HIGHEST
    )
    class_bpart = jnp.sum(grad_logits, axis=0)
    matrices = dict(
        zip(
            param_names[:6],
            (
                lax.all_gather(query_weight, "seq", axis=0, tiled=True),
                lax.all_gather(key_weight, "seq", axis=0, tiled=True),
                lax.all_gather(value_weight, "seq", axis=0, tiled=True),
                lax.all_gather(proj_weight, "seq", axis=0, tiled=True),
                lax.all_gather(up_weight, "seq", axis=0, tiled=True),
                lax.all_gather(down_weight, "seq", axis=0, tiled=True),
            ),
        )
    )
    grad_outcome = cotangent[0] + jnp.dot(picker.T, grad_first, precision=lax.Precision.HIGHEST)
    grad_second, final_gpart, final_spart = final_pull(grad_outcome)
    grad_down = grad_second.astype(jnp.bfloat16)
    down_wpart = jnp.dot(activation.T, grad_down, preferred_element_type=jnp.float32)
    down_bpart = jnp.sum(grad_second, axis=0)
    grad_activation = jnp.dot(
        grad_down, matrices["down_weight"].T, preferred_element_type=jnp.float32
    ).astype(jnp.bfloat16)
    (grad_upward,) = gelu_pull(grad_activation.astype(jnp.float32))
    grad_up_low = grad_upward.astype(jnp.bfloat16)
    up_wpart = jnp.dot(normed_low.T, grad_up_low, preferred_element_type=jnp.float32)
    up_bpart = jnp.sum(grad_upward, axis=0)
    grad_normed = grad_second + jnp.dot(
        grad_up_low, matrices["up_weight"].T, preferred_element_type=jnp.float32
    ).astype(jnp.bfloat16).astype(jnp.float32)
    grad_first_res, norm_gpart, norm_spart = norm_pull(grad_normed)
    grad_proj = grad_first_res.astype(jnp.bfloat16)
    proj_wpart = jnp.dot(attended.T, grad_proj, preferred_element_type=jnp.float32)
    proj_bpart = jnp.sum(grad_first_res, axis=0)
    grad_attended = jnp.dot(
        grad_proj, matrices["proj_weight"].T, preferred_element_type=jnp.float32
    ).astype(jnp.bfloat16)
    grad_heads = grad_attended.reshape((local_rows,) + head_shape)
    row_delta = jnp.sum(
        (grad_attended.astype(jnp.float32) * attended_sum).reshape((local_rows,) + head_shape),
        axis=-1,
    ).T
    zero_heads = jnp.zeros((local_rows,) + head_shape, jnp.float32)

    def grad_step(running, step_in):
        key_part, value_part, number = step_in
        soft_low, grad_scores = score_grads(
            query_heads,
            query_segs,
            key_part,
            value_part,
            number * block_rows,
            grad_heads,
            log_total,
            row_delta,
            starts,
        )
        running = (
            running
            + jnp.einsum("hts,shd->thd", grad_scores, key_part, preferred_element_type=jnp.float32)
            * scaling
        )
        key_term = (
            jnp.einsum("hts,thd->shd", grad_scores, query_heads, preferred_element_type=jnp.float32)
            * scaling
        )
        value_term = jnp.einsum(
            "hts,thd->shd", soft_low, grad_heads, preferred_element_type=jnp.float32
        )
        return (
            running,
            jnp.concatenate(
                [key_term.reshape(block_rows, D), value_term.reshape(block_rows, D)], axis=1
            ),
        )

    query_sum, terms = lax.scan(grad_step, zero_heads, (key_blocks, value_blocks, block_ids))
    pair_grads = lax.psum_scatter(
        terms.reshape(all_rows, 2 * D).astype(jnp.bfloat16), "seq", scatter_dimension=0, tiled=True
    ).astype(jnp.float32)
    query_grad = query_sum.reshape(local_rows, D).astype(jnp.bfloat16)
    key_grad = pair_grads[:, :D].astype(jnp.bfloat16)
    value_grad = pair_grads[:, D:].astype(jnp.bfloat16)
    query_wpart = jnp.dot(tokens.T, query_grad, preferred_element_type=jnp.float32)
    key_wpart = jnp.dot(tokens.T, key_grad, preferred_element_type=jnp.float32)
    value_wpart = jnp.dot(tokens.T, value_grad, preferred_element_type=jnp.float32)
    query_bpart = jnp.sum(query_grad.astype(jnp.float32), axis=0)
    value_bpart = jnp.sum(value_grad.astype(jnp.float32), axis=0)
    input_grad = grad_first_res + jnp.dot(
        query_grad, matrices["query_weight"].T, preferred_element_type=jnp.float32
    )
    input_grad = input_grad + jnp.dot(
        key_grad, matrices["key_weight"].T, preferred_element_type=jnp.float32
    )
    input_grad = input_grad + jnp.dot(
        value_grad, matrices["value_weight"].T, preferred_element_type=jnp.float32
    )
    grouped = (
        lax.psum_scatter(
            query_wpart.astype(jnp.bfloat16), "seq", scatter_dimension=0, tiled=True
        ).astype(jnp.float32),
        lax.psum_scatter(
            key_wpart.astype(jnp.bfloat16), "seq", scatter_dimension=0, tiled=True
        ).astype(jnp.float32),
        lax.psum_scatter(
            value_wpart.astype(jnp.bfloat16), "seq", scatter_dimension=0, tiled=True
        ).astype(jnp.float32),
        lax.psum_scatter(
            proj_wpart.astype(jnp.bfloat16), "seq", scatter_dimension=0, tiled=True
        ).astype(jnp.float32),
        lax.psum_scatter(
            up_wpart.astype(jnp.bfloat16), "seq", scatter_dimension=0, tiled=True
        ).astype(jnp.float32),
        lax.psum_scatter(
            down_wpart.astype(jnp.bfloat16), "seq", scatter_dimension=0, tiled=True
        ).astype(jnp.float32),
        lax.psum_scatter(
            query_bpart.astype(jnp.bfloat16), "seq", scatter_dimension=0, tiled=True
        ).astype(jnp.float32),
        lax.psum_scatter(
            value_bpart.astype(jnp.bfloat16), "seq", scatter_dimension=0, tiled=True
        ).astype(jnp.float32),
        lax.psum_scatter(
            proj_bpart.astype(jnp.bfloat16), "seq", scatter_dimension=0, tiled=True
        ).astype(jnp.float32),
        lax.psum_scatter(
            norm_gpart.astype(jnp.bfloat16), "seq", scatter_dimension=0, tiled=True
        ).astype(jnp.float32),
        lax.psum_scatter(
            norm_spart.astype(jnp.bfloat16), "seq", scatter_dimension=0, tiled=True
        ).astype(jnp.float32),
        lax.psum_scatter(
            up_bpart.astype(jnp.bfloat16), "seq", scatter_dimension=0, tiled=True
        ).astype(jnp.float32),
        lax.psum_scatter(
            down_bpart.astype(jnp.bfloat16), "seq", scatter_dimension=0, tiled=True
        ).astype(jnp.float32),
        lax.psum_scatter(
            final_gpart.astype(jnp.bfloat16), "seq", scatter_dimension=0, tiled=True
        ).astype(jnp.float32),
        lax.psum_scatter(
            final_spart.astype(jnp.bfloat16), "seq", scatter_dimension=0, tiled=True
        ).astype(jnp.float32),
    )
    share = D // lax.axis_size("seq")
    share_start = lax.axis_index("seq") * share
    pool_wshard = lax.dynamic_slice_in_dim(pool_wpart, share_start, share, 0)
    pool_bshard = lax.dynamic_slice_in_dim(pool_bpart, share_start, share, 0)
    class_wshard = lax.dynamic_slice_in_dim(class_wpart, share_start, share, 0)
    summed = (
        lax.psum(grouped[0].astype(jnp.bfloat16), "dp").astype(jnp.float32),
        lax.psum(grouped[1].astype(jnp.bfloat16), "dp").astype(jnp.float32),
        lax.psum(grouped[2].astype(jnp.bfloat16), "dp").astype(jnp.float32),
        lax.psum(grouped[3].astype(jnp.bfloat16), "dp").astype(jnp.float32),
        lax.psum(grouped[4].astype(jnp.bfloat16), "dp").astype(jnp.float32),
        lax.psum(grouped[5].astype(jnp.bfloat16), "dp").astype(jnp.float32),
        lax.psum(grouped[6].astype(jnp.bfloat16), "dp").astype(jnp.float32),
        lax.psum(grouped[7].astype(jnp.bfloat16), "dp").astype(jnp.float32),
        lax.psum(grouped[8].astype(jnp.bfloat16), "dp").astype(jnp.float32),
        lax.psum(grouped[9].astype(jnp.bfloat16), "dp").astype(jnp.float32),
        lax.psum(grouped[10].astype(jnp.bfloat16), "dp").astype(jnp.float32),
        lax.psum(grouped[11].astype(jnp.bfloat16), "dp").astype(jnp.float32),
        lax.psum(grouped[12].astype(jnp.bfloat16), "dp").astype(jnp.float32),
        lax.psum(grouped[13].astype(jnp.bfloat16), "dp").astype(jnp.float32),
        lax.psum(grouped[14].astype(jnp.bfloat16), "dp").astype(jnp.float32),
        lax.psum(pool_wshard.astype(jnp.bfloat16), "dp").astype(jnp.float32),
        lax.psum(pool_bshard.astype(jnp.bfloat16), "dp").astype(jnp.float32),
        lax.psum(class_wshard.astype(jnp.bfloat16), "dp").astype(jnp.float32),
        lax.psum(class_bpart.astype(jnp.bfloat16), "dp").astype(jnp.float32),
    )
    return (
        outcome.astype(jnp.bfloat16)[None],
        logits[None],
        input_grad[None],
        summed[0],
        summed[6],
        summed[1],
        summed[2],
        summed[7],
        summed[3],
        summed[8],
        summed[9],
        summed[10],
        summed[4],
        summed[11],
        summed[5],
        summed[12],
        summed[13],
        summed[14],
        summed[15],
        summed[16],
        summed[17],
        summed[18],
    )


def solution(mesh):
    in_specs = (
        P("dp", "seq", None),
        P("dp", "seq", None),
        P("dp", None),
        P("dp", None),
        P("seq", None),
        P("seq"),
        P("seq", None),
        P("seq", None),
        P("seq"),
        P("seq", None),
        P("seq"),
        P("seq"),
        P("seq"),
        P("seq", None),
        P("seq"),
        P("seq", None),
        P("seq"),
        P("seq"),
        P("seq"),
        P("seq", None),
        P("seq"),
        P("seq", None),
        P(),
    )
    out_specs = (
        P("dp", "seq", None),
        P("dp", None, None),
        P("dp", "seq", None),
        P("seq", None),
        P("seq"),
        P("seq", None),
        P("seq", None),
        P("seq"),
        P("seq", None),
        P("seq"),
        P("seq"),
        P("seq"),
        P("seq", None),
        P("seq"),
        P("seq", None),
        P("seq"),
        P("seq"),
        P("seq"),
        P("seq", None),
        P("seq"),
        P("seq", None),
        P(),
    )
    return jax.shard_map(
        on_device, mesh=mesh, in_specs=in_specs, out_specs=out_specs, check_vma=False
    )
```

profile of v0, /device:TPU:0, one launch (start us, length us, event | category | flops | bytes accessed | tf_op | source)
XLA Modules:
  0.0 853.1 jit_solution(13978584704329422735)
XLA Ops:
  9.5 27.2 %all-gather.16.cloned.1.call-done = bf16[768,768]{1,0:T(8,128)(2,1)} async-done(((bf16[96,768]{1,0:T(8,128)(2,1)}), bf16[768,768]{1,0:T(8,128)(2,1)}) %all-gather.16.cloned.1.call-update) | async-done | bytes 1179664 | tf_op jit(solution)/shard_map/all_gather | solution.py:117
  48.9 23.7 %all-reduce.19 = (bf16[768]{0:T(1024)(128)(2,1)S(1)}, bf16[768]{0:T(1024)(128)(2,1)S(1)}, bf16[768]{0:T(1024)(128)(2,1)S(1)}, bf16[768]{0:T(1024)(128)(2,1)S(1)}...) all-reduce(bf16[768]{0:T(1024)(128)(2,1)S(1)} %dynamic-update-slice, ...), channel_id=1, replica_groups=mesh['dp'=4,'seq'=8] {'seq'}, use_global_device_ids=true, to_apply=%add.2 | all-reduce | flops 6912 | bytes 27648
  81.3 8.8 %all-gather = bf16[8,1,384]{2,1,0:T(2,128)(2,1)S(1)} all-gather(bf16[1,1,384]{2,1,0:T(2,128)(2,1)S(1)} %reshape.333), channel_id=1, replica_groups=mesh['dp'=4,'seq'=8] {'seq'}, dimensions={0}, use_global_device_ids=true | all-gather | bytes 6912 | tf_op jit(solution)/shard_map/all_gather | solution.py:129
  93.1 8.1 all-gather.1
  104.4 19.1 %all-gather.18.cloned.1.call-done = bf16[2048,768]{1,0:T(8,128)(2,1)} async-done(((bf16[256,768]{1,0:T(8,128)(2,1)}), bf16[2048,768]{1,0:T(8,128)(2,1)}) %all-gather.18.cloned.1.call-update) | async-done | bytes 3145744 | tf_op jit(solution)/shard_map/all_gather | solution.py:159
  130.7 4.4 copy.111
  135.1 48.4 %while.43 = (s32[]{:T(128)}, f32[12,256]{1,0:T(8,128)S(1)}, f32[12,256]{1,0:T(8,128)S(1)}, s32[256]{0:T(256)}, s32[4]{0:T(128)S(1)}, /*index=5*/s32[8]{0:T(128)}...) while((s32[]{:T(128)}, f32[12,256]{1,0:T(8,128)S(1)}, ...), condition=%wide.region_6.7_spmd.clone, body=%wide.region_2.6_spmd.clone.sunk | while | flops 214068736 | bytes 14329524 | solution.py:186
  137.9 4.9 fusion.192
  150.0 4.9 fusion.192
  154.9 4.3 select_reduce_fusion.2
  162.1 4.9 fusion.192
  174.2 4.9 fusion.192
  191.2 4.6 copy.110
  196.5 26.1 %while.44 = (s32[]{:T(128)}, f32[256,12,64]{0,2,1:T(8,128)S(1)}, bf16[4,512,12,64]{1,3,2,0:T(8,128)(2,1)}, s32[256]{0:T(256)}, s32[4]{0:T(128)S(1)}, /*index=5*/...) while((s32[]{:T(128)}, f32[256,12,64]{0,2,1:T(8,128)S(1)}, ...), condition=%wide.region_9.10_spmd.clone, body=%wide.region_7.9_spmd.clone.sunk | while | flops 411054592 | bytes 3831995 | solution.py:203
  225.2 11.9 %multiply_convert_fusion = (bf16[256,3072]{1,0:T(8,128)(2,1)}, f32[256,3072]{1,0:T(8,128)}, f32[256,3072]{1,0:T(8,128)}) fusion(f32[3072]{0:T(1024)S(1)} %bitcast.242, bf16[768,3072]{1,0:T(8,128)(2,1)} %all-gather.24.cloned.1.call-done, f32[256,768]{1,0:T(8,128)S(1)} %get-tuple-element.809, f32[768]{0:T(1024)S(1)} %copy-done.31, f32[768]{0:T(1024)S(1)} %copy-done.28, ...), kind=kOutput, calls=%fused_computation.82 | convolution fusion | flops 1260847104 | bytes 13389824 | tf_op jit(solution)/shard_map/dot_general | solution.py:220
  237.0 28.6 %all-gather.26.cloned.1.call-done = bf16[3072,768]{1,0:T(8,128)(2,1)} async-done(((bf16[384,768]{1,0:T(8,128)(2,1)}), bf16[3072,768]{1,0:T(8,128)(2,1)}) %all-gather.26.cloned.1.call-update) | async-done | bytes 4718608 | tf_op jit(solution)/shard_map/all_gather | solution.py:121
  265.7 4.3 fusion.126
  271.5 23.7 %psum.140 = bf16[8,768]{1,0:T(8,128)(2,1)S(1)} all-reduce(f32[8,768]{1,0:T(8,128)S(1)} %fusion.81), channel_id=1, replica_groups=mesh['dp'=4,'seq'=8] {'seq'}, use_global_device_ids=true, to_apply=%region_14.15 | all-reduce | flops 6144 | bytes 36864 | tf_op jit(solution)/shard_map/psum | solution.py:234
  304.7 6.1 fusion.128
  317.3 88.9 %while.45 = (s32[]{:T(128)}, f32[256,12,64]{0,2,1:T(8,128)}, bf16[4,512,1536]{2,1,0:T(8,128)(2,1)}, bf16[4,512,12,64]{1,3,2,0:T(8,128)(2,1)}, s32[256]{0:T(256)}...) while((s32[]{:T(128)}, f32[256,12,64]{0,2,1:T(8,128)}, ...), condition=%wide.region_24.25_spmd.clone, body=%wide.region_22.24_spmd.clone.sunk | while | flops 1030173184 | bytes 46898440 | solution.py:335
  410.9 57.2 %reduce-scatter.14.cloned.1.call-done = bf16[256,1536]{1,0:T(8,128)(2,1)} async-done(((bf16[2048,1536]{1,0:T(8,128)(2,1)}), bf16[256,1536]{1,0:T(8,128)(2,1)}) %reduce-scatter.14.cloned.1.call-update) | async-done | bytes 786448 | tf_op jit(solution)/shard_map/reduce_scatter | solution.py:336
  477.7 5.0 convolution_convert_fusion
  483.9 5.2 convolution_convert_fusion.1
  491.7 17.3 %reduce-scatter.22.cloned.1.call-done = bf16[96,768]{1,0:T(8,128)(2,1)} async-done(((bf16[768,768]{1,0:T(8,128)(2,1)}), bf16[96,768]{1,0:T(8,128)(2,1)}) %reduce-scatter.22.cloned.1.call-update) | async-done | bytes 147472
  510.8 38.7 %reduce-scatter.24.cloned.1.call-done = bf16[96,768]{1,0:T(8,128)(2,1)} async-done(((bf16[768,768]{1,0:T(8,128)(2,1)}), bf16[96,768]{1,0:T(8,128)(2,1)}) %reduce-scatter.24.cloned.1.call-update) | async-done | bytes 147472
  551.2 38.6 %reduce-scatter.26.cloned.1.call-done = bf16[96,768]{1,0:T(8,128)(2,1)} async-done(((bf16[768,768]{1,0:T(8,128)(2,1)}), bf16[96,768]{1,0:T(8,128)(2,1)}) %reduce-scatter.26.cloned.1.call-update) | async-done | bytes 147472
  591.5 38.1 %reduce-scatter.16.cloned.1.call-done = bf16[96,768]{1,0:T(8,128)(2,1)} async-done(((bf16[768,768]{1,0:T(8,128)(2,1)}), bf16[96,768]{1,0:T(8,128)(2,1)}) %reduce-scatter.16.cloned.1.call-update) | async-done | bytes 147472 | tf_op jit(solution)/shard_map/reduce_scatter | solution.py:366
  629.7 57.6 %reduce-scatter.20.cloned.1.call-done = bf16[384,768]{1,0:T(8,128)(2,1)} async-done(((bf16[3072,768]{1,0:T(8,128)(2,1)}), bf16[384,768]{1,0:T(8,128)(2,1)}) %reduce-scatter.20.cloned.1.call-update) | async-done | bytes 589840 | tf_op jit(solution)/shard_map/reduce_scatter | solution.py:372
  687.3 57.2 %reduce-scatter.18.cloned.1.call-done = bf16[96,3072]{1,0:T(8,128)(2,1)} async-done(((bf16[768,3072]{1,0:T(8,128)(2,1)}), bf16[96,3072]{1,0:T(8,128)(2,1)}) %reduce-scatter.18.cloned.1.call-update) | async-done | bytes 589840 | tf_op jit(solution)/shard_map/reduce_scatter | solution.py:369
  753.6 25.4 %all-reduce.18 = (bf16[768]{0:T(1024)(128)(2,1)S(1)}, bf16[768]{0:T(1024)(128)(2,1)S(1)}, bf16[768]{0:T(1024)(128)(2,1)S(1)}, bf16[768]{0:T(1024)(128)(2,1)S(1)}...) all-reduce(bf16[768]{0:T(1024)(128)(2,1)S(1)} %reduce_sum.298, ...), channel_id=4, replica_groups=mesh['dp'=4,'seq'=8] {'seq'}, use_global_device_ids=true, to_apply=%region_29.30.clone | all-reduce | flops 9216 | bytes 36864
  779.7 12.8 %all-reduce.20 = (bf16[96]{0:T(256)(128)(2,1)S(1)}, bf16[96]{0:T(256)(128)(2,1)S(1)}, bf16[96]{0:T(256)(128)(2,1)S(1)}, bf16[96]{0:T(256)(128)(2,1)S(1)}, bf16[9...) all-reduce(bf16[96]{0:T(256)(128)(2,1)S(1)} %dynamic-slice.10, ...), channel_id=1, replica_groups=mesh['dp'=4,'seq'=8] {'dp'}, use_global_device_ids=true, to_apply=%region_30.31 | all-reduce | flops 1539 | bytes 6156 | tf_op jit(solution)/shard_map/psum | solution.py:415
  800.7 37.2 %all-reduce.24.cloned.1.call-done = (bf16[96,768]{0,1:T(8,128)(2,1)}, bf16[96,768]{0,1:T(8,128)(2,1)}, bf16[96,768]{0,1:T(8,128)(2,1)}, bf16[96,768]{1,0:T(8,128...) async-done(((bf16[96,768]{0,1:T(8,128)(2,1)}, bf16[96,768]{0,1:T(8,128)(2,1)}, bf16[96,768]{0,1:T(8,128)(2,1)}, ...) | async-done | bytes 1916944 | tf_op jit(solution)/shard_map/psum | solution.py:409
  (423 shorter events, 242.3 us)
Async XLA Ops:
  7.2 29.5 %all-gather.16.cloned.1.call-start = ((), (), s32[]{:S(2)}) async-start(), calls=%async_computation.9 | async-start | bytes 1327104 | tf_op jit(solution)/shard_map/all_gather | solution.py:117
  7.9 64.7 %all-gather.12.cloned.1.call-start = ((), (), s32[]{:S(2)}) async-start(), calls=%async_computation.7 | async-start | bytes 1327104 | tf_op jit(solution)/shard_map/all_gather | solution.py:118
  8.7 93.8 %all-gather.20.cloned.1.call-start = ((), (), s32[]{:S(2)}) async-start(), calls=%async_computation.11 | async-start | bytes 1327104 | tf_op jit(solution)/shard_map/all_gather | solution.py:116
  9.4 68.7 %copy-start.57 = (s32[1,8]{1,0:T(1,128)S(1)}, s32[1,8]{1,0:T(1,128)}, u32[]{:S(2)}) copy-start(s32[1,8]{1,0:T(1,128)} %param.31) | copy-start | bytes 100
  9.4 71.9 %copy-start.54 = (bf16[384]{0:T(512)(128)(2,1)S(1)}, bf16[384]{0:T(512)(128)(2,1)}, u32[]{:S(2)}) copy-start(bf16[384]{0:T(512)(128)(2,1)} %param.43) | copy-start | bytes 2308
  9.4 83.7 %copy-start.53 = (bf16[96,3]{0,1:T(4,128)(2,1)S(1)}, bf16[96,3]{0,1:T(4,128)(2,1)}, u32[]{:S(2)}) copy-start(bf16[96,3]{0,1:T(4,128)(2,1)} %param.50) | copy-start | bytes 1732
  9.4 92.5 %copy-start.58 = (bf16[3]{0:T(256)(128)(2,1)S(1)}, bf16[3]{0:T(256)(128)(2,1)}, u32[]{:S(2)}) copy-start(bf16[3]{0:T(256)(128)(2,1)} %param.51) | copy-start | bytes 22
  9.5 93.0 %copy-start.5 = (bf16[1,256,768]{2,1,0:T(8,128)(2,1)S(1)}, bf16[1,256,768]{2,1,0:T(8,128)(2,1)}, u32[]{:S(2)}) copy-start(bf16[1,256,768]{2,1,0:T(8,128)(2,1)} %param.29) | copy-start | bytes 1179652
  9.5 114.0 %all-gather.18.cloned.1.call-start = ((), (), s32[]{:S(2)}) async-start(), calls=%async_computation.10 | async-start | bytes 3538944 | tf_op jit(solution)/shard_map/all_gather | solution.py:159
  39.4 144.7 %all-gather.14.cloned.1.call-start = ((), (), s32[]{:S(2)}) async-start(), calls=%async_computation.8 | async-start | bytes 3538944 | tf_op jit(solution)/shard_map/all_gather | solution.py:160
  75.3 147.7 %all-gather.22.cloned.1.call-start = ((), (), s32[]{:S(2)}) async-start(), calls=%async_computation.12 | async-start | bytes 1327104 | tf_op jit(solution)/shard_map/all_gather | solution.py:119
  75.8 149.3 %all-gather.24.cloned.1.call-start = ((), (), s32[]{:S(2)}) async-start(), calls=%async_computation.13 | async-start | bytes 5308416 | tf_op jit(solution)/shard_map/all_gather | solution.py:120
  76.6 189.1 %all-gather.26.cloned.1.call-start = ((), (), s32[]{:S(2)}) async-start(), calls=%async_computation.14 | async-start | bytes 5308416 | tf_op jit(solution)/shard_map/all_gather | solution.py:121
  77.3 217.9 %all-gather.28.cloned.1.call-start = ((), (), s32[]{:S(2)}) async-start(), calls=%async_computation.15 | async-start | bytes 1327104 | tf_op jit(solution)/shard_map/all_gather | solution.py:122
  78.1 390.0 %reduce-scatter.14.cloned.1.call-start = ((), (), s32[]{:S(2)}) async-start(), calls=%async_computation.16 | async-start | bytes 7077888 | tf_op jit(solution)/shard_map/reduce_scatter | solution.py:336
  224.8 88.3 %copy-start.3 = (f32[256,768]{1,0:T(8,128)}, f32[256,768]{1,0:T(8,128)S(1)}, u32[]{:S(2)}) copy-start(f32[256,768]{1,0:T(8,128)S(1)} %get-tuple-element.809) | copy-start | bytes 2359300
  224.8 88.3 %copy-start.37 = (f32[256]{0:T(256)}, f32[256]{0:T(256)S(1)}, u32[]{:S(2)}) copy-start(f32[256]{0:T(256)S(1)} %broadcast_multiply_fusion.1) | copy-start | bytes 3076
  225.1 88.1 %copy-start.45 = (f32[256]{0:T(256)}, f32[256]{0:T(256)S(1)}, u32[]{:S(2)}) copy-start(f32[256]{0:T(256)S(1)} %fusion.114) | copy-start | bytes 3076
  225.1 40.5 %copy-start.52 = (f32[768]{0:T(1024)S(1)}, f32[768]{0:T(1024)}, u32[]{:S(2)}) copy-start(f32[768]{0:T(1024)} %convert_element_type.319) | copy-start | bytes 9220
  265.7 29.6 %copy-start.42 = (f32[768]{0:T(1024)S(1)}, f32[768]{0:T(1024)}, u32[]{:S(2)}) copy-start(f32[768]{0:T(1024)} %convert_element_type.324) | copy-start | bytes 9220
  265.7 31.1 %copy-start.39 = (bf16[768,3]{0,1:T(4,128)(2,1)S(1)}, bf16[768,3]{0,1:T(4,128)(2,1)}, u32[]{:S(2)}) copy-start(bf16[768,3]{0,1:T(4,128)(2,1)} %reshape.336) | copy-start | bytes 13828
  265.7 31.1 %copy-start.59 = (f32[3]{0:T(128)S(1)}, f32[3]{0:T(128)}, u32[]{:S(2)}) copy-start(f32[3]{0:T(128)} %convert_element_type.326) | copy-start | bytes 40
  265.7 31.3 %copy-start.55 = (s32[1,8]{1,0:T(1,128)S(1)}, s32[1,8]{1,0:T(1,128)}, u32[]{:S(2)}) copy-start(s32[1,8]{1,0:T(1,128)} %param.32) | copy-start | bytes 100
  406.3 102.8 %reduce-scatter.22.cloned.1.call-start = ((), (), s32[]{:S(2)}) async-start(), calls=%async_computation.20 | async-start | bytes 1327104
  410.8 138.6 %reduce-scatter.24.cloned.1.call-start = ((), (), s32[]{:S(2)}) async-start(), calls=%async_computation.21 | async-start | bytes 1327104
  471.1 118.7 %reduce-scatter.26.cloned.1.call-start = ((), (), s32[]{:S(2)}) async-start(), calls=%async_computation.22 | async-start | bytes 1327104
  475.2 154.5 %reduce-scatter.16.cloned.1.call-start = ((), (), s32[]{:S(2)}) async-start(), calls=%async_computation.17 | async-start | bytes 1327104 | tf_op jit(solution)/shard_map/reduce_scatter | solution.py:366
  477.6 209.7 %reduce-scatter.20.cloned.1.call-start = ((), (), s32[]{:S(2)}) async-start(), calls=%async_computation.19 | async-start | bytes 5308416 | tf_op jit(solution)/shard_map/reduce_scatter | solution.py:372
  482.8 261.8 %reduce-scatter.18.cloned.1.call-start = ((), (), s32[]{:S(2)}) async-start(), calls=%async_computation.18 | async-start | bytes 5308416 | tf_op jit(solution)/shard_map/reduce_scatter | solution.py:369
  489.1 261.6 %copy-start.36 = (f32[256]{0:T(256)S(1)}, f32[256]{0:T(256)}, u32[]{:S(2)}) copy-start(f32[256]{0:T(256)} %copy-done.35) | copy-start | bytes 3076
  489.1 348.8 %all-reduce.24.cloned.1.call-start = ((), (), s32[]{:S(2)}) async-start(), calls=%async_computation.23 | async-start | bytes 4128768 | tf_op jit(solution)/shard_map/psum | solution.py:409
  744.5 54.3 %copy-start.14 = (bf16[768,768]{1,0:T(8,128)(2,1)S(1)}, bf16[768,768]{1,0:T(8,128)(2,1)}, u32[]{:S(2)}) copy-start(bf16[768,768]{1,0:T(8,128)(2,1)} %all-gather.16.cloned.1.call-done) | copy-start | bytes 3538948
  (53 other events, 275.5 us)
Sparse Core Ops, SparseCore 0:
  9.9 26.7 all-gather.15
  38.6 24.1 all-gather.11
  64.7 24.1 all-gather.19
  91.2 32.2 all-gather.17
  125.8 32.3 all-gather.13
  159.9 24.0 all-gather.21
  185.9 38.9 all-gather.23
  226.7 38.8 all-gather.25
  267.5 24.1 all-gather.27
  406.4 61.6 reduce-scatter.13
  472.2 36.7 reduce-scatter.21
  512.7 36.7 reduce-scatter.23
  553.0 36.7 reduce-scatter.25
  592.9 36.7 reduce-scatter.15
  633.4 53.8 reduce-scatter.19
  690.6 53.8 reduce-scatter.17
  749.3 88.5 all-reduce.23
where the time goes:
time: 859 us; the launch traced here: 853 us
  waiting for transfers between devices  422 us (49%)
  matrix products  148 us (17%)
  blocking collectives  103 us (12%)
  local copies, waits for them, and re-layouts  88.5 us (10%)
  other arithmetic  65.6 us (8%)
  between operations  17 us (2%)
  loops' own time  8.78 us (1%)
    unnamed x20, waiting for transfers between devices  99.5 us
    reduce_scatter x1, waiting for transfers between devices, on_device(): lax.psum_scatter(down_wpart.astype(jnp.bfloat16), 'seq', scatter_dimensio...  57.6 us
    reduce_scatter x1, waiting for transfers between devices, on_device(): lax.psum_scatter(up_wpart.astype(jnp.bfloat16), 'seq', scatter_dimension=...  57.2 us
    reduce_scatter x1, waiting for transfers between devices, on_device(): lax.psum_scatter(terms.reshape(all_rows, 2 * D).astype(jnp.bfloat16), 'se...  57.2 us
    unnamed x2, blocking collectives  49 us
    reduce_scatter x1, waiting for transfers between devices, on_device(): lax.psum_scatter(proj_wpart.astype(jnp.bfloat16), 'seq', scatter_dimensio...  38.1 us
    unnamed x162, local copies, waits for them, and re-layouts  37.9 us
    psum x1, waiting for transfers between devices, on_device(): lax.psum(grouped[0].astype(jnp.bfloat16), 'dp').astype(jnp.float32)  37.2 us
  transfers between devices with their start and end apart: 17, of which 11 were waited for; matrix products, arithmetic and copies ran while one was open for 21% of the time, Pallas kernels for 0%

commit v1 on v0

v1 whole, which is shorter than its diff:
```python
import functools

import jax
import jax.numpy as jnp
from jax import lax
from jax.experimental import pallas as pl
from jax.experimental.pallas import tpu as pltpu
from jax.sharding import PartitionSpec as P

D = 768
HEADS = 12
HEAD_DIM = 64
FF = 3072
CLASSES = 3
PAIR = 2 * HEAD_DIM
ROWS = 256
EPSILON = 1e-06
FAR = -1e30
LIMIT = 56 * 1024 * 1024
F32, BF16 = jnp.float32, jnp.bfloat16

QUERY_B, VALUE_B, PROJ_B, NORM_G, NORM_S, DOWN_B, FINAL_G, FINAL_S, POOL_B, CLASS_W, UP_B = (
    0, 1, 2, 3, 4, 5, 6, 7, 8, 9, 12,
)
TABLE = 16


def swap(value, partner):
    dp, seq = lax.axis_size("dp"), lax.axis_size("seq")
    pairs = []
    for z in range(dp):
        for i in range(seq):
            to_z, to_i = partner(z, i)
            pairs.append((z * seq + i, to_z * seq + to_i))
    return lax.ppermute(value, ("dp", "seq"), pairs)


def along(bit):
    return lambda z, i: (z, i ^ bit)


def is_small():
    return lax.axis_size("seq") == 8 and lax.axis_size("dp") == 4


def gather_shared(shard, role):
    me, z = lax.axis_index("seq"), lax.axis_index("dp")
    if not is_small():
        whole = lax.all_gather(shard, "seq", axis=shard.ndim - 2, tiled=True)
        return [whole], [jnp.int32(0)]
    one = swap(shard, lambda z, i: (z, i ^ (2 if (z + role) % 2 == 0 else 4)))
    both = swap(one, lambda z, i: (z, i ^ (4 if (z + role) % 2 == 0 else 2)))
    other = swap(one, lambda z, i: (z ^ 1, i))
    near = jnp.where((z + role) % 2 == 0, 2, 4)
    blocks = [shard, one, both, other]
    owners = [me, me ^ near, me ^ 6, me ^ (6 - near)]
    blocks += [swap(block, along(1)) for block in blocks]
    owners += [owner ^ 1 for owner in owners]
    return blocks, owners


def gather_own(shard, order):
    if not is_small():
        return [lax.all_gather(shard, "seq", axis=0)]
    near = {2: swap(shard, along(order[0]))}
    near = {order[0]: near[2], order[1]: swap(shard, along(order[1]))}
    both = swap(near[order[0]], along(order[1]))
    blocks = [shard, near[4], near[2], both]
    return blocks + [swap(block, along(1)) for block in blocks]


def slot_owners():
    if not is_small():
        return jnp.arange(lax.axis_size("seq"), dtype=jnp.int32)
    return lax.axis_index("seq") ^ jnp.array([0, 4, 2, 6, 1, 5, 3, 7], jnp.int32)


def scatter_sum(parts, order):
    if not is_small():
        (part,) = parts
        return lax.psum_scatter(part, "seq", scatter_dimension=0, tiled=True)[0].astype(F32)
    keep, away = parts
    come = swap(away, along(1))
    if order == (2, 4):
        last, far = 1, slice(2, 4)
    else:
        last, far = 2, slice(1, 4, 2)
    send = (keep[far].astype(F32) + come[far].astype(F32)).astype(BF16)
    second = swap(send, along(order[0]))
    send = (
        keep[last].astype(F32) + come[last].astype(F32) + second[1].astype(F32)
    ).astype(BF16)
    third = swap(send, along(order[1]))
    return (
        keep[0].astype(F32) + come[0].astype(F32) + second[0].astype(F32) + third.astype(F32)
    )


def sum_dp(shard):
    if not is_small():
        return lax.psum(shard.astype(BF16), "dp").astype(F32)
    z = lax.axis_index("dp")
    half = shard.shape[0] // 2
    low = jnp.logical_or(z == 0, z == 3)
    first, second = shard[:half], shard[half:]
    keep, away = jnp.where(low, first, second), jnp.where(low, second, first)
    come = swap(away.astype(BF16), lambda z, i: (z ^ 1, i))
    pair = (keep + come.astype(F32)).astype(BF16)
    cross = swap(pair, lambda z, i: (z ^ 3, i))
    total = (pair.astype(F32) + cross.astype(F32)).astype(BF16)
    back = swap(total, lambda z, i: (z ^ 1, i))
    return jnp.concatenate(
        [jnp.where(low, total, back), jnp.where(low, back, total)], axis=0
    ).astype(F32)


def sum_seq(value):
    if not is_small():
        return lax.psum(value, "seq")
    for bit in (1, 2, 4):
        value = value + swap(value, along(bit))
    return value


def sum_all(value):
    value = sum_seq(value)
    if not is_small():
        return lax.psum(value, "dp")
    for bit in (1, 2):
        value = value + swap(value, lambda z, i: (z ^ bit, i))
    return value


def stack_dp(value):
    if not is_small():
        return lax.all_gather(value, "dp", axis=0, tiled=True)
    for bit in (1, 2):
        value = jnp.concatenate([value, swap(value, lambda z, i: (z ^ bit, i))], axis=0)
    return value


def dot(left, right, contract=((1,), (0,))):
    return lax.dot_general(left, right, (contract, ((), ())), preferred_element_type=F32)


def call(body, name, **kwargs):
    return pl.pallas_call(
        body,
        name=name,
        compiler_params=pltpu.CompilerParams(vmem_limit_bytes=LIMIT),
        **kwargs,
    )


VMEM = pl.BlockSpec(memory_space=pltpu.VMEM)
ANY = pl.BlockSpec(memory_space=pl.ANY)
SMEM = pl.BlockSpec(memory_space=pltpu.SMEM)


def block_copies(owners, refs, target, sems, part=None):
    copies = []
    for slot, ref in enumerate(refs):
        source = ref if part is None else ref.at[part]
        rows = source.shape[-2]
        start = pl.multiple_of(owners[0, slot] * rows, rows)
        if source.ndim == 3:
            place = target.at[:, pl.ds(start, rows), :]
        else:
            place = target.at[pl.ds(start, rows), :]
        copies.append(pltpu.make_async_copy(source, place, sems.at[slot]))
    for copy in copies:
        copy.start()
    return copies


def wait(copies):
    for copy in copies:
        copy.wait()


def qkv_kernel(count, owners, *refs):
    blocks, (tokens, table, query, key, value, weights, sems) = refs[:count], refs[count:]
    wait(block_copies(owners, blocks, weights, sems))
    rows = tokens[...]
    key[...] = dot(rows, weights[1]).astype(BF16)
    value[...] = (dot(rows, weights[2]) + table[VALUE_B : VALUE_B + 1]).astype(BF16)
    query[...] = (dot(rows, weights[0]) + table[QUERY_B : QUERY_B + 1]).astype(BF16)


def qkv_project(owners, blocks, tokens, table):
    out = jax.ShapeDtypeStruct(tokens.shape, BF16)
    count = len(blocks)
    return call(
        functools.partial(qkv_kernel, count),
        "qkv",
        out_shape=(out,) * 3,
        in_specs=[SMEM] + [ANY] * count + [VMEM] * 2,
        out_specs=(VMEM,) * 3,
        scratch_shapes=[pltpu.VMEM((3, D, D), BF16), pltpu.SemaphoreType.DMA((count,))],
    )(owners, *blocks, tokens, table)


def left_half(shape):
    return lax.broadcasted_iota(jnp.int32, shape, len(shape) - 1) < HEAD_DIM


def split3(value):
    high = value.astype(BF16).astype(F32)
    middle = (value - high).astype(BF16).astype(F32)
    low = (value - high - middle).astype(BF16).astype(F32)
    return high, middle, low


def spread3(value, docs, shape):
    lane = lax.broadcasted_iota(jnp.int32, shape, 1) % HEAD_DIM
    high, middle, low = split3(value)
    return jnp.where(
        lane == docs, high, jnp.where(lane == docs + 1, middle, jnp.where(lane == docs + 2, low, 0.0))
    )


def attend_kernel(count, docs, *refs):
    query, feature_q, feature_k = refs[:3]
    keys, values = refs[3 : 3 + count], refs[3 + count : 3 + 2 * count]
    out, total, scores = refs[3 + 2 * count :]
    chunks = feature_k.shape[0]
    left = left_half((ROWS, PAIR))
    rows = query[...] * 0.125
    spare = feature_q[...]
    results, totals = [], []
    for head in range(2):
        mine = left if head == 0 else jnp.logical_not(left)
        aug = jnp.where(mine, rows, spare)

        def score_step(chunk, key):
            full = jnp.where(mine, key, feature_k[chunk])
            scores[chunk] = dot(aug, full, ((1,), (1,)))

        def value_step(chunk, value, top):
            full = jnp.where(mine, value, feature_k[chunk])
            return dot(jnp.exp(scores[chunk] - top).astype(BF16), full)

        if count > 1:
            for chunk in range(count):
                score_step(chunk, keys[chunk][...])
            most = scores[0]
            for chunk in range(1, count):
                most = jnp.maximum(most, scores[chunk])
            top = jnp.max(most, axis=1, keepdims=True)
            acc = value_step(0, values[0][...], top)
            for chunk in range(1, count):
                acc = acc + value_step(chunk, values[chunk][...], top)
        else:

            @pl.loop(0, chunks)
            def _(chunk):
                score_step(chunk, keys[0][chunk])

            most = lax.fori_loop(
                1, chunks, lambda chunk, had: jnp.maximum(had, scores[chunk]), scores[0]
            )
            top = jnp.max(most, axis=1, keepdims=True)
            acc = lax.fori_loop(
                0,
                chunks,
                lambda chunk, had: had + value_step(chunk, values[0][chunk], top),
                jnp.zeros((ROWS, PAIR), F32),
            )
        lane = docs + (HEAD_DIM if head == 0 else 0)
        weight = acc[:, lane : lane + 1]
        results.append(acc / weight)
        totals.append(top + jnp.log(weight))
    out[...] = jnp.where(left, results[0], results[1])
    total[...] = jnp.where(left, totals[0], totals[1])


def pair_spec(array):
    lead = array.shape[:-1]
    return pl.BlockSpec(lead + (PAIR,), lambda pair: (0,) * len(lead) + (pair,))


def fixed_spec(array):
    return pl.BlockSpec(array.shape, lambda pair: (0,) * array.ndim)


def attend(query, keys, values, feature_q, feature_k, docs):
    count = len(keys)
    out = jax.ShapeDtypeStruct((ROWS, D), F32)
    return call(
        functools.partial(attend_kernel, count, docs),
        "attend",
        grid=(HEADS // 2,),
        out_shape=(out, out),
        in_specs=[pair_spec(query), fixed_spec(feature_q), fixed_spec(feature_k)]
        + [pair_spec(block) for block in (*keys, *values)],
        out_specs=(pair_spec(out), pair_spec(out)),
        scratch_shapes=[pltpu.VMEM((feature_k.shape[0], ROWS, ROWS), F32)],
    )(query, feature_q, feature_k, *keys, *values)


def attend_back_kernel(count, docs, groups, *refs):
    query, grad, attended, total, feature_q, feature_k = refs[:6]
    keys, values = refs[6 : 6 + count], refs[6 + count : 6 + 2 * count]
    rest = refs[6 + 2 * count :]
    grad_q, grad_k, grad_v = rest[0], rest[1 : 1 + groups], rest[1 + groups : 1 + 2 * groups]
    acc = rest[-1]
    chunks = feature_k.shape[0]
    left = left_half((ROWS, PAIR))
    rows = query[...] * 0.125
    grads = grad[...]
    product = grads.astype(F32) * attended[...]
    spare = feature_q[...]
    zero = jnp.zeros_like(rows)
    sides = []
    for head in range(2):
        mine = left if head == 0 else jnp.logical_not(left)
        at = head * HEAD_DIM
        delta = jnp.sum(jnp.where(mine, product, 0.0), axis=1, keepdims=True)
        sums = total[:, at : at + 1]
        query_aug = jnp.where(
            mine, rows.astype(F32), spare.astype(F32) + spread3(-sums, docs, (ROWS, PAIR))
        )
        grad_aug = jnp.where(mine, grads.astype(F32), spread3(-delta, docs, (ROWS, PAIR)))
        sides.append(
            (
                mine,
                query_aug.T.astype(BF16),
                grad_aug.T.astype(BF16),
                jnp.where(mine, rows, zero),
                jnp.where(mine, grads, zero),
            )
        )
    acc[...] = jnp.zeros_like(acc)

    def step(chunk, key, value):
        feature = feature_k[chunk]
        key_t = key.astype(F32).T.astype(BF16)
        out_k, out_v = 0.0, 0.0
        for head in range(2):
            mine, query_t, grad_t, query_own, grad_own = sides[head]
            soft = jnp.exp(dot(jnp.where(mine, key, feature), query_t))
            change = dot(jnp.where(mine, value, feature), grad_t)
            slope = (soft * change).astype(BF16)
            out_v = out_v + dot(soft.astype(BF16), grad_own)
            out_k = out_k + dot(slope, query_own)
            at = head * HEAD_DIM
            acc[at : at + HEAD_DIM] += dot(key_t[at : at + HEAD_DIM], slope)
        return out_k.astype(BF16), out_v.astype(BF16)

    if count > 1:
        per = count // groups
        for chunk in range(count):
            out_k, out_v = step(chunk, keys[chunk][...], values[chunk][...])
            grad_k[chunk // per][chunk % per] = out_k
            grad_v[chunk // per][chunk % per] = out_v
    else:

        @pl.loop(0, chunks)
        def _(chunk):
            out_k, out_v = step(chunk, keys[0][chunk], values[0][chunk])
            grad_k[0][chunk] = out_k
            grad_v[0][chunk] = out_v

    grad_q[...] = (acc[...].T * 0.125).astype(BF16)


def attend_back(query, keys, values, grad, attended, total, feature_q, feature_k, docs):
    count = len(keys)
    groups = 2 if count > 1 else 1
    chunks = feature_k.shape[0]
    grad_q = jax.ShapeDtypeStruct((ROWS, D), BF16)
    grad_kv = jax.ShapeDtypeStruct((chunks // groups, ROWS, D), BF16)
    outs = (grad_q,) + (grad_kv,) * (2 * groups)
    made = call(
        functools.partial(attend_back_kernel, count, docs, groups),
        "attend_back",
        grid=(HEADS // 2,),
        out_shape=outs,
        in_specs=[pair_spec(a) for a in (query, grad, attended, total)]
        + [fixed_spec(feature_q), fixed_spec(feature_k)]
        + [pair_spec(block) for block in (*keys, *values)],
        out_specs=tuple(pair_spec(a) for a in outs),
        scratch_shapes=[pltpu.VMEM((PAIR, ROWS), F32)],
    )(query, grad, attended, total, feature_q, feature_k, *keys, *values)
    return made[0], made[1 : 1 + groups], made[1 + groups :]


def normalise(value):
    centred = value - jnp.mean(value, axis=-1, keepdims=True)
    inverse = lax.rsqrt(jnp.mean(centred * centred, axis=-1, keepdims=True) + EPSILON)
    return centred * inverse, inverse


def norm_back(grad, gain, unit, inverse):
    scaled = grad * gain
    return inverse * (
        scaled
        - jnp.mean(scaled, axis=-1, keepdims=True)
        - unit * jnp.mean(scaled * unit, axis=-1, keepdims=True)
    )


def erf(value):
    value = jnp.clip(value, -3.7439211627767994, 3.7439211627767994)
    square = value * value
    top = 0.00022905065861350646
    for factor in (0.0034082910107109506, 0.050955695062380861, 0.18520832239976145, 1.128379143519084):
        top = top * square + factor
    bottom = -1.1791602954361697e-7
    for factor in (
        0.000023547966471313185, 0.0010179625278914885, 0.014070470171167667,
        0.11098505178285362, 0.49746925110067538, 1.0,
    ):
        bottom = bottom * square + factor
    return value * top / bottom


def column_sum(value):
    return jnp.sum(value, axis=0, keepdims=True)


def first_kernel(count, docs, owners, *refs):
    groups = 2 if count > 1 else 1
    proj_blocks, up_blocks, down_blocks = (refs[k * count : (k + 1) * count] for k in range(3))
    refs = refs[3 * count :]
    attended, tokens, cotangent, table, place, labels, class_b = refs[:7]
    output, lines, docs_out, grad_second, unit, inverse, slope = refs[7:14]
    down_g = refs[14 : 14 + groups]
    both, up, down, active, wgrad, sems, out_sems = refs[14 + groups :]
    proj_copies = block_copies(owners, proj_blocks, both, sems.at[0])
    up_copies = block_copies(owners, up_blocks, up, sems.at[1])
    down_copies = block_copies(owners, down_blocks, down, sems.at[2])

    def row(at):
        return table[at : at + 1]

    wait(proj_copies)
    residual = tokens[...].astype(F32) + dot(attended[...].astype(BF16), both[0]) + row(PROJ_B)
    first_unit, first_inverse = normalise(residual)
    unit[...] = first_unit
    inverse[...] = first_inverse
    normed = first_unit * row(NORM_G) + row(NORM_S)
    normed_low = normed.astype(BF16)
    wait(up_copies)
    step = 384
    for at in range(0, FF, step):
        line, col = UP_B + at // D, at % D
        upward = dot(normed_low, up[:, at : at + step]) + table[line : line + 1, col : col + step]
        share = 0.5 + 0.5 * erf(upward * 0.7071067811865476)
        bell = jnp.exp(upward * upward * -0.5) * 0.3989422804014327
        active[:, at : at + step] = (upward * share).astype(BF16)
        slope[:, at : at + step] = share + upward * bell
    wait(down_copies)
    residual = normed + dot(active[...], down[...]) + row(DOWN_B)
    last_unit, last_inverse = normalise(residual)
    outcome = last_unit * row(FINAL_G) + row(FINAL_S)
    out_low = outcome.astype(BF16)
    output[...] = out_low

    at_row = place[...]
    here = jnp.logical_and(at_row >= 0, at_row < ROWS)
    pick = jnp.where(lax.broadcasted_iota(jnp.int32, (docs, ROWS), 1) == at_row, 1.0, 0.0)
    first_low = dot(pick.astype(BF16), out_low).astype(BF16)
    pooled = jnp.tanh(dot(first_low, both[1]) + row(POOL_B))
    pooled_low = pooled.astype(BF16).astype(F32)
    logits = [
        jnp.sum(pooled_low * row(CLASS_W + c), axis=1, keepdims=True) + class_b[0, c]
        for c in range(CLASSES)
    ]
    top = functools.reduce(jnp.maximum, logits)
    powers = [jnp.exp(logit - top) for logit in logits]
    whole = functools.reduce(jnp.add, powers)
    label = labels[...]
    grads = [powers[c] / whole - jnp.where(label == c, 1.0, 0.0) for c in range(CLASSES)]
    grad_pre = functools.reduce(jnp.add, [grads[c] * row(CLASS_W + c) for c in range(CLASSES)])
    grad_pre = grad_pre * (1.0 - pooled * pooled)
    parts = jnp.concatenate(split3(grad_pre), axis=0).astype(BF16)
    made = dot(parts, both[1], ((1,), (1,)))
    grad_first = made[:docs] + made[docs : 2 * docs] + made[2 * docs :]
    parts = jnp.concatenate(split3(grad_first), axis=0).astype(BF16)
    picks = jnp.concatenate([pick] * 3, axis=0).astype(BF16)
    grad_outcome = cotangent[...] + dot(picks, parts, ((0,), (0,)))
    lane = lax.broadcasted_iota(jnp.int32, (docs, 128), 1)
    small = jnp.zeros((docs, 128), F32)
    for c in range(CLASSES):
        small = jnp.where(lane == c, grads[c], jnp.where(lane == CLASSES + c, logits[c], small))
    docs_out[...] = jnp.where(
        here,
        jnp.concatenate([first_low.astype(F32), pooled_low, grad_pre, small], axis=1),
        0.0,
    )

    grad = norm_back(grad_outcome, row(FINAL_G), last_unit, last_inverse)
    grad_second[...] = grad
    lines[0:1] = column_sum(grad)
    lines[1:2] = column_sum(grad_outcome * last_unit)
    lines[2:3] = column_sum(grad_outcome)
    lines[3:8] = jnp.zeros((5, D), F32)
    grad_low = grad.astype(BF16)
    step = 512
    for at in range(0, FF, step):
        wgrad[at : at + step] = dot(active[:, at : at + step], grad_low, ((0,), (0,))).astype(BF16)
    slot_copies(owners, wgrad, [g.at[j] for g in down_g for j in range(g.shape[0])], out_sems)


def slot_copies(owners, source, targets, sems):
    copies = []
    for slot, target in enumerate(targets):
        rows = target.shape[0]
        start = pl.multiple_of(owners[1, slot] * rows, rows)
        copies.append(pltpu.make_async_copy(source.at[pl.ds(start, rows), :], target, sems.at[slot]))
    for copy in copies:
        copy.start()
    wait(copies)


def slot_shapes(count, rows):
    if count == 1:
        return (jax.ShapeDtypeStruct((1, rows, D), BF16),)
    return (jax.ShapeDtypeStruct((count // 2, rows // count, D), BF16),) * 2


def first_part(
    owners, proj_blocks, up_blocks, down_blocks, attended, tokens, cotangent, table, place, labels, class_b
):
    count, docs = len(proj_blocks), place.shape[0]
    down_shapes = slot_shapes(count, FF)
    shape = jax.ShapeDtypeStruct
    outs = (
        shape((ROWS, D), BF16),
        shape((8, D), F32),
        shape((docs, 3 * D + 128), F32),
        shape((ROWS, D), F32),
        shape((ROWS, D), F32),
        shape((ROWS, 1), F32),
        shape((ROWS, FF), F32),
    ) + down_shapes
    made = call(
        functools.partial(first_kernel, count, docs),
        "forward_and_head",
        out_shape=outs,
        in_specs=[SMEM] + [ANY] * (3 * count) + [VMEM] * 6 + [SMEM],
        out_specs=(VMEM,) * 7 + (ANY,) * len(down_shapes),
        scratch_shapes=[
            pltpu.VMEM((2, D, D), BF16),
            pltpu.VMEM((D, FF), BF16),
            pltpu.VMEM((FF, D), BF16),
            pltpu.VMEM((ROWS, FF), BF16),
            pltpu.VMEM((FF, D), BF16),
            pltpu.SemaphoreType.DMA((3, count)),
            pltpu.SemaphoreType.DMA((count,)),
        ],
    )(
        owners, *proj_blocks, *up_blocks, *down_blocks,
        attended, tokens, cotangent, table, place, labels, class_b,
    )
    return made[:7], made[7:]


def second_kernel(count, owners, *refs):
    groups = 2 if count > 1 else 1
    proj_blocks, up_blocks, down_blocks = (refs[k * count : (k + 1) * count] for k in range(3))
    refs = refs[3 * count :]
    attended, table, grad_second, unit, inverse, slope = refs[:6]
    lines, grad_first, grad_attended = refs[6:9]
    up_g = refs[9 : 9 + groups]
    both, up, down, grad_up, wgrad, pgrad, sems, out_sems = refs[9 + groups :]
    down_copies = block_copies(owners, down_blocks, down, sems.at[2])
    up_copies = block_copies(owners, up_blocks, up, sems.at[1])
    proj_copies = block_copies(owners, proj_blocks, both, sems.at[0], 0)

    def row(at):
        return table[at : at + 1]

    grad_low = grad_second[...].astype(BF16)
    normed_t = (unit[...] * row(NORM_G) + row(NORM_S)).T.astype(BF16)
    attended_t = attended[...].T.astype(BF16)
    wait(down_copies)
    step = 384
    for at in range(0, FF, step):
        grad = dot(grad_low, down[at : at + step], ((1,), (1,))).astype(BF16).astype(F32)
        grad = grad * slope[:, at : at + step]
        line, col = at // D, at % D
        lines[line : line + 1, col : col + step] = column_sum(grad)
        grad_up[:, at : at + step] = grad.astype(BF16)
    wait(up_copies)
    grad_normed = grad_second[...] + dot(grad_up[...], up[...], ((1,), (1,))).astype(BF16).astype(F32)
    lines[4:5] = column_sum(grad_normed * unit[...])
    lines[5:6] = column_sum(grad_normed)
    grad = norm_back(grad_normed, row(NORM_G), unit[...], inverse[...])
    grad_first[...] = grad
    lines[6:7] = column_sum(grad)
    lines[7:8] = jnp.zeros((1, D), F32)
    grad_low = grad.astype(BF16)
    wait(proj_copies)
    grad_attended[...] = dot(grad_low, both[...], ((1,), (1,))).astype(BF16)
    pgrad[...] = dot(attended_t, grad_low).astype(BF16)
    for at in range(0, FF, D):
        wgrad[at // D] = dot(normed_t, grad_up[:, at : at + D]).astype(BF16)
    copies = []
    slots = [g.at[j] for g in up_g for j in range(g.shape[0])]
    for slot, target in enumerate(slots):
        rows = target.shape[0] // 5
        start = pl.multiple_of(owners[1, slot] * rows, rows)
        for piece in range(4):
            copies.append((wgrad.at[piece, pl.ds(start, rows), :], target.at[piece * rows : (piece + 1) * rows]))
        copies.append((pgrad.at[pl.ds(start, rows), :], target.at[4 * rows :]))
    copies = [
        pltpu.make_async_copy(source, target, out_sems.at[k])
        for k, (source, target) in enumerate(copies)
    ]
    for copy in copies:
        copy.start()
    wait(copies)


def second_part(owners, proj_blocks, up_blocks, down_blocks, attended, table, grad_second, unit, inverse, slope):
    count = len(proj_blocks)
    up_shapes = slot_shapes(count, 5 * D)
    shape = jax.ShapeDtypeStruct
    outs = (shape((8, D), F32), shape((ROWS, D), F32), shape((ROWS, D), BF16)) + up_shapes
    made = call(
        functools.partial(second_kernel, count),
        "backward_to_attention",
        out_shape=outs,
        in_specs=[SMEM] + [ANY] * (3 * count) + [VMEM] * 6,
        out_specs=(VMEM,) * 3 + (ANY,) * len(up_shapes),
        scratch_shapes=[
            pltpu.VMEM((D, D), BF16),
            pltpu.VMEM((D, FF), BF16),
            pltpu.VMEM((FF, D), BF16),
            pltpu.VMEM((ROWS, FF), BF16),
            pltpu.VMEM((4, D, D), BF16),
            pltpu.VMEM((D, D), BF16),
            pltpu.SemaphoreType.DMA((3, count)),
            pltpu.SemaphoreType.DMA((5 * count,)),
        ],
    )(
        owners, *proj_blocks, *up_blocks, *down_blocks,
        attended, table, grad_second, unit, inverse, slope,
    )
    return made[:3], made[3:]


def last_kernel(count, owners, *refs):
    groups = 2 if count > 1 else 1
    blocks, refs = refs[:count], refs[count:]
    tokens, grad_q, grad_k, grad_v, grad_first = refs[:5]
    lines, input_grad = refs[5:7]
    outs = refs[7 : 7 + groups]
    weights, wgrad, sems, out_sems = refs[7 + groups :]
    copies = block_copies(owners, blocks, weights, sems)
    tokens_t = tokens[...].astype(F32).T.astype(BF16)
    grads = [grad_q[...], grad_k[...].astype(BF16), grad_v[...].astype(BF16)]
    for k in range(3):
        wgrad[k] = dot(tokens_t, grads[k]).astype(BF16)
    sends = []
    slots = [g.at[j] for g in outs for j in range(g.shape[0])]
    for slot, target in enumerate(slots):
        rows = target.shape[0] // 3
        start = pl.multiple_of(owners[1, slot] * rows, rows)
        for k in range(3):
            sends.append((wgrad.at[k, pl.ds(start, rows), :], target.at[k * rows : (k + 1) * rows]))
    sends = [
        pltpu.make_async_copy(source, target, out_sems.at[k])
        for k, (source, target) in enumerate(sends)
    ]
    for copy in sends:
        copy.start()
    lines[0:1] = column_sum(grads[0].astype(F32))
    lines[1:2] = column_sum(grads[2].astype(F32))
    lines[2:8] = jnp.zeros((6, D), F32)
    wait(copies)
    total = grad_first[...]
    for k in range(3):
        total = total + dot(grads[k], weights[k], ((1,), (1,)))
    input_grad[...] = total
    wait(sends)


def last_part(owners, blocks, tokens, grad_q, grad_k, grad_v, grad_first):
    count = len(blocks)
    shapes = slot_shapes(count, 3 * D)
    shape = jax.ShapeDtypeStruct
    outs = (shape((8, D), F32), shape((ROWS, D), F32)) + shapes
    made = call(
        functools.partial(last_kernel, count),
        "input_gradients",
        out_shape=outs,
        in_specs=[SMEM] + [ANY] * count + [VMEM] * 5,
        out_specs=(VMEM,) * 2 + (ANY,) * len(shapes),
        scratch_shapes=[
            pltpu.VMEM((3, D, D), BF16),
            pltpu.VMEM((3, D, D), BF16),
            pltpu.SemaphoreType.DMA((count,)),
            pltpu.SemaphoreType.DMA((3 * count,)),
        ],
    )(owners, *blocks, tokens, grad_q, grad_k, grad_v, grad_first)
    return made[0], made[1], made[2:]


def weight_slots(parts, pieces):
    if is_small():
        return parts
    seq = lax.axis_size("seq")
    (part,) = parts
    rows = part.shape[1] // pieces // seq
    part = part.reshape(pieces, seq, rows, D).transpose(1, 0, 2, 3)
    return (part.reshape(seq, pieces * rows, D),)


def features(positions, starts):
    docs = starts.shape[0]
    segment = jnp.sum((positions[..., None] >= starts).astype(jnp.int32), axis=-1) - 1
    lane = jnp.arange(PAIR, dtype=jnp.int32) % HEAD_DIM
    own = segment[..., None] == lane
    return own, lane, docs


def on_device(
    inputs,
    cotangent,
    doc_lengths,
    doc_labels,
    query_weight,
    query_bias,
    key_weight,
    value_weight,
    value_bias,
    proj_weight,
    proj_bias,
    norm_gain,
    norm_shift,
    up_weight,
    up_bias,
    down_weight,
    down_bias,
    final_gain,
    final_shift,
    pool_weight,
    pool_bias,
    class_weight,
    class_bias,
):
    me = lax.axis_index("seq")
    tokens = inputs[0]
    share = query_bias.shape[0]
    lengths = doc_lengths[0]
    docs = lengths.shape[0]
    order = jnp.arange(docs, dtype=jnp.int32)
    starts = jnp.sum(jnp.where(order[None, :] < order[:, None], lengths[None, :], 0), axis=1)

    qkv_blocks, qkv_owners = gather_shared(jnp.stack([query_weight, key_weight, value_weight]), 0)
    small = jnp.stack(
        [
            query_bias, value_bias, proj_bias, norm_gain, norm_shift, down_bias,
            final_gain, final_shift, pool_bias, *class_weight.T,
        ]
    )
    table = jnp.zeros((TABLE, D), BF16)
    table = lax.dynamic_update_slice(table, small, (0, me * share))
    wide = me * up_bias.shape[0]
    if up_bias.shape[0] <= D:
        table = lax.dynamic_update_slice(table, up_bias[None], (UP_B + wide // D, wide % D))
    table = sum_seq(table).astype(F32)
    proj_blocks, proj_owners = gather_shared(jnp.stack([proj_weight, pool_weight]), 1)
    up_blocks, up_owners = gather_shared(up_weight, 1)
    down_blocks, down_owners = gather_shared(down_weight, 1)
    slots = slot_owners()
    targets = slots if is_small() else jnp.zeros((1,), jnp.int32)
    qkv_owners = jnp.stack([jnp.stack(qkv_owners), targets])
    owners = jnp.stack([jnp.stack(proj_owners), targets])

    query, key, value = qkv_project(qkv_owners, qkv_blocks, tokens, table)
    keys, values = gather_own(key, (2, 4)), gather_own(value, (4, 2))
    line = jnp.arange(ROWS, dtype=jnp.int32)
    own, lane, _ = features(me * ROWS + line, starts)
    feature_q = jnp.where(own, FAR, 0.0).astype(BF16)
    own, lane, _ = features(slots[:, None] * ROWS + line, starts)
    feature_k = jnp.where(
        lane < docs, jnp.where(own, 0.0, 1.0), jnp.where(lane < docs + 3, 1.0, 0.0)
    ).astype(BF16)
    attended, total = attend(query, keys, values, feature_q, feature_k, docs)

    place = (starts - me * ROWS)[:, None]
    made, down_parts = first_part(
        owners, proj_blocks, up_blocks, down_blocks, attended, tokens, cotangent[0], table,
        place, doc_labels[0][:, None], class_bias.astype(F32)[None],
    )
    output, lines_one, docs_out, grad_second, unit, inverse, slope = made
    made, up_parts = second_part(
        owners, proj_blocks, up_blocks, down_blocks, attended, table, grad_second, unit, inverse, slope
    )
    lines_two, grad_first, grad_attended = made

    grad_q, grad_k, grad_v = attend_back(
        query, keys, values, grad_attended, attended, total, feature_q, feature_k, docs
    )
    grad_k = scatter_sum(grad_k, (2, 4))
    grad_v = scatter_sum(grad_v, (4, 2))
    lines_three, input_grad, qkv_parts = last_part(
        qkv_owners, qkv_blocks, tokens, grad_q, grad_k, grad_v, grad_first
    )

    down_wgrad = sum_dp(scatter_sum(weight_slots(down_parts, 1), (2, 4)))
    up_wgrad = sum_dp(scatter_sum(weight_slots(up_parts, 5), (4, 2)))
    qkv_wgrad = sum_dp(scatter_sum(weight_slots(qkv_parts, 3), (2, 4)))
    proj_wgrad = up_wgrad[4 * share :]
    up_wgrad = up_wgrad[: 4 * share].reshape(4, share, D).transpose(1, 0, 2).reshape(share, FF)
    qkv_wgrad = qkv_wgrad.reshape(3, share, D)
    lines = sum_all(jnp.concatenate([lines_one, lines_two, lines_three], axis=0))
    docs_sum = sum_seq(docs_out)
    logits = docs_sum[:, 3 * D + CLASSES : 3 * D + 2 * CLASSES]
    every_doc = stack_dp(docs_sum)
    at = me * share

    def my_share(vector):
        return lax.dynamic_slice_in_dim(vector, at, share, 0)

    first_all, pooled_all = (
        lax.dynamic_slice_in_dim(every_doc, k * D + at, share, 1) for k in range(2)
    )
    pre_all = every_doc[:, 2 * D : 3 * D]
    logit_all = every_doc[:, 3 * D : 3 * D + CLASSES]
    exact = functools.partial(jnp.dot, precision=lax.Precision.HIGHEST)
    return (
        output[None],
        logits[None],
        input_grad[None],
        qkv_wgrad[0],
        my_share(lines[16]),
        qkv_wgrad[1],
        qkv_wgrad[2],
        my_share(lines[17]),
        proj_wgrad,
        my_share(lines[14]),
        my_share(lines[12]),
        my_share(lines[13]),
        up_wgrad,
        lax.dynamic_slice_in_dim(lines[8:12].reshape(-1), wide, up_bias.shape[0], 0),
        down_wgrad,
        my_share(lines[0]),
        my_share(lines[1]),
        my_share(lines[2]),
        exact(first_all.T, pre_all),
        my_share(jnp.sum(pre_all, axis=0)),
        exact(pooled_all.T, logit_all),
        jnp.sum(logit_all, axis=0),
    )


def solution(mesh):
    rows, row, part = P("dp", "seq", None), P("seq", None), P("seq")
    per_sequence = P("dp", None)
    in_specs = (
        rows, rows, per_sequence, per_sequence, row, part, row, row, part, row, part, part,
        part, row, part, row, part, part, part, row, part, row, P(),
    )
    out_specs = (
        rows, P("dp", None, None), rows, row, part, row, row, part, row, part, part, part,
        row, part, row, part, part, part, row, part, row, P(),
    )
    return jax.shard_map(
        on_device, mesh=mesh, in_specs=in_specs, out_specs=out_specs, check_vma=False
    )
```

time: 859 us -> 408 us (0.47)
  waiting for transfers between devices: 422 us -> 189 us
  matrix products: 148 us -> 2.03 us
  blocking collectives: 103 us -> 0 us
  Pallas kernels: 0 us -> 87.1 us
  local copies, waits for them, and re-layouts: 88.5 us -> 16.9 us
  starting transfers between devices: 0.85 us -> 66.3 us
  other arithmetic: 65.6 us -> 37.3 us
  between operations: 17 us -> 1.92 us
  loops' own time: 8.78 us -> 0 us
    reduce_scatter x4 -> x0, waiting for transfers between devices: 210 us -> none  [the longest x1 57.6 us: on_device(): lax.psum_scatter(down_wpart.astype(jnp.bfloat16), 'seq', scatter_dimensio...]
    ppermute x0 -> x79, waiting for transfers between devices: none -> 189 us  [swap(): return lax.ppermute(value, ('dp', 'seq'), pairs)]
    dot_general x54 -> x2, matrix products: 148 us -> 2.03 us  [the longest x1 1.22 us: on_device(): exact(first_all.T, pre_all)]
    unnamed x20 -> x0, waiting for transfers between devices: 99.5 us -> none
    pallas_call x0 -> x6, Pallas kernels: none -> 87.1 us  [the longest x1 27.3 us: attend_back(): call(functools.partial(attend_back_kernel, count, docs, groups), 'attend_...]
    all_gather x9 -> x0, waiting for transfers between devices: 75 us -> none  [the longest x1 28.6 us: on_device(): lax.all_gather(down_weight, 'seq', axis=0, tiled=True)]
    ppermute x0 -> x79, starting transfers between devices: none -> 66.3 us  [swap(): return lax.ppermute(value, ('dp', 'seq'), pairs)]
    unnamed x2 -> x0, blocking collectives: 49 us -> none
  transfers between devices with their start and end apart: 17 -> 79, of which waited for: 11 -> 37; matrix products, arithmetic and copies ran while one was open for 21% -> 12% of each run, Pallas kernels for 0% -> 6%
where the time goes in v1:
time: 408 us; the launch traced here: 401 us
  waiting for transfers between devices  189 us (46%)
  Pallas kernels  87.1 us (21%)
  starting transfers between devices  66.3 us (16%)
  other arithmetic  37.3 us (9%)
  local copies, waits for them, and re-layouts  16.9 us (4%)
    ppermute x79, waiting for transfers between devices, swap(): return lax.ppermute(value, ('dp', 'seq'), pairs)  189 us
    ppermute x79, starting transfers between devices, swap(): return lax.ppermute(value, ('dp', 'seq'), pairs)  66.3 us
    pallas_call x1, Pallas kernels, attend_back(): call(functools.partial(attend_back_kernel, count, docs, groups), 'attend_...  27.3 us
    pallas_call x1, Pallas kernels, first_part(): call(functools.partial(first_kernel, count, docs), 'forward_and_head', ou...  19 us
    pallas_call x1, Pallas kernels, second_part(): call(functools.partial(second_kernel, count), 'backward_to_attention', ou...  15.9 us
    pallas_call x1, Pallas kernels, attend(): call(functools.partial(attend_kernel, count, docs), 'attend', grid=(HEADS...  13.5 us
    convert_element_type x5, other arithmetic, scatter_sum(): send = (keep[far].astype(F32) + come[far].astype(F32)).astype(BF16)  9.3 us
    add x5, other arithmetic, scatter_sum(): keep[0].astype(F32) + come[0].astype(F32) + second[0].astype(F32)  8.96 us
  transfers between devices with their start and end apart: 79, of which 37 were waited for; matrix products, arithmetic and copies ran while one was open for 12% of the time, Pallas kernels for 6%

profile of v1, /device:TPU:0, one launch (start us, length us, event | category | flops | bytes accessed | tf_op | source)
XLA Modules:
  0.0 400.6 jit_solution(450296916170602499)
XLA Ops:
  1.8 3.0 collective-permute-start
  12.8 6.4 %collective-permute-done.29 = bf16[16,768]{1,0:T(8,128)(2,1)S(1)} collective-permute-done((bf16[16,768]{1,0:T(8,128)(2,1)S(1)}, bf16[16,768]{1,0:T(8,128)(2,1)S(1)}, u32[]{:S(2)}, u32[]{:S(2)}) %collective-permute-start.29) | collective-permute-done | bytes 24608 | tf_op jit(solution)/shard_map/ppermute | solution.py:35
  19.5 3.6 collective-permute-done.30
  25.5 5.4 %collective-permute-done.2.refs_3_ = bf16[2,96,768]{2,1,0:T(8,128)(2,1)} collective-permute-done((bf16[2,96,768]{2,1,0:T(8,128)(2,1)}, bf16[2,96,768]{2,1,0:T(8,128)(2,1)}, u32[]{:S(2)}, u32[]{:S(2)}) %collective-permute-start.2) | collective-permute-done | bytes 294944 | tf_op jit(solution)/shard_map/ppermute | solution.py:35
  32.7 8.3 %collective-permute-done.7.refs_9_ = bf16[96,3072]{1,0:T(8,128)(2,1)S(1)} collective-permute-done((bf16[96,3072]{1,0:T(8,128)(2,1)S(1)}, bf16[96,3072]{1,0:T(8,128)(2,1)S(1)}, u32[]{:S(2)}, u32[]{:S(2)}) %collective-permute-start.7) | collective-permute-done | bytes 589856 | tf_op jit(solution)/shard_map/ppermute | solution.py:35
  42.0 11.6 %collective-permute-done.14.refs_17_ = bf16[384,768]{1,0:T(8,128)(2,1)S(1)} collective-permute-done((bf16[384,768]{1,0:T(8,128)(2,1)S(1)}, bf16[384,768]{1,0:T(8,128)(2,1)S(1)}, u32[]{:S(2)}, u32[]{:S(2)}) %collective-permute-start.14) | collective-permute-done | bytes 589856 | tf_op jit(solution)/shard_map/ppermute | solution.py:35
  58.7 4.1 %collective-permute-done.22.refs_2_ = bf16[3,96,768]{2,1,0:T(8,128)(2,1)} collective-permute-done((bf16[3,96,768]{2,1,0:T(8,128)(2,1)}, bf16[3,96,768]{2,1,0:T(8,128)(2,1)}, u32[]{:S(2)}, u32[]{:S(2)}) %collective-permute-start.22) | collective-permute-done | bytes 442400 | tf_op jit(solution)/shard_map/ppermute | solution.py:35
  68.7 4.9 %qkv.1 = (bf16[256,768]{1,0:T(8,128)(2,1)}, bf16[256,768]{1,0:T(8,128)(2,1)}, bf16[256,768]{1,0:T(8,128)(2,1)}) custom-call(s32[2,8]{1,0:T(2,128)} %get-tuple-element.141.owners, bf16[3,96,768]{2,1,0:T(8,128)(2,1)} %copy-done, bf16[3,96,768]{2,1,0:T(8,128)(2,1)} %collective-permute-done.21.refs_1_, bf16[3,96,768]{2,1,0:T(8,128)(2,1)} %collective-permute-done.22.refs_2_, ...), custom_call_target="tpu_custom_call" | custom-call | tf_op jit(solution)/shard_map/qkv/pallas_call | solution.py:193
  75.9 8.4 %collective-permute-done.16.refs_19_ = bf16[384,768]{1,0:T(8,128)(2,1)} collective-permute-done((bf16[384,768]{1,0:T(8,128)(2,1)}, bf16[384,768]{1,0:T(8,128)(2,1)}, u32[]{:S(2)}, u32[]{:S(2)}) %collective-permute-start.16) | collective-permute-done | bytes 589856 | tf_op jit(solution)/shard_map/ppermute | solution.py:35
  87.7 6.8 %collective-permute-done.32.refs_5_.refs_8_ = bf16[256,768]{1,0:T(8,128)(2,1)S(1)} collective-permute-done((bf16[256,768]{1,0:T(8,128)(2,1)}, bf16[256,768]{1,0:T(8,128)(2,1)S(1)}, u32[]{:S(2)}, u32[]{:S(2)}) %collective-permute-start.32) | collective-permute-done | bytes 393248 | tf_op jit(solution)/shard_map/ppermute | solution.py:35
  98.2 4.8 %collective-permute-done.39.refs_13_.refs_16_ = bf16[256,768]{1,0:T(8,128)(2,1)S(1)} collective-permute-done((bf16[256,768]{1,0:T(8,128)(2,1)}, bf16[256,768]{1,0:T(8,128)(2,1)S(1)}, u32[]{:S(2)}, u32[]{:S(2)}) %collective-permute-start.39) | collective-permute-done | bytes 393248 | tf_op jit(solution)/shard_map/ppermute | solution.py:35
  106.1 4.2 %collective-permute-done.40.refs_14_.refs_17_ = bf16[256,768]{1,0:T(8,128)(2,1)S(1)} collective-permute-done((bf16[256,768]{1,0:T(8,128)(2,1)S(1)}, bf16[256,768]{1,0:T(8,128)(2,1)S(1)}, u32[]{:S(2)}, u32[]{:S(2)}) %collective-permute-start.40) | collective-permute-done | bytes 393248 | tf_op jit(solution)/shard_map/ppermute | solution.py:35
  115.9 13.5 %attend.1 = (f32[256,768]{1,0:T(8,128)}, f32[256,768]{1,0:T(8,128)}) custom-call(bf16[256,768]{1,0:T(8,128)(2,1)} %get-tuple-element.50.refs_0_, bf16[256,128]{1,0:T(8,128)(2,1)} %select_convert_fusion.4.refs_1_.refs_4_, bf16[8,256,128]{2,1,0:T(8,128)(2,1)} %select_convert_fusion.refs_2_.refs_5_, bf16[256,768]{1,0:T(8,128)(2,1)} %get-tuple-element.51.refs_3_.refs_6_, ...), custom_call_target="tpu_custom_call" | custom-call | tf_op jit(solution)/shard_map/attend/pallas_call | solution.py:289
  130.6 19.0 %forward_and_head.1 = (bf16[256,768]{1,0:T(8,128)(2,1)}, f32[8,768]{1,0:T(8,128)}, f32[8,2432]{1,0:T(8,128)}, f32[256,768]{1,0:T(8,128)}, f32[256,768]{1,0:T(8,1...) custom-call(s32[2,8]{1,0:T(2,128)} %get-tuple-element.142.owners, ...), custom_call_target="tpu_custom_call" | custom-call | tf_op jit(solution)/shard_map/forward_and_head/pallas_call | solution.py:538
  149.6 15.9 %backward_to_attention.1 = (f32[8,768]{1,0:T(8,128)}, f32[256,768]{1,0:T(8,128)}, bf16[256,768]{1,0:T(8,128)(2,1)}, bf16[4,480,768]{2,1,0:T(8,128)(2,1)}, bf16[4,480,768]{2,1,0:T(8,128)(2,1)}) custom-call(s32[2,8]{1,0:T(2,128)} %get-tuple-element.142.owners, bf16[2,96,768]{2,1,0:T(8,128)(2,1)} %copy-done.2, ...), custom_call_target="tpu_custom_call" | custom-call | tf_op jit(solution)/shard_map/backward_to_attention/pallas_call | solution.py:622
  165.5 27.3 %attend_back.1 = (bf16[256,768]{1,0:T(8,128)(2,1)}, bf16[4,256,768]{2,1,0:T(8,128)(2,1)}, bf16[4,256,768]{2,1,0:T(8,128)(2,1)}, bf16[4,256,768]{2,1,0:T(8,128)(2,1)}, bf16[4,256,768]{2,1,0:T(8,128)(2,1)}) custom-call(bf16[256,768]{1,0:T(8,128)(2,1)} %get-tuple-element.50.refs_0_, bf16[256,768]{1,0:T(8,128)(2,1)} %get-tuple-element.60.refs_1_, ...), custom_call_target="tpu_custom_call" | custom-call | tf_op jit(solution)/shard_map/attend_back/pallas_call | solution.py:374
  198.2 3.1 collective-permute-done.46
  202.8 2.9 collective-permute-done.47
  222.0 11.3 %collective-permute-done.49 = bf16[2,256,768]{2,1,0:T(8,128)(2,1)S(1)} collective-permute-done((bf16[2,256,768]{2,1,0:T(8,128)(2,1)}, bf16[2,256,768]{2,1,0:T(8,128)(2,1)S(1)}, u32[]{:S(2)}, u32[]{:S(2)}) %collective-permute-start.49) | collective-permute-done | bytes 786464 | tf_op jit(solution)/shard_map/ppermute | solution.py:35
  235.7 3.3 collective-permute-done.52
  246.9 5.7 %collective-permute-done.53 = bf16[256,768]{1,0:T(8,128)(2,1)S(1)} collective-permute-done((bf16[256,768]{1,0:T(8,128)(2,1)S(1)}, bf16[256,768]{1,0:T(8,128)(2,1)S(1)}, u32[]{:S(2)}, u32[]{:S(2)}) %collective-permute-start.53) | collective-permute-done | bytes 393248 | tf_op jit(solution)/shard_map/ppermute | solution.py:35
  254.8 6.6 %input_gradients.1 = (f32[8,768]{1,0:T(8,128)}, f32[256,768]{1,0:T(8,128)}, bf16[4,288,768]{2,1,0:T(8,128)(2,1)}, bf16[4,288,768]{2,1,0:T(8,128)(2,1)}) custom-call(s32[2,8]{1,0:T(2,128)} %get-tuple-element.141.owners, bf16[3,96,768]{2,1,0:T(8,128)(2,1)} %copy-done, bf16[3,96,768]{2,1,0:T(8,128)(2,1)} %collective-permute-done.21.refs_1_, ...), custom_call_target="tpu_custom_call" | custom-call | tf_op jit(solution)/shard_map/input_gradients/pallas_call | solution.py:686
  265.2 6.5 %collective-permute-done.61 = f32[24,768]{1,0:T(8,128)S(1)} collective-permute-done((f32[24,768]{1,0:T(8,128)S(1)}, f32[24,768]{1,0:T(8,128)S(1)}, u32[]{:S(2)}, u32[]{:S(2)}) %collective-permute-start.61) | collective-permute-done | bytes 73760 | tf_op jit(solution)/shard_map/ppermute | solution.py:35
  289.0 34.9 %collective-permute-done.73 = bf16[384,768]{1,0:T(8,128)(2,1)S(1)} collective-permute-done((bf16[384,768]{1,0:T(8,128)(2,1)S(1)}, bf16[384,768]{1,0:T(8,128)(2,1)S(1)}, u32[]{:S(2)}, u32[]{:S(2)}) %collective-permute-start.73) | collective-permute-done | bytes 589856 | tf_op jit(solution)/shard_map/ppermute | solution.py:35
  334.3 3.3 collective-permute-start.55
  344.6 4.5 %collective-permute-done.67 = bf16[480,768]{1,0:T(8,128)(2,1)} collective-permute-done((bf16[480,768]{1,0:T(8,128)(2,1)}, bf16[480,768]{1,0:T(8,128)(2,1)}, u32[]{:S(2)}, u32[]{:S(2)}) %collective-permute-start.67) | collective-permute-done | bytes 737312 | tf_op jit(solution)/shard_map/ppermute | solution.py:35
  352.6 10.7 %collective-permute-done.55 = bf16[2,288,768]{2,1,0:T(8,128)(2,1)} collective-permute-done((bf16[2,288,768]{2,1,0:T(8,128)(2,1)}, bf16[2,288,768]{2,1,0:T(8,128)(2,1)}, u32[]{:S(2)}, u32[]{:S(2)}) %collective-permute-start.55) | collective-permute-done | bytes 884768 | tf_op jit(solution)/shard_map/ppermute | solution.py:35
  366.3 6.5 %collective-permute-done.56 = bf16[288,768]{1,0:T(8,128)(2,1)S(1)} collective-permute-done((bf16[288,768]{1,0:T(8,128)(2,1)S(1)}, bf16[288,768]{1,0:T(8,128)(2,1)S(1)}, u32[]{:S(2)}, u32[]{:S(2)}) %collective-permute-start.56) | collective-permute-done | bytes 442400 | tf_op jit(solution)/shard_map/ppermute | solution.py:35
  376.7 3.5 collective-permute-start.70
  382.6 7.5 %collective-permute-done.70 = bf16[240,768]{1,0:T(8,128)(2,1)S(1)} collective-permute-done((bf16[240,768]{1,0:T(8,128)(2,1)S(1)}, bf16[240,768]{1,0:T(8,128)(2,1)S(1)}, u32[]{:S(2)}, u32[]{:S(2)}) %collective-permute-start.70) | collective-permute-done | bytes 368672 | tf_op jit(solution)/shard_map/ppermute | solution.py:35
  390.2 3.0 collective-permute-done.58
  395.2 4.0 collective-permute-done.59
  (323 shorter events, 134.7 us)
Async XLA Ops:
  1.8 17.7 %collective-permute-start = (bf16[2,96,768]{2,1,0:T(8,128)(2,1)S(1)}, bf16[2,96,768]{2,1,0:T(8,128)(2,1)}, u32[]{:S(2)}, u32[]{:S(2)}) collective-permute-start(bf16[2,96,768]{2,1,0:T(8,128)(2,1)S(1)} %pad_maximum_fusion.3.refs_0_), channel_id=1, source_target_pairs={{0,4},{1,5},{2,6},{3,7},{4,0},{5,1},{6,2},{7,3},{8,10},{9,11},{10,... | collective-permute-start | bytes 884744 | tf_op jit(solution)/shard_map/ppermute | solution.py:35
  6.0 18.7 %collective-permute-start.24 = (bf16[3,96,768]{2,1,0:T(8,128)(2,1)S(1)}, bf16[3,96,768]{2,1,0:T(8,128)(2,1)S(1)}, u32[]{:S(2)}, u32[]{:S(2)}) collective-permute-start(bf16[3,96,768]{2,1,0:T(8,128)(2,1)S(1)} %pad_maximum_fusion.1.refs_0_), channel_id=1, source_target_pairs={{0,1},{1,0},{2,3},{3,2},{4,5},{5,4},{6,7},{7,6},{8,9},{9,8},{10,11... | collective-permute-start | bytes 1327112 | tf_op jit(solution)/shard_map/ppermute | solution.py:35
  6.0 18.7 %collective-permute-start.21 = (bf16[3,96,768]{2,1,0:T(8,128)(2,1)S(1)}, bf16[3,96,768]{2,1,0:T(8,128)(2,1)}, u32[]{:S(2)}, u32[]{:S(2)}) collective-permute-start(bf16[3,96,768]{2,1,0:T(8,128)(2,1)S(1)} %pad_maximum_fusion.1.refs_0_), channel_id=1, source_target_pairs={{0,2},{1,3},{2,0},{3,1},{4,6},{5,7},{6,4},{7,5},{8,12},{9,13},{10,... | collective-permute-start | bytes 1327112 | tf_op jit(solution)/shard_map/ppermute | solution.py:35
  30.9 22.7 %collective-permute-start.14 = (bf16[384,768]{1,0:T(8,128)(2,1)S(1)}, bf16[384,768]{1,0:T(8,128)(2,1)S(1)}, u32[]{:S(2)}, u32[]{:S(2)}) collective-permute-start(bf16[384,768]{1,0:T(8,128)(2,1)S(1)} %copy-done.4), channel_id=1, source_target_pairs={{0,4},{1,5},{2,6},{3,7},{4,0},{5,1},{6,2},{7,3},{8,10},{9,11},{10,... | collective-permute-start | bytes 1769480 | tf_op jit(solution)/shard_map/ppermute | solution.py:35
  32.7 24.5 %collective-permute-start.25 = (bf16[3,96,768]{2,1,0:T(8,128)(2,1)}, bf16[3,96,768]{2,1,0:T(8,128)(2,1)}, u32[]{:S(2)}, u32[]{:S(2)}) collective-permute-start(bf16[3,96,768]{2,1,0:T(8,128)(2,1)} %collective-permute-done.21.refs_1_), channel_id=1, source_target_pairs={{0,1},{1,0},{2,3},{3,2},{4,5},{5,4},{6,7},{7,6},{8,9},{9,8},{10,11... | collective-permute-start | bytes 1327112 | tf_op jit(solution)/shard_map/ppermute | solution.py:35
  41.0 21.8 %collective-permute-start.22 = (bf16[3,96,768]{2,1,0:T(8,128)(2,1)}, bf16[3,96,768]{2,1,0:T(8,128)(2,1)}, u32[]{:S(2)}, u32[]{:S(2)}) collective-permute-start(bf16[3,96,768]{2,1,0:T(8,128)(2,1)} %collective-permute-done.21.refs_1_), channel_id=1, source_target_pairs={{0,4},{1,5},{2,6},{3,7},{4,0},{5,1},{6,2},{7,3},{8,10},{9,11},{10,... | collective-permute-start | bytes 1327112 | tf_op jit(solution)/shard_map/ppermute | solution.py:35
  41.5 22.0 %collective-permute-start.27 = (bf16[3,96,768]{2,1,0:T(8,128)(2,1)}, bf16[3,96,768]{2,1,0:T(8,128)(2,1)}, u32[]{:S(2)}, u32[]{:S(2)}) collective-permute-start(bf16[3,96,768]{2,1,0:T(8,128)(2,1)} %collective-permute-done.23.refs_3_), channel_id=1, source_target_pairs={{0,1},{1,0},{2,3},{3,2},{4,5},{5,4},{6,7},{7,6},{8,9},{9,8},{10,11... | collective-permute-start | bytes 1327112 | tf_op jit(solution)/shard_map/ppermute | solution.py:35
  54.6 19.1 %collective-permute-start.11 = (bf16[96,3072]{1,0:T(8,128)(2,1)S(1)}, bf16[96,3072]{1,0:T(8,128)(2,1)S(1)}, u32[]{:S(2)}, u32[]{:S(2)}) collective-permute-start(bf16[96,3072]{1,0:T(8,128)(2,1)S(1)} %collective-permute-done.7.refs_9_), channel_id=1, source_target_pairs={{0,1},{1,0},{2,3},{3,2},{4,5},{5,4},{6,7},{7,6},{8,9},{9,8},{10,11... | collective-permute-start | bytes 1769480 | tf_op jit(solution)/shard_map/ppermute | solution.py:35
  56.2 17.6 %collective-permute-start.9 = (bf16[96,3072]{1,0:T(8,128)(2,1)S(1)}, bf16[96,3072]{1,0:T(8,128)(2,1)}, u32[]{:S(2)}, u32[]{:S(2)}) collective-permute-start(bf16[96,3072]{1,0:T(8,128)(2,1)S(1)} %collective-permute-done.7.refs_9_), channel_id=1, source_target_pairs={{0,8},{1,9},{2,10},{3,11},{4,12},{5,13},{6,14},{7,15},{8,0},{9,1},... | collective-permute-start | bytes 1769480 | tf_op jit(solution)/shard_map/ppermute | solution.py:35
  57.2 16.9 %collective-permute-start.8 = (bf16[96,3072]{1,0:T(8,128)(2,1)S(1)}, bf16[96,3072]{1,0:T(8,128)(2,1)}, u32[]{:S(2)}, u32[]{:S(2)}) collective-permute-start(bf16[96,3072]{1,0:T(8,128)(2,1)S(1)} %collective-permute-done.7.refs_9_), channel_id=1, source_target_pairs={{0,2},{1,3},{2,0},{3,1},{4,6},{5,7},{6,4},{7,5},{8,12},{9,13},{10,... | collective-permute-start | bytes 1769480 | tf_op jit(solution)/shard_map/ppermute | solution.py:35
  62.8 21.6 %collective-permute-start.16 = (bf16[384,768]{1,0:T(8,128)(2,1)}, bf16[384,768]{1,0:T(8,128)(2,1)}, u32[]{:S(2)}, u32[]{:S(2)}) collective-permute-start(bf16[384,768]{1,0:T(8,128)(2,1)} %copy-done.8), channel_id=1, source_target_pairs={{0,8},{1,9},{2,10},{3,11},{4,12},{5,13},{6,14},{7,15},{8,0},{9,1},... | collective-permute-start | bytes 1769480 | tf_op jit(solution)/shard_map/ppermute | solution.py:35
  65.6 20.6 %collective-permute-start.15 = (bf16[384,768]{1,0:T(8,128)(2,1)}, bf16[384,768]{1,0:T(8,128)(2,1)}, u32[]{:S(2)}, u32[]{:S(2)}) collective-permute-start(bf16[384,768]{1,0:T(8,128)(2,1)} %copy-done.8), channel_id=1, source_target_pairs={{0,2},{1,3},{2,0},{3,1},{4,6},{5,7},{6,4},{7,5},{8,12},{9,13},{10,... | collective-permute-start | bytes 1769480 | tf_op jit(solution)/shard_map/ppermute | solution.py:35
  73.8 20.7 %collective-permute-start.32 = (bf16[256,768]{1,0:T(8,128)(2,1)}, bf16[256,768]{1,0:T(8,128)(2,1)S(1)}, u32[]{:S(2)}, u32[]{:S(2)}) collective-permute-start(bf16[256,768]{1,0:T(8,128)(2,1)} %get-tuple-element.51.refs_3_.refs_6_), channel_id=1, source_target_pairs={{0,2},{1,3},{2,0},{3,1},{4,6},{5,7},{6,4},{7,5},{8,10},{9,11},{10,... | collective-permute-start | bytes 1179656 | tf_op jit(solution)/shard_map/ppermute | solution.py:35
  74.2 20.4 %collective-permute-start.31 = (bf16[256,768]{1,0:T(8,128)(2,1)}, bf16[256,768]{1,0:T(8,128)(2,1)S(1)}, u32[]{:S(2)}, u32[]{:S(2)}) collective-permute-start(bf16[256,768]{1,0:T(8,128)(2,1)} %get-tuple-element.51.refs_3_.refs_6_), channel_id=1, source_target_pairs={{0,4},{1,5},{2,6},{3,7},{4,0},{5,1},{6,2},{7,3},{8,12},{9,13},{10,... | collective-permute-start | bytes 1179656 | tf_op jit(solution)/shard_map/ppermute | solution.py:35
  110.4 19.0 %collective-permute-start.18 = (bf16[384,768]{1,0:T(8,128)(2,1)S(1)}, bf16[384,768]{1,0:T(8,128)(2,1)S(1)}, u32[]{:S(2)}, u32[]{:S(2)}) collective-permute-start(bf16[384,768]{1,0:T(8,128)(2,1)S(1)} %copy-done.9), channel_id=1, source_target_pairs={{0,1},{1,0},{2,3},{3,2},{4,5},{5,4},{6,7},{7,6},{8,9},{9,8},{10,11... | collective-permute-start | bytes 1769480 | tf_op jit(solution)/shard_map/ppermute | solution.py:35
  111.0 18.5 %collective-permute-start.13 = (bf16[96,3072]{1,0:T(8,128)(2,1)}, bf16[96,3072]{1,0:T(8,128)(2,1)S(1)}, u32[]{:S(2)}, u32[]{:S(2)}) collective-permute-start(bf16[96,3072]{1,0:T(8,128)(2,1)} %collective-permute-done.9.refs_11_), channel_id=1, source_target_pairs={{0,1},{1,0},{2,3},{3,2},{4,5},{5,4},{6,7},{7,6},{8,9},{9,8},{10,11... | collective-permute-start | bytes 1769480 | tf_op jit(solution)/shard_map/ppermute | solution.py:35
  111.1 18.4 %collective-permute-start.12 = (bf16[96,3072]{1,0:T(8,128)(2,1)}, bf16[96,3072]{1,0:T(8,128)(2,1)S(1)}, u32[]{:S(2)}, u32[]{:S(2)}) collective-permute-start(bf16[96,3072]{1,0:T(8,128)(2,1)} %collective-permute-done.8.refs_10_), channel_id=1, source_target_pairs={{0,1},{1,0},{2,3},{3,2},{4,5},{5,4},{6,7},{7,6},{8,9},{9,8},{10,11... | collective-permute-start | bytes 1769480 | tf_op jit(solution)/shard_map/ppermute | solution.py:35
  111.7 17.8 %collective-permute-start.20 = (bf16[384,768]{1,0:T(8,128)(2,1)}, bf16[384,768]{1,0:T(8,128)(2,1)}, u32[]{:S(2)}, u32[]{:S(2)}) collective-permute-start(bf16[384,768]{1,0:T(8,128)(2,1)} %collective-permute-done.16.refs_19_), channel_id=1, source_target_pairs={{0,1},{1,0},{2,3},{3,2},{4,5},{5,4},{6,7},{7,6},{8,9},{9,8},{10,11... | collective-permute-start | bytes 1769480 | tf_op jit(solution)/shard_map/ppermute | solution.py:35
  112.0 17.5 %collective-permute-start.19 = (bf16[384,768]{1,0:T(8,128)(2,1)}, bf16[384,768]{1,0:T(8,128)(2,1)}, u32[]{:S(2)}, u32[]{:S(2)}) collective-permute-start(bf16[384,768]{1,0:T(8,128)(2,1)} %collective-permute-done.15.refs_18_), channel_id=1, source_target_pairs={{0,1},{1,0},{2,3},{3,2},{4,5},{5,4},{6,7},{7,6},{8,9},{9,8},{10,11... | collective-permute-start | bytes 1769480 | tf_op jit(solution)/shard_map/ppermute | solution.py:35
  192.8 21.2 %collective-permute-start.48 = (bf16[4,256,768]{2,1,0:T(8,128)(2,1)}, bf16[4,256,768]{2,1,0:T(8,128)(2,1)}, u32[]{:S(2)}, u32[]{:S(2)}) collective-permute-start(bf16[4,256,768]{2,1,0:T(8,128)(2,1)} %get-tuple-element.64), channel_id=1, source_target_pairs={{0,1},{1,0},{2,3},{3,2},{4,5},{5,4},{6,7},{7,6},{8,9},{9,8},{10,11... | collective-permute-start | bytes 4718600 | tf_op jit(solution)/shard_map/ppermute | solution.py:35
  193.2 24.4 %collective-permute-start.51 = (bf16[4,256,768]{2,1,0:T(8,128)(2,1)}, bf16[4,256,768]{2,1,0:T(8,128)(2,1)}, u32[]{:S(2)}, u32[]{:S(2)}) collective-permute-start(bf16[4,256,768]{2,1,0:T(8,128)(2,1)} %get-tuple-element.66), channel_id=1, source_target_pairs={{0,1},{1,0},{2,3},{3,2},{4,5},{5,4},{6,7},{7,6},{8,9},{9,8},{10,11... | collective-permute-start | bytes 4718600 | tf_op jit(solution)/shard_map/ppermute | solution.py:35
  193.7 47.7 %collective-permute-start.71 = (bf16[4,384,768]{2,1,0:T(8,128)(2,1)}, bf16[4,384,768]{2,1,0:T(8,128)(2,1)S(1)}, u32[]{:S(2)}, u32[]{:S(2)}) collective-permute-start(bf16[4,384,768]{2,1,0:T(8,128)(2,1)} %get-tuple-element.77), channel_id=1, source_target_pairs={{0,1},{1,0},{2,3},{3,2},{4,5},{5,4},{6,7},{7,6},{8,9},{9,8},{10,11... | collective-permute-start | bytes 7077896 | tf_op jit(solution)/shard_map/ppermute | solution.py:35
  198.2 79.5 %collective-permute-start.65 = (bf16[4,480,768]{2,1,0:T(8,128)(2,1)}, bf16[4,480,768]{2,1,0:T(8,128)(2,1)}, u32[]{:S(2)}, u32[]{:S(2)}) collective-permute-start(bf16[4,480,768]{2,1,0:T(8,128)(2,1)} %get-tuple-element.75), channel_id=1, source_target_pairs={{0,1},{1,0},{2,3},{3,2},{4,5},{5,4},{6,7},{7,6},{8,9},{9,8},{10,11... | collective-permute-start | bytes 8847368 | tf_op jit(solution)/shard_map/ppermute | solution.py:35
  216.5 16.8 %collective-permute-start.49 = (bf16[2,256,768]{2,1,0:T(8,128)(2,1)}, bf16[2,256,768]{2,1,0:T(8,128)(2,1)S(1)}, u32[]{:S(2)}, u32[]{:S(2)}) collective-permute-start(bf16[2,256,768]{2,1,0:T(8,128)(2,1)} %add_convert_fusion.4), channel_id=1, source_target_pairs={{0,2},{1,3},{2,0},{3,1},{4,6},{5,7},{6,4},{7,5},{8,10},{9,11},{10,... | collective-permute-start | bytes 2359304 | tf_op jit(solution)/shard_map/ppermute | solution.py:35
  219.8 19.3 %collective-permute-start.52 = (bf16[2,256,768]{2,1,0:T(8,128)(2,1)}, bf16[2,256,768]{2,1,0:T(8,128)(2,1)}, u32[]{:S(2)}, u32[]{:S(2)}) collective-permute-start(bf16[2,256,768]{2,1,0:T(8,128)(2,1)} %add_convert_fusion.3), channel_id=1, source_target_pairs={{0,4},{1,5},{2,6},{3,7},{4,0},{5,1},{6,2},{7,3},{8,12},{9,13},{10,... | collective-permute-start | bytes 2359304 | tf_op jit(solution)/shard_map/ppermute | solution.py:35
  243.1 38.5 %collective-permute-start.72 = (bf16[2,384,768]{2,1,0:T(8,128)(2,1)}, bf16[2,384,768]{2,1,0:T(8,128)(2,1)}, u32[]{:S(2)}, u32[]{:S(2)}) collective-permute-start(bf16[2,384,768]{2,1,0:T(8,128)(2,1)} %add_convert_fusion.1), channel_id=1, source_target_pairs={{0,2},{1,3},{2,0},{3,1},{4,6},{5,7},{6,4},{7,5},{8,10},{9,11},{10,... | collective-permute-start | bytes 3538952 | tf_op jit(solution)/shard_map/ppermute | solution.py:35
  273.2 59.5 %collective-permute-start.54 = (bf16[4,288,768]{2,1,0:T(8,128)(2,1)}, bf16[4,288,768]{2,1,0:T(8,128)(2,1)S(1)}, u32[]{:S(2)}, u32[]{:S(2)}) collective-permute-start(bf16[4,288,768]{2,1,0:T(8,128)(2,1)} %get-tuple-element.70), channel_id=1, source_target_pairs={{0,1},{1,0},{2,3},{3,2},{4,5},{5,4},{6,7},{7,6},{8,9},{9,8},{10,11... | collective-permute-start | bytes 5308424 | tf_op jit(solution)/shard_map/ppermute | solution.py:35
  279.5 46.4 %collective-permute-start.66 = (bf16[2,480,768]{2,1,0:T(8,128)(2,1)S(1)}, bf16[2,480,768]{2,1,0:T(8,128)(2,1)S(1)}, u32[]{:S(2)}, u32[]{:S(2)}) collective-permute-start(bf16[2,480,768]{2,1,0:T(8,128)(2,1)S(1)} %add_convert_fusion), channel_id=1, source_target_pairs={{0,4},{1,5},{2,6},{3,7},{4,0},{5,1},{6,2},{7,3},{8,12},{9,13},{10,... | collective-permute-start | bytes 4423688 | tf_op jit(solution)/shard_map/ppermute | solution.py:35
  282.9 40.9 %collective-permute-start.73 = (bf16[384,768]{1,0:T(8,128)(2,1)S(1)}, bf16[384,768]{1,0:T(8,128)(2,1)S(1)}, u32[]{:S(2)}, u32[]{:S(2)}) collective-permute-start(bf16[384,768]{1,0:T(8,128)(2,1)S(1)} %fusion.1), channel_id=1, source_target_pairs={{0,4},{1,5},{2,6},{3,7},{4,0},{5,1},{6,2},{7,3},{8,12},{9,13},{10,... | collective-permute-start | bytes 1769480 | tf_op jit(solution)/shard_map/ppermute | solution.py:35
  329.3 19.7 %collective-permute-start.67 = (bf16[480,768]{1,0:T(8,128)(2,1)}, bf16[480,768]{1,0:T(8,128)(2,1)}, u32[]{:S(2)}, u32[]{:S(2)}) collective-permute-start(bf16[480,768]{1,0:T(8,128)(2,1)} %fusion), channel_id=1, source_target_pairs={{0,2},{1,3},{2,0},{3,1},{4,6},{5,7},{6,4},{7,5},{8,10},{9,11},{10,... | collective-permute-start | bytes 2211848 | tf_op jit(solution)/shard_map/ppermute | solution.py:35
  334.3 29.0 %collective-permute-start.55 = (bf16[2,288,768]{2,1,0:T(8,128)(2,1)}, bf16[2,288,768]{2,1,0:T(8,128)(2,1)}, u32[]{:S(2)}, u32[]{:S(2)}) collective-permute-start(bf16[2,288,768]{2,1,0:T(8,128)(2,1)} %add_convert_fusion.2), channel_id=1, source_target_pairs={{0,2},{1,3},{2,0},{3,1},{4,6},{5,7},{6,4},{7,5},{8,10},{9,11},{10,... | collective-permute-start | bytes 2654216 | tf_op jit(solution)/shard_map/ppermute | solution.py:35
  342.1 22.4 %collective-permute-start.76 = (bf16[192,768]{1,0:T(8,128)(2,1)S(1)}, bf16[192,768]{1,0:T(8,128)(2,1)S(1)}, u32[]{:S(2)}, u32[]{:S(2)}) collective-permute-start(bf16[192,768]{1,0:T(8,128)(2,1)S(1)} %add_convert_fusion.12), channel_id=1, source_target_pairs={{0,8},{1,9},{2,10},{3,11},{4,12},{5,13},{6,14},{7,15},{8,0},{9,1},... | collective-permute-start | bytes 884744 | tf_op jit(solution)/shard_map/ppermute | solution.py:35
  (97 other events, 1320.5 us)

commit v2 on v1

v2 whole, which is shorter than its diff:
```python
import functools

import jax
import jax.numpy as jnp
from jax import lax
from jax.experimental import pallas as pl
from jax.experimental.pallas import tpu as pltpu
from jax.sharding import PartitionSpec as P

D = 768
HEADS = 12
HEAD_DIM = 64
FF = 3072
CLASSES = 3
PAIR = 2 * HEAD_DIM
ROWS = 256
EPSILON = 1e-06
FAR = -1e30
LIMIT = 56 * 1024 * 1024
F32, BF16 = jnp.float32, jnp.bfloat16

QUERY_B, VALUE_B, PROJ_B, NORM_G, NORM_S, DOWN_B, FINAL_G, FINAL_S, POOL_B, CLASS_W, UP_B = (
    0, 1, 2, 3, 4, 5, 6, 7, 8, 9, 12,
)
TABLE = 16


def swap(value, partner):
    dp, seq = lax.axis_size("dp"), lax.axis_size("seq")
    pairs = []
    for z in range(dp):
        for i in range(seq):
            to_z, to_i = partner(z, i)
            pairs.append((z * seq + i, to_z * seq + to_i))
    return lax.ppermute(value, ("dp", "seq"), pairs)


def along(bit):
    return lambda z, i: (z, i ^ bit)


def is_small():
    return lax.axis_size("seq") == 8 and lax.axis_size("dp") == 4


class Shared:
    def __init__(self, shard, role):
        self.shard, self.role = shard, role

    def near(self):
        role = self.role
        self.one = swap(self.shard, lambda z, i: (z, i ^ (2 if (z + role) % 2 == 0 else 4)))

    def far(self):
        role = self.role
        self.both = swap(self.one, lambda z, i: (z, i ^ (4 if (z + role) % 2 == 0 else 2)))
        self.blocks = [self.shard, self.one]
        self.crossed = [swap(block, along(1)) for block in self.blocks]

    def rest(self, *earlier):
        self.other = swap(after(self.one, *earlier), lambda z, i: (z ^ 1, i))

    def finish(self):
        late = [self.both, self.other]
        return self.blocks + late + self.crossed + [swap(block, along(1)) for block in late]

    def owners(self):
        me, z = lax.axis_index("seq"), lax.axis_index("dp")
        near = jnp.where((z + self.role) % 2 == 0, 2, 4)
        owners = [me, me ^ near, me ^ 6, me ^ (6 - near)]
        owners = [owners[k] for k in (0, 1, 2, 3)] + [owners[k] ^ 1 for k in (0, 1, 2, 3)]
        return jnp.stack(owners)


def gather_tokens(tokens):
    if not is_small():
        return [tokens]
    far = swap(tokens, along(6))
    return [tokens, swap(tokens, along(2)), swap(tokens, along(4)), far]


def exchange(pieces):
    return [pieces[0]] + [swap(pieces[s], along(2 * s)) for s in range(1, len(pieces))]


def slot_owners():
    if not is_small():
        return jnp.arange(lax.axis_size("seq"), dtype=jnp.int32)
    return lax.axis_index("seq") ^ jnp.array([0, 2, 4, 6, 1, 3, 5, 7], jnp.int32)


def add(*terms):
    return functools.reduce(jnp.add, [term.astype(F32) for term in terms])


class Scatter:
    def __init__(self, parts):
        self.firsts, self.seconds, self.own = parts[0:2], parts[2:4], parts[4]
        self.comes = [swap(a, along(bit)) for a, bit in zip(self.firsts, (2, 4))]

    def combine(self, *earlier):
        seconds = after(self.seconds, *earlier)
        self.sends = [add(a, come[1]).astype(BF16) for a, come in zip(seconds, self.comes)]

    def turn(self):
        self.lasts = [swap(a, along(bit)) for a, bit in zip(self.sends, (4, 2))]

    def total(self):
        half = self.own.shape[0] // 2
        owns = (self.own[:half], self.own[half:])
        return jnp.concatenate(
            [add(own, come[0], last) for own, come, last in zip(owns, self.comes, self.lasts)]
        )


def after(values, *others):
    return lax.optimization_barrier((values, others))[0]


class SumDp:
    def __init__(self, shard):
        z = lax.axis_index("dp")
        half = shard.shape[0] // 2
        self.low = jnp.logical_or(z == 0, z == 3)
        first, second = shard[:half], shard[half:]
        self.keep = jnp.where(self.low, first, second)
        self.come = swap(
            jnp.where(self.low, second, first).astype(BF16), lambda z, i: (z ^ 1, i)
        )

    def across(self):
        self.pair = add(self.keep, self.come).astype(BF16)
        self.cross = swap(self.pair, lambda z, i: (z ^ 3, i))

    def back(self):
        total = add(self.pair, self.cross).astype(BF16)
        come = swap(total, lambda z, i: (z ^ 1, i))
        low = self.low
        return jnp.concatenate(
            [jnp.where(low, total, come), jnp.where(low, come, total)], axis=0
        ).astype(F32)


def sum_dp(shard):
    if not is_small():
        return lax.psum(shard.astype(BF16), "dp").astype(F32)
    total = SumDp(shard)
    total.across()
    return total.back()


def sum_seq(value):
    if not is_small():
        return lax.psum(value, "seq")
    for bit in (1, 2, 4):
        value = value + swap(value, along(bit))
    return value


def sum_all(value):
    value = sum_seq(value)
    if not is_small():
        return lax.psum(value, "dp")
    for bit in (1, 2):
        value = value + swap(value, lambda z, i: (z ^ bit, i))
    return value


def stack_dp(value):
    if not is_small():
        return lax.all_gather(value, "dp", axis=0, tiled=True)
    for bit in (1, 2):
        value = jnp.concatenate([value, swap(value, lambda z, i: (z ^ bit, i))], axis=0)
    return value


def dot(left, right, contract=((1,), (0,))):
    return lax.dot_general(left, right, (contract, ((), ())), preferred_element_type=F32)


def call(body, name, micros, **kwargs):
    return pl.pallas_call(
        body,
        name=name,
        cost_estimate=pl.CostEstimate(
            flops=int(micros * 1.1e9), transcendentals=0, bytes_accessed=int(micros * 1e6)
        ),
        compiler_params=pltpu.CompilerParams(vmem_limit_bytes=LIMIT),
        **kwargs,
    )


VMEM = pl.BlockSpec(memory_space=pltpu.VMEM)
ANY = pl.BlockSpec(memory_space=pl.ANY)
SMEM = pl.BlockSpec(memory_space=pltpu.SMEM)


def start(copies):
    for copy in copies:
        copy.start()
    return copies


def wait(copies):
    for copy in copies:
        copy.wait()


def block_copies(places, line, refs, target, sems, part=None):
    copies = []
    for slot, ref in enumerate(refs):
        source = ref if part is None else ref.at[part]
        rows = source.shape[-2]
        first = pl.multiple_of(places[line, slot] * rows, rows)
        if len(source.shape) == 3:
            place = target.at[:, pl.ds(first, rows), :]
        else:
            place = target.at[pl.ds(first, rows), :]
        copies.append(pltpu.make_async_copy(source, place, sems.at[slot]))
    return start(copies)


def weight_refs(weights):
    return [ref.at[s] for ref in weights for s in range(ref.shape[0])]


def qkv_kernel(blocks, sides, places, *refs):
    tokens, refs = refs[:blocks], refs[blocks:]
    weights, (bias, query, keyval, held, sems) = refs[:sides], refs[sides:]
    wait(block_copies(places, 0, weight_refs(weights), held, sems))
    for s in range(query.shape[0]):
        rows = tokens[s][...]
        keyval[0, s] = dot(rows, held[1]).astype(BF16)
        keyval[1, s] = (dot(rows, held[2]) + bias[1:2]).astype(BF16)
        query[s] = (dot(rows, held[0]) + bias[0:1]).astype(BF16)


def qkv_project(places, tokens, weights, bias):
    slots = len(tokens)
    lanes = weights[0].shape[-1]
    out = jax.ShapeDtypeStruct((slots, ROWS, lanes), BF16)
    pair = jax.ShapeDtypeStruct((2, slots, ROWS, lanes), BF16)
    return call(
        functools.partial(qkv_kernel, len(tokens), len(weights)),
        "qkv",
        5,
        out_shape=(out, pair),
        in_specs=[SMEM] + [VMEM] * len(tokens) + [ANY] * len(weights) + [VMEM],
        out_specs=(VMEM,) * 2,
        scratch_shapes=[
            pltpu.VMEM((3, D, lanes), BF16),
            pltpu.SemaphoreType.DMA((len(weights) * weights[0].shape[0],)),
        ],
    )(places, *tokens, *weights, bias)


def left_half(shape):
    return lax.broadcasted_iota(jnp.int32, shape, len(shape) - 1) < HEAD_DIM


def split3(value):
    high = value.astype(BF16).astype(F32)
    middle = (value - high).astype(BF16).astype(F32)
    low = (value - high - middle).astype(BF16).astype(F32)
    return high, middle, low


def spread3(value, docs, shape):
    lane = lax.broadcasted_iota(jnp.int32, shape, 1) % HEAD_DIM
    high, middle, low = split3(value)
    return jnp.where(
        lane == docs, high, jnp.where(lane == docs + 1, middle, jnp.where(lane == docs + 2, low, 0.0))
    )


def chunks_of(refs):
    number = 0
    for ref in refs:
        for index in range(ref.shape[1]):
            yield ref, index, number
            number += 1


def over_chunks(refs, step):
    if len(refs) > 1:
        for at in chunks_of(refs):
            step(*at)
    else:
        pl.loop(0, refs[0].shape[1])(lambda index: step(refs[0], index, index))


def attend_kernel(sides, docs, odd, *refs):
    query, feature_q, feature_k = refs[:3]
    keyvals = refs[3 : 3 + sides]
    slots = feature_q.shape[0]
    rest = refs[3 + sides :]
    wide, total, lows, (scores, acc, most) = rest[0], rest[1], rest[2:-3], rest[-3:]
    tile, slot = pl.program_id(0), pl.program_id(1)
    left = left_half((ROWS, PAIR))
    rows = query[0] * 0.125
    spare = feature_q[slot]

    def one_head(head):
        mine = left if head == 0 else jnp.logical_not(left)
        aug = jnp.where(mine, rows, spare)
        most[...] = jnp.full_like(most, FAR)

        def score_step(ref, index, number):
            full = jnp.where(mine, ref[0, index], feature_k[number])
            made = dot(aug, full, ((1,), (1,)))
            scores[number] = made
            most[...] = jnp.maximum(most[...], jnp.maximum(made[:, :PAIR], made[:, PAIR:]))

        over_chunks(keyvals, score_step)
        top = jnp.max(most[...], axis=1, keepdims=True)
        acc[...] = jnp.zeros_like(acc)

        def value_step(ref, index, number):
            full = jnp.where(mine, ref[1, index], feature_k[number])
            acc[...] += dot(jnp.exp(scores[number] - top).astype(BF16), full)

        over_chunks(keyvals, value_step)
        found = acc[...]
        lane = docs + (HEAD_DIM if head == 0 else 0)
        weight = found[:, lane : lane + 1]
        return found / weight, top + jnp.log(weight)

    result, sums = one_head(0)
    wide[0] = result
    total[0] = jnp.broadcast_to(sums, (ROWS, PAIR))

    def second_head():
        result, sums = one_head(1)
        wide[0] = jnp.where(left, wide[0], result)
        total[0] = jnp.where(left, total[0], sums)

    if odd:
        pl.when(tile < pl.num_programs(0) - 1)(second_head)
    else:
        second_head()
    for s in range(slots):

        @pl.when(slot == s)
        def _(s=s):
            lows[s][...] = wide[0].astype(BF16)


def slot_spec(array, base=0):
    return pl.BlockSpec((1, ROWS, PAIR), lambda tile, slot: (slot, 0, tile + base))


def tile_spec(array, base=0):
    lead = array.shape[:-1]
    return pl.BlockSpec(lead + (PAIR,), lambda tile, slot: (0,) * len(lead) + (tile + base,))


def fixed_spec(array):
    return pl.BlockSpec(array.shape, lambda tile, slot: (0,) * array.ndim)


def attend(query, keyvals, feature_q, feature_k, docs):
    slots, tiles = query.shape[0], query.shape[-1] // PAIR
    wide = jax.ShapeDtypeStruct(query.shape, F32)
    low = jax.ShapeDtypeStruct(wide.shape[1:], BF16)
    chunks = feature_k.shape[0]
    made = call(
        functools.partial(attend_kernel, len(keyvals), docs, slots > 1),
        "attend",
        15,
        grid=(tiles, slots),
        out_shape=(wide, wide) + (low,) * slots,
        in_specs=[slot_spec(query), fixed_spec(feature_q), fixed_spec(feature_k)]
        + [tile_spec(a) for a in keyvals],
        out_specs=(slot_spec(wide),) * 2 + (tile_spec(low),) * slots,
        scratch_shapes=[
            pltpu.VMEM((chunks, ROWS, ROWS), F32),
            pltpu.VMEM((ROWS, PAIR), F32),
            pltpu.VMEM((ROWS, PAIR), F32),
        ],
    )(query, feature_q, feature_k, *keyvals)
    return made[0], made[1], list(made[2:])


def attend_back_kernel(sides, docs, single, *refs):
    query, wide, total, feature_q, feature_k = refs[:5]
    slots = feature_q.shape[0]
    grads_in, keyvals = refs[5 : 5 + slots], refs[5 + slots : 5 + slots + sides]
    rest = refs[5 + slots + sides :]
    grad_q, outs, (grad, acc_q, acc_k, acc_v) = rest[0], rest[1 : 1 + sides], rest[1 + sides :]
    slot = pl.program_id(1)
    left = left_half((ROWS, PAIR))
    for s in range(slots):

        @pl.when(slot == s)
        def _(s=s):
            grad[...] = grads_in[s][...]

    @pl.when(slot == 0)
    def _():
        acc_k[...] = jnp.zeros_like(acc_k)
        acc_v[...] = jnp.zeros_like(acc_v)

    rows = query[0] * 0.125
    grads = grad[...]
    product = grads.astype(F32) * wide[0]
    spare = feature_q[slot].astype(F32)
    zero = jnp.zeros_like(rows)
    acc_q[...] = jnp.zeros_like(acc_q)

    def one_head(head):
        mine = left if head == 0 else jnp.logical_not(left)
        at = head * HEAD_DIM
        delta = jnp.sum(jnp.where(mine, product, 0.0), axis=1, keepdims=True)
        sums = total[0, :, at : at + 1]
        query_t = jnp.where(
            mine, rows.astype(F32), spare + spread3(-sums, docs, (ROWS, PAIR))
        ).T.astype(BF16)
        grad_t = jnp.where(
            mine, grads.astype(F32), spread3(-delta, docs, (ROWS, PAIR))
        ).T.astype(BF16)
        query_own, grad_own = jnp.where(mine, rows, zero), jnp.where(mine, grads, zero)

        def step(ref, index, number):
            key, value, feature = ref[0, index], ref[1, index], feature_k[number]
            soft = jnp.exp(dot(jnp.where(mine, key, feature), query_t))
            change = dot(jnp.where(mine, value, feature), grad_t)
            slope = (soft * change).astype(BF16)
            acc_v[number] += dot(soft.astype(BF16), grad_own)
            acc_k[number] += dot(slope, query_own)
            key_t = key.astype(F32).T[at : at + HEAD_DIM].astype(BF16)
            acc_q[at : at + HEAD_DIM] += dot(key_t, slope)

        over_chunks(keyvals, step)

    one_head(0)
    if not single:
        one_head(1)
    grad_q[0] = (acc_q[...].T * 0.125).astype(BF16)

    @pl.when(slot == slots - 1)
    def _():
        number = 0
        for out in outs:
            count = out.shape[1]
            out[0] = acc_k[number : number + count].astype(BF16)
            out[1] = acc_v[number : number + count].astype(BF16)
            number += count


def attend_back(query, keyvals, grads, wide, total, feature_q, feature_k, docs, base, tiles, single):
    slots = query.shape[0]
    chunks = feature_k.shape[0]
    outs = tuple(
        jax.ShapeDtypeStruct(a.shape[:-1] + (tiles * PAIR,), BF16) for a in (query, *keyvals)
    )
    made = call(
        functools.partial(attend_back_kernel, len(keyvals), docs, single),
        "attend_back",
        10 if single else 21,
        grid=(tiles, slots),
        out_shape=outs,
        in_specs=[slot_spec(a, base) for a in (query, wide, total)]
        + [fixed_spec(feature_q), fixed_spec(feature_k)]
        + [tile_spec(a, base) for a in (*grads, *keyvals)],
        out_specs=(slot_spec(outs[0]),) + tuple(tile_spec(a) for a in outs[1:]),
        scratch_shapes=[
            pltpu.VMEM((ROWS, PAIR), BF16),
            pltpu.VMEM((PAIR, ROWS), F32),
            pltpu.VMEM((chunks, ROWS, PAIR), F32),
            pltpu.VMEM((chunks, ROWS, PAIR), F32),
        ],
    )(query, wide, total, feature_q, feature_k, *grads, *keyvals)
    return made[0], list(made[1:])


def normalise(value):
    centred = value - jnp.mean(value, axis=-1, keepdims=True)
    inverse = lax.rsqrt(jnp.mean(centred * centred, axis=-1, keepdims=True) + EPSILON)
    return centred * inverse, inverse


def norm_back(grad, gain, unit, inverse):
    scaled = grad * gain
    return inverse * (
        scaled
        - jnp.mean(scaled, axis=-1, keepdims=True)
        - unit * jnp.mean(scaled * unit, axis=-1, keepdims=True)
    )


def erf(value):
    value = jnp.clip(value, -3.7439211627767994, 3.7439211627767994)
    square = value * value
    top = 0.00022905065861350646
    for factor in (0.0034082910107109506, 0.050955695062380861, 0.18520832239976145, 1.128379143519084):
        top = top * square + factor
    bottom = -1.1791602954361697e-7
    for factor in (
        0.000023547966471313185, 0.0010179625278914885, 0.014070470171167667,
        0.11098505178285362, 0.49746925110067538, 1.0,
    ):
        bottom = bottom * square + factor
    return value * top / bottom


def column_sum(value):
    return jnp.sum(value, axis=0, keepdims=True)


def first_kernel(count, slots, places, *refs):
    blocks, refs = refs[:count], refs[count:]
    attended, refs = refs[:slots], refs[slots:]
    tokens, table = refs[:2]
    unit, inverse, active, slope, sides = *refs[2:6], refs[6:-3]
    weights, turned, sems = refs[-3:]
    copies = block_copies(places, 1, blocks, weights, sems)
    width = D // slots

    def row(at):
        return table[at : at + 1]

    def put(target, s, value):
        target[s] = value

    core = places[0, 0] % 2 if slots > 1 else 0
    per = width // 2 if slots > 1 else width
    rows_of = [a[...] for a in attended]
    for s in range(slots):
        turned[0 : rows_of[s].shape[1]] = rows_of[s].astype(F32).T.astype(BF16)
        if slots > 1:
            sides[0][slots + s] = turned[pl.ds(pl.multiple_of(core * per, per), per)]
            sides[1][slots + s] = turned[pl.ds(pl.multiple_of((1 - core) * per, per), per)]
        else:
            sides[0][1] = turned[...]
    wait(copies)
    residual = tokens[...].astype(F32) + row(PROJ_B)
    for s in range(slots):
        first = pl.multiple_of((places[0, s] // 2) * width, width)
        residual = residual + dot(rows_of[s][:, :width], weights[0, pl.ds(first, width), :])
    first_unit, first_inverse = normalise(residual)
    unit[...] = first_unit
    inverse[...] = first_inverse
    normed = first_unit * row(NORM_G) + row(NORM_S)
    normed_low = normed.astype(BF16)
    turned[...] = normed.T.astype(BF16)
    for side, target in enumerate(sides[:2] if slots > 1 else sides[:1]):
        for s in range(slots):
            rows = target.shape[1]
            first = pl.multiple_of(places[0, side * slots + s] * rows, rows)
            target[s] = turned[pl.ds(first, rows)]
    step = 384
    for at in range(0, FF, step):
        line, col = at // D, at % D
        upward = (
            dot(normed_low, weights[1 + line, :, col : col + step])
            + table[UP_B + line : UP_B + line + 1, col : col + step]
        )
        share = 0.5 + 0.5 * erf(upward * 0.7071067811865476)
        bell = jnp.exp(upward * upward * -0.5) * 0.3989422804014327
        active[:, at : at + step] = (upward * share).astype(BF16)
        slope[:, at : at + step] = share + upward * bell
    for side, target in enumerate(sides[2:] if slots > 1 else sides[1:]):
        for s in range(slots):
            rows = target.shape[1]
            if slots > 1:
                first = pl.multiple_of(places[0, side * slots + s] * rows, rows)
                target[s] = active[:, pl.ds(first, rows)].astype(F32).T.astype(BF16)
            else:
                for at in range(0, FF, D):
                    target[s, at : at + D] = active[:, at : at + D].astype(F32).T.astype(BF16)


def first_part(places, blocks, attended, tokens, table):
    slots = len(attended)
    shape = jax.ShapeDtypeStruct
    sides = 2 if slots > 1 else 1
    outs = (
        shape((ROWS, D), F32), shape((ROWS, 1), F32), shape((ROWS, FF), BF16), shape((ROWS, FF), F32),
    )
    outs += (shape((2 * slots, D // sides // slots, ROWS), BF16),) * sides
    outs += (shape((slots, FF // sides // slots, ROWS), BF16),) * sides
    made = call(
        functools.partial(first_kernel, len(blocks), slots),
        "forward_up",
        11,
        out_shape=outs,
        in_specs=[SMEM] + [ANY] * len(blocks) + [VMEM] * (slots + 2),
        out_specs=(VMEM,) * len(outs),
        scratch_shapes=[
            pltpu.VMEM((5, D, D), BF16),
            pltpu.VMEM((D, ROWS), BF16),
            pltpu.SemaphoreType.DMA((len(blocks),)),
        ],
    )(places, *blocks, *attended, tokens, table)
    return made[:4], made[4 : 4 + sides], made[4 + sides :]


def head_kernel(count, docs, places, *refs):
    blocks, refs = refs[:count], refs[count:]
    unit, active, cotangent, table, place, labels, class_b = refs[:7]
    output, lines, docs_out, grad_second, grad_out = refs[7:12]
    pool, down, sems = refs[12:]
    down_copies = block_copies(places, 2, blocks, down, sems.at[1], slice(0, FF // count))
    pool_copies = block_copies(places, 2, blocks, pool, sems.at[0], slice(FF // count, (FF + D) // count))

    def row(at):
        return table[at : at + 1]

    normed = unit[...] * row(NORM_G) + row(NORM_S)
    wait(down_copies)
    residual = normed + dot(active[...], down[...]) + row(DOWN_B)
    last_unit, last_inverse = normalise(residual)
    outcome = last_unit * row(FINAL_G) + row(FINAL_S)
    out_low = outcome.astype(BF16)
    output[...] = out_low

    at_row = place[...]
    here = jnp.logical_and(at_row >= 0, at_row < ROWS)
    pick = jnp.where(lax.broadcasted_iota(jnp.int32, (docs, ROWS), 1) == at_row, 1.0, 0.0)
    first_low = dot(pick.astype(BF16), out_low).astype(BF16)
    wait(pool_copies)
    pooled = jnp.tanh(dot(first_low, pool[...]) + row(POOL_B))
    pooled_low = pooled.astype(BF16).astype(F32)
    logits = [
        jnp.sum(pooled_low * row(CLASS_W + c), axis=1, keepdims=True) + class_b[0, c]
        for c in range(CLASSES)
    ]
    top = functools.reduce(jnp.maximum, logits)
    powers = [jnp.exp(logit - top) for logit in logits]
    whole = functools.reduce(jnp.add, powers)
    label = labels[...]
    grads = [powers[c] / whole - jnp.where(label == c, 1.0, 0.0) for c in range(CLASSES)]
    grad_pre = functools.reduce(jnp.add, [grads[c] * row(CLASS_W + c) for c in range(CLASSES)])
    grad_pre = grad_pre * (1.0 - pooled * pooled)
    parts = jnp.concatenate(split3(grad_pre), axis=0).astype(BF16)
    made = dot(parts, pool[...], ((1,), (1,)))
    grad_first = made[:docs] + made[docs : 2 * docs] + made[2 * docs :]
    parts = jnp.concatenate(split3(grad_first), axis=0).astype(BF16)
    picks = jnp.concatenate([pick] * 3, axis=0).astype(BF16)
    grad_outcome = cotangent[...] + dot(picks, parts, ((0,), (0,)))
    lane = lax.broadcasted_iota(jnp.int32, (docs, 128), 1)
    small = jnp.zeros((docs, 128), F32)
    for c in range(CLASSES):
        small = jnp.where(lane == c, grads[c], jnp.where(lane == CLASSES + c, logits[c], small))
    docs_out[...] = jnp.where(
        here,
        jnp.concatenate([first_low.astype(F32), pooled_low, grad_pre, small], axis=1),
        0.0,
    )

    grad = norm_back(grad_outcome, row(FINAL_G), last_unit, last_inverse)
    grad_second[...] = grad
    grad_out[...] = grad.astype(BF16)
    lines[0:1] = column_sum(grad)
    lines[1:2] = column_sum(grad_outcome * last_unit)
    lines[2:3] = column_sum(grad_outcome)
    lines[3:8] = jnp.zeros((5, D), F32)


def head_part(places, blocks, unit, active, cotangent, table, place, labels, class_b):
    count, docs = len(blocks), place.shape[0]
    shape = jax.ShapeDtypeStruct
    outs = (
        shape((ROWS, D), BF16),
        shape((8, D), F32),
        shape((docs, 3 * D + 128), F32),
        shape((ROWS, D), F32),
        shape((ROWS, D), BF16),
    )
    return call(
        functools.partial(head_kernel, count, docs),
        "head",
        7,
        out_shape=outs,
        in_specs=[SMEM] + [ANY] * count + [VMEM] * 6 + [SMEM],
        out_specs=(VMEM,) * len(outs),
        scratch_shapes=[
            pltpu.VMEM((D, D), BF16),
            pltpu.VMEM((FF, D), BF16),
            pltpu.SemaphoreType.DMA((2, count)),
        ],
    )(places, *blocks, unit, active, cotangent, table, place, labels, class_b)


def second_kernel(count, places, *refs):
    downs, (grad_down, slope, lines, grad_up, down, sems) = refs[:count], refs[count:]
    wait(block_copies(places, 2, downs, down, sems, slice(0, FF // count)))
    grad_low = grad_down[...]
    step = 384
    for at in range(0, FF, step):
        grad = dot(grad_low, down[at : at + step], ((1,), (1,))).astype(BF16).astype(F32)
        grad = grad * slope[:, at : at + step]
        line, col = at // D, at % D
        lines[line : line + 1, col : col + step] = column_sum(grad)
        grad_up[line, :, col : col + step] = grad.astype(BF16)
    lines[4:8] = jnp.zeros((4, D), F32)


def second_part(places, down_blocks, grad_down, slope):
    count, shape = len(down_blocks), jax.ShapeDtypeStruct
    outs = (shape((8, D), F32), shape((4, ROWS, D), BF16))
    return call(
        functools.partial(second_kernel, count),
        "backward_down",
        5,
        out_shape=outs,
        in_specs=[SMEM] + [ANY] * count + [VMEM] * 2,
        out_specs=(VMEM,) * 2,
        scratch_shapes=[pltpu.VMEM((FF, D), BF16), pltpu.SemaphoreType.DMA((count,))],
    )(places, *down_blocks, grad_down, slope)


def third_kernel(count, slots, places, *refs):
    blocks, refs = refs[:count], refs[count:]
    table, grad_second, grad_up, unit, inverse = refs[:5]
    lines, grad_first, grad_out = refs[5:8]
    grad_attended = refs[8 : 8 + slots]
    weights, sems = refs[8 + slots :]
    wait(block_copies(places, 1, blocks, weights, sems))
    width = D // slots

    def row(at):
        return table[at : at + 1]

    back = dot(grad_up[0], weights[1], ((1,), (1,)))
    for line in range(1, 4):
        back = back + dot(grad_up[line], weights[1 + line], ((1,), (1,)))
    grad_normed = grad_second[...] + back.astype(BF16).astype(F32)
    lines[0:4] = jnp.zeros((4, D), F32)
    lines[4:5] = column_sum(grad_normed * unit[...])
    lines[5:6] = column_sum(grad_normed)
    grad = norm_back(grad_normed, row(NORM_G), unit[...], inverse[...])
    grad_first[...] = grad
    lines[6:7] = column_sum(grad)
    lines[7:8] = jnp.zeros((1, D), F32)
    grad_low = grad.astype(BF16)
    grad_out[...] = grad_low
    for s in range(slots):
        first = pl.multiple_of((places[0, s] // 2) * width, width)
        made = dot(grad_low, weights[0, pl.ds(first, width), :], ((1,), (1,))).astype(BF16)
        if width < grad_attended[s].shape[1]:
            grad_attended[s][:, PAIR:] = jnp.zeros((ROWS, PAIR), BF16)
        grad_attended[s][:, :width] = made


def third_part(places, blocks, table, grad_second, grad_up, unit, inverse, slots, lanes):
    count = len(blocks)
    shape = jax.ShapeDtypeStruct
    outs = (shape((8, D), F32), shape((ROWS, D), F32), shape((ROWS, D), BF16))
    outs += (shape((ROWS, lanes), BF16),) * slots
    made = call(
        functools.partial(third_kernel, count, slots),
        "backward_up",
        7,
        out_shape=outs,
        in_specs=[SMEM] + [ANY] * count + [VMEM] * 5,
        out_specs=(VMEM,) * len(outs),
        scratch_shapes=[pltpu.VMEM((5, D, D), BF16), pltpu.SemaphoreType.DMA((count,))],
    )(places, *blocks, table, grad_second, grad_up, unit, inverse)
    return made[:3], list(made[3:])


def wgrad_outs(slots, rows):
    shape = jax.ShapeDtypeStruct
    if slots == 1:
        return (shape((1, rows, D), BF16),)
    half = rows // 2
    return (shape((2, half, D), BF16),) * 2 + (shape((half, D), BF16),) * 2 + (shape((rows, D), F32),)


def put_slot(outs, s, first, value):
    if len(outs) == 1:
        outs[0][0, first : first + value.shape[0]] = value.astype(BF16)
        return
    if s == 0:
        outs[4][first : first + value.shape[0]] = value
        return
    half = outs[2].shape[0]
    for k, order in enumerate(((1, 3, 2), (2, 3, 1))):
        low, high = max(first, k * half), min(first + value.shape[0], (k + 1) * half)
        if low >= high:
            continue
        rows, part = slice(low - k * half, high - k * half), value[low - first : high - first]
        if s == order[2]:
            outs[2 + k][rows] = part.astype(BF16)
        else:
            outs[k][order.index(s), rows] = part.astype(BF16)


def down_kernel(sides, *refs):
    lefts, rights, outs = refs[:sides], refs[sides : 2 * sides], refs[2 * sides :]
    step = min(lefts[0].shape[1], 384)
    for s in range(lefts[0].shape[0]):
        for at in range(0, lefts[0].shape[1], step):
            made = dot(lefts[0][s, at : at + step], rights[0][...])
            for side in range(1, sides):
                made = made + dot(lefts[side][s, at : at + step], rights[side][...])
            put_slot(outs, s, at, made)


def down_gradient(lefts, rights):
    sides, (slots, rows, _) = len(lefts), lefts[0].shape
    outs = wgrad_outs(slots, rows)
    return call(
        functools.partial(down_kernel, sides),
        "down_gradient",
        3,
        out_shape=outs,
        in_specs=[VMEM] * (2 * sides),
        out_specs=(VMEM,) * len(outs),
    )(*lefts, *rights)


def up_kernel(sides, *refs):
    lefts, ups, projs = (refs[k * sides : (k + 1) * sides] for k in range(3))
    outs = refs[3 * sides :]
    slots, rows = lefts[0].shape[0] // 2, lefts[0].shape[1]
    for line in range(5):
        at = 0 if line < 4 else slots
        made = 0.0
        for left, up, proj in zip(lefts, ups, projs):
            left = left[at : at + slots].reshape(slots * rows, ROWS)
            made = made + dot(left, up[line] if line < 4 else proj[...])
        for s in range(slots):
            put_slot(outs, s, line * rows, made[s * rows : (s + 1) * rows])


def up_gradient(lefts, ups, projs):
    sides, (slots, rows, _) = len(lefts), lefts[0].shape
    outs = wgrad_outs(slots // 2, 5 * rows)
    return call(
        functools.partial(up_kernel, sides),
        "up_gradient",
        4,
        out_shape=outs,
        in_specs=[VMEM] * (3 * sides),
        out_specs=(VMEM,) * len(outs),
    )(*lefts, *ups, *projs)


def last_kernel(blocks, sides, groups, parts, places, *refs):
    tokens, refs = refs[:blocks], refs[blocks:]
    weights, refs = refs[:sides], refs[sides:]
    grad_qs, refs = refs[:groups], refs[groups:]
    changes, refs = refs[: groups * parts], refs[groups * parts :]
    grad_first, lines, own, outs = *refs[:3], refs[3:-6]
    held, turned, grads, made, sems, out_sems = refs[-6:]
    slots = grad_qs[0].shape[0]
    copies = block_copies(places, 0, weight_refs(weights), held, sems)
    sums = [0.0, 0.0]
    for s in range(slots):
        rows = slice(s * ROWS, (s + 1) * ROWS)
        turned[:, rows] = tokens[s][...].astype(F32).T.astype(BF16)
        lane = 0
        for group in range(groups):
            lanes = slice(lane, lane + grad_qs[group].shape[2])
            lane = lanes.stop
            grads[0, rows, lanes] = grad_qs[group][s]
            for k in range(2):
                total = changes[group * parts][k, s].astype(F32)
                for change in changes[group * parts + 1 : (group + 1) * parts]:
                    total = total + change[k, s].astype(F32)
                grads[1 + k, rows, lanes] = total.astype(BF16)
        sums[0] = sums[0] + column_sum(grads[0, rows].astype(F32))
        sums[1] = sums[1] + column_sum(grads[2, rows].astype(F32))
    lines[0:1], lines[1:2] = sums
    lines[2:8] = jnp.zeros((6, lines.shape[1]), F32)
    for k in range(3):
        made[k] = dot(turned[...], grads[k]).astype(BF16)
    sends = []
    for side, out in enumerate(outs[:sides]):
        for s in range(out.shape[0]):
            rows = out.shape[2]
            first = pl.multiple_of(places[0, side * out.shape[0] + s] * rows, rows)
            sends.append((made.at[:, pl.ds(first, rows), :], out.at[s]))
    sends = start(
        [pltpu.make_async_copy(a, b, out_sems.at[k]) for k, (a, b) in enumerate(sends)]
    )
    wait(copies)

    def partial(s):
        rows = slice(s * ROWS, (s + 1) * ROWS)
        total = dot(grads[0, rows], held[0], ((1,), (1,)))
        for k in range(1, 3):
            total = total + dot(grads[k, rows], held[k], ((1,), (1,)))
        return total

    if slots > 1:
        a_first, b_first, a_last, b_last = outs[sides:]
        half = ROWS // 2
        for s in (3, 1, 2):
            total = partial(s).astype(BF16)
            if s in (1, 3):
                a_first[s // 2] = total[:half]
            else:
                a_last[...] = total[:half]
            if s in (2, 3):
                b_first[s - 2] = total[half:]
            else:
                b_last[...] = total[half:]
    own[...] = grad_first[...] + partial(0)
    wait(sends)


def last_part(places, tokens, weights, grad_qs, changes, grad_first):
    slots, lanes = grad_qs[0].shape[0], sum(grad.shape[2] for grad in grad_qs)
    groups, parts = len(grad_qs), len(changes) // len(grad_qs)
    sides, shape = len(weights), jax.ShapeDtypeStruct
    outs = (shape((8, lanes), F32), shape((ROWS, D), F32))
    outs += tuple(shape(a.shape, BF16) for a in weights)
    if slots > 1:
        half = ROWS // 2
        outs += (shape((2, half, D), BF16),) * 2 + (shape((half, D), BF16),) * 2
    blocks = sides * weights[0].shape[0]
    made = call(
        functools.partial(last_kernel, len(tokens), sides, groups, parts),
        "input_gradients",
        8,
        out_shape=outs,
        in_specs=[SMEM] + [VMEM] * len(tokens) + [ANY] * sides
        + [VMEM] * (1 + groups + len(changes)),
        out_specs=(VMEM,) * 2 + (ANY,) * sides + (VMEM,) * (len(outs) - 2 - sides),
        scratch_shapes=[
            pltpu.VMEM((3, D, lanes), BF16),
            pltpu.VMEM((D, slots * ROWS), BF16),
            pltpu.VMEM((3, slots * ROWS, lanes), BF16),
            pltpu.VMEM((3, D, lanes), BF16),
            pltpu.SemaphoreType.DMA((blocks,)),
            pltpu.SemaphoreType.DMA((blocks,)),
        ],
    )(places, *tokens, *weights, *grad_qs, *changes, grad_first)
    return made[0], made[1], list(made[2 : 2 + sides]), made[2 + sides :]


def whole_scatter(part, pieces):
    seq = lax.axis_size("seq")
    rows = part.shape[1] // pieces // seq
    part = part.reshape(pieces, seq, rows, D).transpose(1, 0, 2, 3)
    part = part.reshape(seq, pieces * rows, D)
    return lax.psum_scatter(part, "seq", scatter_dimension=0, tiled=True)[0].astype(F32)


def by_chip(pieces):
    me = lax.axis_index("seq")
    for bit in (1, 2):
        odd = (me & (2 * bit)) != 0
        pieces = [jnp.where(odd, pieces[s ^ bit], pieces[s]) for s in range(len(pieces))]
    return pieces


def features(positions, starts):
    docs = starts.shape[0]
    segment = jnp.sum((positions[..., None] >= starts).astype(jnp.int32), axis=-1) - 1
    lane = jnp.arange(PAIR, dtype=jnp.int32) % HEAD_DIM
    own = segment[..., None] == lane
    return own, lane, docs


def on_device(
    inputs,
    cotangent,
    doc_lengths,
    doc_labels,
    query_weight,
    query_bias,
    key_weight,
    value_weight,
    value_bias,
    proj_weight,
    proj_bias,
    norm_gain,
    norm_shift,
    up_weight,
    up_bias,
    down_weight,
    down_bias,
    final_gain,
    final_shift,
    pool_weight,
    pool_bias,
    class_weight,
    class_bias,
):
    me = lax.axis_index("seq")
    tokens = inputs[0]
    share = query_bias.shape[0]
    lengths = doc_lengths[0]
    docs = lengths.shape[0]
    order = jnp.arange(docs, dtype=jnp.int32)
    starts = jnp.sum(jnp.where(order[None, :] < order[:, None], lengths[None, :], 0), axis=1)

    small_mesh = is_small()
    slot_list = slot_owners()
    chip, core = me // 2, me % 2
    width = D // 4
    slots = 4 if small_mesh else 1
    line = jnp.arange(ROWS, dtype=jnp.int32)
    mine = slot_list[:slots] if small_mesh else me[None]
    own, lane, _ = features(mine[:, None] * ROWS + line, starts)
    feature_q = jnp.where(own, FAR, 0.0).astype(BF16)
    own, lane, _ = features(slot_list[:, None] * ROWS + line, starts)
    feature_k = jnp.where(
        lane < docs, jnp.where(own, 0.0, 1.0), jnp.where(lane < docs + 3, 1.0, 0.0)
    ).astype(BF16)

    matrices = jnp.stack([query_weight, key_weight, value_weight])
    bias = jnp.stack([query_bias, value_bias])
    small = jnp.stack(
        [
            query_bias, value_bias, proj_bias, norm_gain, norm_shift, down_bias,
            final_gain, final_shift, pool_bias, *class_weight.T,
        ]
    )
    table = jnp.zeros((TABLE, D), BF16)
    table = lax.dynamic_update_slice(table, small, (0, me * share))
    wide = me * up_bias.shape[0]
    table = lax.dynamic_update_slice(table, up_bias[None], (UP_B + wide // D, wide % D))
    proj_up = jnp.concatenate([proj_weight[None], up_weight.reshape(share, 4, D).transpose(1, 0, 2)])
    down_pool = jnp.concatenate([down_weight, pool_weight])
    token_blocks = gather_tokens(tokens)
    if small_mesh:
        pieces = [
            lax.dynamic_slice_in_dim(matrices, (chip ^ s) * width, width, 2) for s in range(4)
        ]
        own = jnp.pad(jnp.stack(exchange(pieces)), ((0, 0), (0, 0), (0, 0), (0, PAIR * 2 - width)))
        weights = [own, swap(own, along(1))]
        come = swap(bias, along(1))
        bias = jnp.where(
            core == 0, jnp.concatenate([bias, come], axis=1), jnp.concatenate([come, bias], axis=1)
        )
        bias = jnp.pad(bias, ((0, 0), (0, PAIR * 2 - width))).astype(F32)
        early, late = Shared(proj_up, 0), Shared(down_pool, 1)
        places = jnp.stack([slot_list, early.owners(), late.owners()])
        early.near()
        late.near()
    else:
        weights = [lax.all_gather(matrices, "seq", axis=1, tiled=True)[None]]
        table = sum_seq(table).astype(F32)
        bias = table[:2]
        blocks = [lax.all_gather(proj_up, "seq", axis=1, tiled=True)]
        whole = lax.all_gather(down_pool, "seq", axis=0)
        down_blocks = [
            jnp.concatenate([whole[:, : 4 * share].reshape(FF, D), whole[:, 4 * share :].reshape(D, D)])
        ]
        places = jnp.zeros((3, 1), jnp.int32)

    query, keyval = qkv_project(places, token_blocks, weights, bias)
    if small_mesh:
        keyval = after(keyval, early.one, late.one)
        keyvals = [keyval, swap(keyval, along(1))]
        early.far()
        early.rest()
        late.far()
        table = after(table, keyval)
        come = swap(table, along(1))
    else:
        keyvals = [lax.all_gather(keyval, "seq", axis=1, tiled=True)]
    attended, total, lows = attend(query, keyvals, feature_q, feature_k, docs)
    if small_mesh:
        late.rest(lows)
        lows, table = after((lows, table), come, early.both, late.both)
        table = table + come
        lows = exchange(lows)
        table = table + swap(table, along(2))
        table = (table + swap(table, along(4))).astype(F32)
        blocks, down_blocks = early.finish(), late.finish()
    else:
        lows = exchange(lows)

    place = (starts - me * ROWS)[:, None]
    made, turned, active_t = first_part(places, blocks, lows, tokens, table)
    unit, inverse, active, slope = made
    output, lines_one, docs_out, grad_second, grad_down = head_part(
        places, down_blocks, unit, active, cotangent[0], table,
        place, doc_labels[0][:, None], class_bias.astype(F32)[None],
    )

    def both(keep, *away):
        return [keep] + [swap(a, along(1)) for a in away]

    def own_and_other(value):
        return both(value, *([value] if small_mesh else []))

    down_parts = down_gradient(both(*active_t), own_and_other(grad_down))
    if small_mesh:
        down_sum = Scatter(down_parts)
    grad_down = after(grad_down, down_parts)
    lines_two, grad_up = second_part(places, down_blocks, grad_down, slope)
    grad_second = after(grad_second, grad_up)
    made, grads = third_part(
        places, blocks, table, grad_second, grad_up, unit, inverse, slots, query.shape[-1]
    )
    lines_three, grad_first, grad_proj = made
    lines_two = lines_two + lines_three
    pack = jnp.concatenate([docs_out, lines_one, lines_two], axis=1)
    ups = own_and_other(grad_up)
    if small_mesh:
        grad_proj, grads, turned = after((grad_proj, grads, turned), down_sum.comes)
        down_sum.combine()
        down_sum.turn()
        grads = exchange(grads)
    up_parts = up_gradient(both(*turned), ups, own_and_other(grad_proj))

    back = functools.partial(
        attend_back, keyvals=keyvals, wide=attended, total=total,
        feature_q=feature_q, feature_k=feature_k, docs=docs,
    )
    if small_mesh:
        up_parts, pack, grads, down_sum.lasts = after(
            (up_parts, pack, grads, down_sum.lasts), up_parts
        )
        down_dp = SumDp(down_sum.total())
        up_sum = Scatter(up_parts)
        come = swap(pack, along(1))
        grad_q, changes = back(query, grads=grads, base=0, tiles=1, single=False)
        changes, pack, come, up_sum.seconds, down_dp.come = after(
            (changes, pack, come, up_sum.seconds, down_dp.come), grad_q, up_sum.comes
        )
        grad_qs, changes = [grad_q], both(*changes)
        up_sum.combine()
        up_sum.turn()
        down_dp.across()
        pack = pack + come
        come = swap(pack, along(2))
        rows = after(query, grad_q, up_sum.sends, down_dp.pair, pack)
        grad_q, more = back(rows, grads=grads, base=1, tiles=1, single=True)
        more, pack, come, up_sum.lasts, down_dp.cross = after(
            (more, pack, come, up_sum.lasts, down_dp.cross), grad_q
        )
        grad_qs, changes = grad_qs + [grad_q], changes + both(*more)
        up_dp = SumDp(up_sum.total())
        pack = pack + come
        come = swap(pack, along(4))
        changes = after(changes, up_dp.keep, pack)
    else:
        grad_q, changes = back(
            query, grads=grads, base=0, tiles=HEADS // 2, single=False
        )
        grad_qs = [grad_q]
        change = changes[0].transpose(1, 0, 2, 3)
        change = lax.psum_scatter(change, "seq", scatter_dimension=0, tiled=True)
        changes = [change.transpose(1, 0, 2, 3)]
        pack = sum_seq(pack)
    ends, input_grad, qkv_parts, sums = last_part(
        places, token_blocks, weights, grad_qs, changes, grad_first
    )

    if small_mesh:
        qkv_parts, ends, pack, come, up_dp.come, down_dp.cross = after(
            (qkv_parts, ends, pack, come, up_dp.come, down_dp.cross), input_grad
        )
        keep, away = both(*qkv_parts)
        ends = ends + swap(ends, along(1))
        rows_sum = Scatter((*sums, input_grad))
        up_dp.across()
        away, pack, come, down_dp.cross = after((away, pack, come, down_dp.cross), away)
        pieces = [add(keep[s], away[s])[..., :width].astype(BF16) for s in range(4)]
        pieces = exchange(pieces)
        down_wgrad = down_dp.back()
        pieces, pack, come, rows_sum.comes, up_dp.cross = after(
            (pieces, pack, come, rows_sum.comes, up_dp.cross), pieces
        )
        qkv_wgrad = jnp.concatenate(by_chip(pieces), axis=2).reshape(3 * share, D)
        ends = jnp.pad(
            lax.dynamic_slice_in_dim(ends[:2], core * share, share, 1),
            ((0, 30), (0, D - share)),
        )
        qkv_dp = SumDp(jnp.concatenate([qkv_wgrad.astype(F32), ends]))
        rows_sum.combine()
        rows_sum.turn()
        pack = pack + come
        qkv_dp.come, up_dp.cross, pack = after((qkv_dp.come, up_dp.cross, pack), qkv_dp.come)
        qkv_dp.across()
        up_wgrad = up_dp.back()
        input_grad = rows_sum.total()
        qkv_wgrad = qkv_dp.back()
    else:
        qkv_wgrad = whole_scatter(qkv_parts[0].reshape(1, 3 * D, D), 3)
        ends = lax.dynamic_slice_in_dim(sum_seq(ends)[:2], me * share, share, 1)
        qkv_wgrad = sum_dp(jnp.concatenate([qkv_wgrad, jnp.pad(ends, ((0, 30), (0, D - share)))]))
        down_wgrad = sum_dp(whole_scatter(down_parts[0], 1))
        up_wgrad = sum_dp(whole_scatter(up_parts[0], 5))
    proj_wgrad = up_wgrad[4 * share :]
    up_wgrad = up_wgrad[: 4 * share].reshape(4, share, D).transpose(1, 0, 2).reshape(share, FF)
    ends = qkv_wgrad[3 * share : 3 * share + 2, :share]
    qkv_wgrad = qkv_wgrad[: 3 * share].reshape(3, share, D)
    logits = pack[:, 3 * D + CLASSES : 3 * D + 2 * CLASSES]
    every_doc = stack_dp(pack)
    lines = jnp.sum(every_doc[:, 3 * D + 128 :].reshape(-1, docs, 2, D), axis=0)
    lines = jnp.concatenate([lines[:, 0], lines[:, 1]])
    at = me * share

    def my_share(vector):
        return lax.dynamic_slice_in_dim(vector, at, share, 0)

    first_all, pooled_all = (
        lax.dynamic_slice_in_dim(every_doc, k * D + at, share, 1) for k in range(2)
    )
    pre_all = every_doc[:, 2 * D : 3 * D]
    logit_all = every_doc[:, 3 * D : 3 * D + CLASSES]
    exact = functools.partial(jnp.dot, precision=lax.Precision.HIGHEST)
    return (
        output[None],
        logits[None],
        input_grad[None],
        qkv_wgrad[0],
        ends[0],
        qkv_wgrad[1],
        qkv_wgrad[2],
        ends[1],
        proj_wgrad,
        my_share(lines[14]),
        my_share(lines[12]),
        my_share(lines[13]),
        up_wgrad,
        lax.dynamic_slice_in_dim(lines[8:12].reshape(-1), wide, up_bias.shape[0], 0),
        down_wgrad,
        my_share(lines[0]),
        my_share(lines[1]),
        my_share(lines[2]),
        exact(first_all.T, pre_all),
        my_share(jnp.sum(pre_all, axis=0)),
        exact(pooled_all.T, logit_all),
        jnp.sum(logit_all, axis=0),
    )


def solution(mesh):
    rows, row, part = P("dp", "seq", None), P("seq", None), P("seq")
    per_sequence = P("dp", None)
    in_specs = (
        rows, rows, per_sequence, per_sequence, row, part, row, row, part, row, part, part,
        part, row, part, row, part, part, part, row, part, row, P(),
    )
    out_specs = (
        rows, P("dp", None, None), rows, row, part, row, row, part, row, part, part, part,
        row, part, row, part, part, part, row, part, row, P(),
    )
    return jax.shard_map(
        on_device, mesh=mesh, in_specs=in_specs, out_specs=out_specs, check_vma=False
    )
```

time: 408 us -> 291 us (0.71)
  waiting for transfers between devices: 189 us -> 73.9 us
  other arithmetic: 37.3 us -> 13.6 us
  Pallas kernels: 87.1 us -> 109 us
  starting transfers between devices: 66.3 us -> 72.7 us
  local copies, waits for them, and re-layouts: 16.9 us -> 12 us
    ppermute x79 -> x70, waiting for transfers between devices: 189 us -> 73.9 us  [swap(): return lax.ppermute(value, ('dp', 'seq'), pairs)]
    pallas_call x6 -> x11, Pallas kernels: 87.1 us -> 109 us  [the longest x2 32.7 us: attend_back(): call(functools.partial(attend_back_kernel, len(keyvals), docs, single), '...]
    convert_element_type x23 -> x21, other arithmetic: 20 us -> 4.11 us  [the longest x3 1.24 us: back(): return jnp.concatenate([jnp.where(low, total, come), jnp.where(low, come,...]
    add x17 -> x11, other arithmetic: 9.13 us -> 1.4 us  [the longest x1 0.81 us: on_device(): lines_two = lines_two + lines_three]
    ppermute x79 -> x70, starting transfers between devices: 66.3 us -> 72.7 us  [swap(): return lax.ppermute(value, ('dp', 'seq'), pairs)]
  transfers between devices with their start and end apart: 79 -> 70, of which waited for: 37 -> 21; matrix products, arithmetic and copies ran while one was open for 12% -> 8% of each run, Pallas kernels for 6% -> 37%
where the time goes in v2:
time: 291 us; the launch traced here: 286 us
  Pallas kernels  109 us (37%)
  waiting for transfers between devices  73.9 us (25%)
  starting transfers between devices  72.7 us (25%)
  other arithmetic  13.6 us (5%)
  local copies, waits for them, and re-layouts  12 us (4%)
    ppermute x70, waiting for transfers between devices, swap(): return lax.ppermute(value, ('dp', 'seq'), pairs)  73.9 us
    ppermute x70, starting transfers between devices, swap(): return lax.ppermute(value, ('dp', 'seq'), pairs)  72.7 us
    pallas_call x2, Pallas kernels, attend_back(): call(functools.partial(attend_back_kernel, len(keyvals), docs, single), '...  32.7 us
    pallas_call x1, Pallas kernels, attend(): call(functools.partial(attend_kernel, len(keyvals), docs, slots > 1), 'at...  15.2 us
    pallas_call x1, Pallas kernels, first_part(): call(functools.partial(first_kernel, len(blocks), slots), 'forward_up', 1...  13.1 us
    pallas_call x1, Pallas kernels, head_part(): call(functools.partial(head_kernel, count, docs), 'head', 7, out_shape=ou...  9.12 us
    pallas_call x1, Pallas kernels, third_part(): call(functools.partial(third_kernel, count, slots), 'backward_up', 7, out...  8.27 us
    pallas_call x1, Pallas kernels, last_part(): call(functools.partial(last_kernel, len(tokens), sides, groups, parts), '...  8.11 us
  transfers between devices with their start and end apart: 70, of which 21 were waited for; matrix products, arithmetic and copies ran while one was open for 8% of the time, Pallas kernels for 37%

profile of v2, /device:TPU:0, one launch (start us, length us, event | category | flops | bytes accessed | tf_op | source)
XLA Modules:
  0.0 285.6 jit_solution(222383521201481096)
XLA Ops:
  0.7 4.0 %collective-permute-start.4 = (bf16[256,768]{1,0:T(8,128)(2,1)}, bf16[256,768]{1,0:T(8,128)(2,1)}, u32[]{:S(2)}, u32[]{:S(2)}) collective-permute-start(bf16[256,768]{1,0:T(8,128)(2,1)} %bitcast.197), channel_id=1, source_target_pairs={{0,6},{1,7},{2,4},{3,5},{4,2},{5,3},{6,0},{7,1},{8,14},{9,15},{10,... | collective-permute-start | bytes 1179656 | tf_op jit(solution)/shard_map/ppermute | solution.py:35
  8.3 1.9 collective-permute-start.5
  10.8 7.2 %collective-permute-done.7 = bf16[3,96,192]{2,1,0:T(8,128)(2,1)S(1)} collective-permute-done((bf16[3,96,192]{2,1,0:T(8,128)(2,1)S(1)}, bf16[3,96,192]{2,1,0:T(8,128)(2,1)S(1)}, u32[]{:S(2)}, u32[]{:S(2)}) %collective-permute-start.7) | collective-permute-done | bytes 110624 | tf_op jit(solution)/shard_map/ppermute | solution.py:35
  18.0 2.0 collective-permute-start.2
  20.0 8.7 %collective-permute-done.6 = bf16[3,96,192]{2,1,0:T(8,128)(2,1)S(1)} collective-permute-done((bf16[3,96,192]{2,1,0:T(8,128)(2,1)S(1)}, bf16[3,96,192]{2,1,0:T(8,128)(2,1)S(1)}, u32[]{:S(2)}, u32[]{:S(2)}) %collective-permute-start.6) | collective-permute-done | bytes 110624 | tf_op jit(solution)/shard_map/ppermute | solution.py:35
  30.3 1.8 collective-permute-start
  33.6 5.3 %qkv.1 = (bf16[4,256,256]{2,1,0:T(8,128)(2,1)}, bf16[2,4,256,256]{3,2,1,0:T(8,128)(2,1)}) custom-call(s32[3,8]{1,0:T(4,128)} %pad_add_fusion.places, bf16[256,768]{1,0:T(8,128)(2,1)} %bitcast.199, bf16[256,768]{1,0:T(8,128)(2,1)} %collective-permute-done.2.refs_1_, bf16[256,768]{1,0:T(8,128)(2,1)} %collective-permute-done.3.refs_2_, ...), custom_call_target="tpu_custom_call" | custom-call | flops 5500000256 | bytes 5000000 | tf_op jit(solution)/shard_map/qkv/pallas_call | solution.py:243
  38.9 10.0 %collective-permute-done.refs_1_ = bf16[480,768]{1,0:T(8,128)(2,1)} collective-permute-done((bf16[480,768]{1,0:T(8,128)(2,1)S(1)}, bf16[480,768]{1,0:T(8,128)(2,1)}, u32[]{:S(2)}, u32[]{:S(2)}) %collective-permute-start) | collective-permute-done | bytes 737312 | tf_op jit(solution)/shard_map/ppermute | solution.py:35
  57.8 15.2 %attend.1 = (f32[4,256,256]{2,1,0:T(8,128)}, f32[4,256,256]{2,1,0:T(8,128)}, bf16[256,256]{1,0:T(8,128)(2,1)}, bf16[256,256]{1,0:T(8,128)(2,1)}, bf16[256,256]{1,0:T(8,128)(2,1)}, /*index=5*/bf16[256,256]{1,0:T(8,128)(2,1)}) custom-call(bf16[4,256,256]{2,1,0:T(8,128)(2,1)} %get-tuple-element.232.refs_0_, ...), custom_call_target="tpu_custom_call" | custom-call | flops 16499999744 | bytes 15000000 | tf_op jit(solution)/shard_map/attend/pallas_call | solution.py:366
  77.5 1.9 collective-permute-done.27
  87.9 4.8 %collective-permute-done.25.refs_10_ = bf16[256,256]{1,0:T(8,128)(2,1)S(1)} collective-permute-done((bf16[256,256]{1,0:T(8,128)(2,1)}, bf16[256,256]{1,0:T(8,128)(2,1)S(1)}, u32[]{:S(2)}, u32[]{:S(2)}) %collective-permute-start.25) | collective-permute-done | bytes 131104 | tf_op jit(solution)/shard_map/ppermute | solution.py:35
  93.4 2.9 %collective-permute-done.12.refs_3_ = bf16[480,768]{1,0:T(8,128)(2,1)} collective-permute-done((bf16[480,768]{1,0:T(8,128)(2,1)}, bf16[480,768]{1,0:T(8,128)(2,1)}, u32[]{:S(2)}, u32[]{:S(2)}) %collective-permute-start.12) | collective-permute-done | bytes 737312 | tf_op jit(solution)/shard_map/ppermute | solution.py:35
  96.3 13.1 %forward_up.1 = (f32[256,768]{1,0:T(8,128)}, f32[256,1]{1,0:T(8,128)}, bf16[256,3072]{1,0:T(8,128)(2,1)}, f32[256,3072]{1,0:T(8,128)}, bf16[8,96,256]{2,1,0:T(8,...) custom-call(s32[3,8]{1,0:T(4,128)} %pad_add_fusion.places, ...), custom_call_target="tpu_custom_call" | custom-call | flops 12099999744 | bytes 11000000 | tf_op jit(solution)/shard_map/forward_up/pallas_call | solution.py:582
  111.6 9.1 %head.1 = (bf16[256,768]{1,0:T(8,128)(2,1)}, f32[8,768]{1,0:T(8,128)}, f32[8,2432]{1,0:T(8,128)}, f32[256,768]{1,0:T(8,128)}, bf16[256,768]{1,0:T(8,128)(2,1)}) custom-call(s32[3,8]{1,0:T(4,128)} %pad_add_fusion.places, bf16[480,768]{1,0:T(8,128)(2,1)} %copy-done.8, bf16[480,768]{1,0:T(8,128)(2,1)} %collective-permute-done.refs_1_, ...), custom_call_target="tpu_custom_call" | custom-call | flops 7699999744 | bytes 7000000 | tf_op jit(solution)/shard_map/head/pallas_call | solution.py:670
  120.8 1.9 collective-permute-done.30.refs_3_
  123.4 4.0 %down_gradient.1 = (bf16[2,192,768]{2,1,0:T(8,128)(2,1)}, bf16[2,192,768]{2,1,0:T(8,128)(2,1)}, bf16[192,768]{1,0:T(8,128)(2,1)}, bf16[192,768]{1,0:T(8,128)(2,1)}, f32[384,768]{1,0:T(8,128)}) custom-call(bf16[4,384,256]{2,1,0:T(8,128)(2,1)} %get-tuple-element.174.refs_0_, bf16[4,384,256]{2,1,0:T(8,128)(2,1)} %copy-done.36, ...), custom_call_target="tpu_custom_call" | custom-call | flops 3300000000 | bytes 3000000 | tf_op jit(solution)/shard_map/down_gradient/pallas_call | solution.py:804
  129.5 7.7 %backward_down.1 = (f32[8,768]{1,0:T(8,128)}, bf16[4,256,768]{2,1,0:T(8,128)(2,1)}) custom-call(s32[3,8]{1,0:T(4,128)} %pad_add_fusion.places, bf16[480,768]{1,0:T(8,128)(2,1)} %copy-done.8, bf16[480,768]{1,0:T(8,128)(2,1)} %collective-permute-done.refs_1_, bf16[480,768]{1,0:T(8,128)(2,1)} %collective-permute-done.1.refs_2_, ...), custom_call_target="tpu_custom_call" | custom-call | flops 5500000256 | bytes 5000000 | tf_op jit(solution)/shard_map/backward_down/pallas_call | solution.py:702
  137.3 8.3 %backward_up.1 = (f32[8,768]{1,0:T(8,128)}, f32[256,768]{1,0:T(8,128)}, bf16[256,768]{1,0:T(8,128)(2,1)}, bf16[256,256]{1,0:T(8,128)(2,1)}, bf16[256,256]{1,0:T(...) custom-call(s32[3,8]{1,0:T(4,128)} %pad_add_fusion.places, bf16[5,96,768]{2,1,0:T(8,128)(2,1)} %copy-done.3, ...), custom_call_target="tpu_custom_call" | custom-call | flops 7699999744 | bytes 7000000 | tf_op jit(solution)/shard_map/backward_up/pallas_call | solution.py:751
  153.0 5.6 %up_gradient.1 = (bf16[2,240,768]{2,1,0:T(8,128)(2,1)}, bf16[2,240,768]{2,1,0:T(8,128)(2,1)}, bf16[240,768]{1,0:T(8,128)(2,1)}, bf16[240,768]{1,0:T(8,128)(2,1)}, f32[480,768]{1,0:T(8,128)}) custom-call(bf16[8,96,256]{2,1,0:T(8,128)(2,1)} %get-tuple-element.193.refs_0_, bf16[8,96,256]{2,1,0:T(8,128)(2,1)} %copy-done.49, ...), custom_call_target="tpu_custom_call" | custom-call | flops 4400000000 | bytes 4000000 | tf_op jit(solution)/shard_map/up_gradient/pallas_call | solution.py:831
  158.6 3.6 %collective-permute-done.37.refs_7_ = bf16[256,256]{1,0:T(8,128)(2,1)S(1)} collective-permute-done((bf16[256,256]{1,0:T(8,128)(2,1)S(1)}, bf16[256,256]{1,0:T(8,128)(2,1)S(1)}, u32[]{:S(2)}, u32[]{:S(2)}) %collective-permute-start.37) | collective-permute-done | bytes 131104 | tf_op jit(solution)/shard_map/ppermute | solution.py:35
  166.0 19.9 %attend_back.2 = (bf16[4,256,128]{2,1,0:T(8,128)(2,1)}, bf16[2,4,256,128]{3,2,1,0:T(8,128)(2,1)}, bf16[2,4,256,128]{3,2,1,0:T(8,128)(2,1)}) custom-call(bf16[4,256,256]{2,1,0:T(8,128)(2,1)} %get-tuple-element.232.refs_0_, f32[4,256,256]{2,1,0:T(8,128)} %get-tuple-element.170.refs_1_, f32[4,256,256]{2,1,0:T(8,128)} %get-tuple-element.171.refs_2_, ...), custom_call_target="tpu_custom_call" | custom-call | flops 23100000256 | bytes 21000000 | tf_op jit(solution)/shard_map/attend_back/pallas_call | solution.py:456
  187.5 3.3 %collective-permute-start.49 = (bf16[192,768]{1,0:T(8,128)(2,1)S(1)}, bf16[192,768]{1,0:T(8,128)(2,1)S(1)}, u32[]{:S(2)}, u32[]{:S(2)}) collective-permute-start(bf16[192,768]{1,0:T(8,128)(2,1)S(1)} %add_convert_fusion.3), channel_id=1, source_target_pairs={{0,24},{1,25},{2,26},{3,27},{4,28},{5,29},{6,30},{7,31},{8,16},{9,... | collective-permute-start | bytes 884744 | tf_op jit(solution)/shard_map/ppermute | solution.py:35
  193.2 12.8 %attend_back.3 = (bf16[4,256,128]{2,1,0:T(8,128)(2,1)}, bf16[2,4,256,128]{3,2,1,0:T(8,128)(2,1)}, bf16[2,4,256,128]{3,2,1,0:T(8,128)(2,1)}) custom-call(bf16[4,256,256]{2,1,0:T(8,128)(2,1)} %get-tuple-element.232.refs_0_, f32[4,256,256]{2,1,0:T(8,128)} %get-tuple-element.170.refs_1_, f32[4,256,256]{2,1,0:T(8,128)} %get-tuple-element.171.refs_2_, ...), custom_call_target="tpu_custom_call" | custom-call | flops 11000000512 | bytes 10000000 | tf_op jit(solution)/shard_map/attend_back/pallas_call | solution.py:456
  208.7 8.1 %input_gradients.1 = (f32[8,256]{1,0:T(8,128)}, f32[256,768]{1,0:T(8,128)}, bf16[4,3,96,256]{3,2,1,0:T(8,128)(2,1)}, bf16[4,3,96,256]{3,2,1,0:T(8,128)(2,1)}, bf...) custom-call(s32[3,8]{1,0:T(4,128)} %pad_add_fusion.places, ...), custom_call_target="tpu_custom_call" | custom-call | flops 8800000000 | bytes 8000000 | tf_op jit(solution)/shard_map/input_gradients/pallas_call | solution.py:915
  224.1 7.0 %collective-permute-done.59 = bf16[240,768]{1,0:T(8,128)(2,1)S(1)} collective-permute-done((bf16[240,768]{1,0:T(8,128)(2,1)S(1)}, bf16[240,768]{1,0:T(8,128)(2,1)S(1)}, u32[]{:S(2)}, u32[]{:S(2)}) %collective-permute-start.59) | collective-permute-done | bytes 368672 | tf_op jit(solution)/shard_map/ppermute | solution.py:35
  232.4 6.9 %collective-permute-start.69 = (bf16[192,768]{1,0:T(8,128)(2,1)S(1)}, bf16[192,768]{1,0:T(8,128)(2,1)S(1)}, u32[]{:S(2)}, u32[]{:S(2)}) collective-permute-start(bf16[192,768]{1,0:T(8,128)(2,1)S(1)} %add_convert_fusion.2), channel_id=1, source_target_pairs={{0,8},{1,9},{2,10},{3,11},{4,12},{5,13},{6,14},{7,15},{8,0},{9,1},... | collective-permute-start | bytes 884744 | tf_op jit(solution)/shard_map/ppermute | solution.py:35
  242.0 3.9 %collective-permute-start.61 = (bf16[160,768]{1,0:T(8,128)(2,1)S(1)}, bf16[160,768]{1,0:T(8,128)(2,1)S(1)}, u32[]{:S(2)}, u32[]{:S(2)}) collective-permute-start(bf16[160,768]{1,0:T(8,128)(2,1)S(1)} %select_convert_fusion.4), channel_id=1, source_target_pairs={{0,8},{1,9},{2,10},{3,11},{4,12},{5,13},{6,14},{7,15},{8,0},{9,1},... | collective-permute-start | bytes 737288 | tf_op jit(solution)/shard_map/ppermute | solution.py:35
  249.2 1.9 collective-permute-done.61
  255.3 2.6 collective-permute-done.67
  259.2 5.2 %collective-permute-done.64 = bf16[160,768]{1,0:T(8,128)(2,1)S(1)} collective-permute-done((bf16[160,768]{1,0:T(8,128)(2,1)S(1)}, bf16[160,768]{1,0:T(8,128)(2,1)S(1)}, u32[]{:S(2)}, u32[]{:S(2)}) %collective-permute-start.64) | collective-permute-done | bytes 245792 | tf_op jit(solution)/shard_map/ppermute | solution.py:35
  264.5 3.3 %collective-permute-start.65 = (bf16[160,768]{1,0:T(8,128)(2,1)S(1)}, bf16[160,768]{1,0:T(8,128)(2,1)S(1)}, u32[]{:S(2)}, u32[]{:S(2)}) collective-permute-start(bf16[160,768]{1,0:T(8,128)(2,1)S(1)} %add_convert_fusion.4), channel_id=1, source_target_pairs={{0,8},{1,9},{2,10},{3,11},{4,12},{5,13},{6,14},{7,15},{8,0},{9,1},... | collective-permute-start | bytes 737288 | tf_op jit(solution)/shard_map/ppermute | solution.py:35
  267.8 8.1 %collective-permute-done.66 = bf16[240,768]{1,0:T(8,128)(2,1)S(1)} collective-permute-done((bf16[240,768]{1,0:T(8,128)(2,1)S(1)}, bf16[240,768]{1,0:T(8,128)(2,1)S(1)}, u32[]{:S(2)}, u32[]{:S(2)}) %collective-permute-start.66) | collective-permute-done | bytes 368672 | tf_op jit(solution)/shard_map/ppermute | solution.py:35
  (343 shorter events, 81.3 us)
Async XLA Ops:
  0.7 31.4 %collective-permute-start.4 = (bf16[256,768]{1,0:T(8,128)(2,1)}, bf16[256,768]{1,0:T(8,128)(2,1)}, u32[]{:S(2)}, u32[]{:S(2)}) collective-permute-start(bf16[256,768]{1,0:T(8,128)(2,1)} %bitcast.197), channel_id=1, source_target_pairs={{0,6},{1,7},{2,4},{3,5},{4,2},{5,3},{6,0},{7,1},{8,14},{9,15},{10,... | collective-permute-start | bytes 1179656 | tf_op jit(solution)/shard_map/ppermute | solution.py:35
  4.7 28.8 %collective-permute-start.3 = (bf16[256,768]{1,0:T(8,128)(2,1)}, bf16[256,768]{1,0:T(8,128)(2,1)}, u32[]{:S(2)}, u32[]{:S(2)}) collective-permute-start(bf16[256,768]{1,0:T(8,128)(2,1)} %bitcast.198), channel_id=1, source_target_pairs={{0,4},{1,5},{2,6},{3,7},{4,0},{5,1},{6,2},{7,3},{8,12},{9,13},{10,... | collective-permute-start | bytes 1179656 | tf_op jit(solution)/shard_map/ppermute | solution.py:35
  8.2 20.6 %collective-permute-start.6 = (bf16[3,96,192]{2,1,0:T(8,128)(2,1)S(1)}, bf16[3,96,192]{2,1,0:T(8,128)(2,1)S(1)}, u32[]{:S(2)}, u32[]{:S(2)}) collective-permute-start(bf16[3,96,192]{2,1,0:T(8,128)(2,1)S(1)} %get-tuple-element.397), channel_id=1, source_target_pairs={{0,4},{1,5},{2,6},{3,7},{4,0},{5,1},{6,2},{7,3},{8,12},{9,13},{10,... | collective-permute-start | bytes 331784 | tf_op jit(solution)/shard_map/ppermute | solution.py:35
  8.3 20.6 %collective-permute-start.5 = (bf16[3,96,192]{2,1,0:T(8,128)(2,1)S(1)}, bf16[3,96,192]{2,1,0:T(8,128)(2,1)S(1)}, u32[]{:S(2)}, u32[]{:S(2)}) collective-permute-start(bf16[3,96,192]{2,1,0:T(8,128)(2,1)S(1)} %get-tuple-element.398), channel_id=1, source_target_pairs={{0,2},{1,3},{2,0},{3,1},{4,6},{5,7},{6,4},{7,5},{8,10},{9,11},{10,... | collective-permute-start | bytes 331784 | tf_op jit(solution)/shard_map/ppermute | solution.py:35
  18.0 15.5 %collective-permute-start.2 = (bf16[256,768]{1,0:T(8,128)(2,1)S(1)}, bf16[256,768]{1,0:T(8,128)(2,1)}, u32[]{:S(2)}, u32[]{:S(2)}) collective-permute-start(bf16[256,768]{1,0:T(8,128)(2,1)S(1)} %bitcast.202), channel_id=1, source_target_pairs={{0,2},{1,3},{2,0},{3,1},{4,6},{5,7},{6,4},{7,5},{8,10},{9,11},{10,... | collective-permute-start | bytes 1179656 | tf_op jit(solution)/shard_map/ppermute | solution.py:35
  30.3 18.7 %collective-permute-start = (bf16[480,768]{1,0:T(8,128)(2,1)S(1)}, bf16[480,768]{1,0:T(8,128)(2,1)}, u32[]{:S(2)}, u32[]{:S(2)}) collective-permute-start(bf16[480,768]{1,0:T(8,128)(2,1)S(1)} %constant_dynamic-update-slice_fusion.refs_0_), channel_id=1, source_target_pairs={{0,4},{1,5},{2,6},{3,7},{4,0},{5,1},{6,2},{7,3},{8,10},{9,11},{10,... | collective-permute-start | bytes 2211848 | tf_op jit(solution)/shard_map/ppermute | solution.py:35
  32.0 18.3 %collective-permute-start.10 = (bf16[5,96,768]{2,1,0:T(8,128)(2,1)S(1)}, bf16[5,96,768]{2,1,0:T(8,128)(2,1)}, u32[]{:S(2)}, u32[]{:S(2)}) collective-permute-start(bf16[5,96,768]{2,1,0:T(8,128)(2,1)S(1)} %pad_maximum_fusion.refs_0_), channel_id=1, source_target_pairs={{0,2},{1,3},{2,0},{3,1},{4,6},{5,7},{6,4},{7,5},{8,12},{9,13},{10,... | collective-permute-start | bytes 2211848 | tf_op jit(solution)/shard_map/ppermute | solution.py:35
  33.5 45.9 %collective-permute-start.19 = (bf16[5,96,768]{2,1,0:T(8,128)(2,1)S(1)}, bf16[5,96,768]{2,1,0:T(8,128)(2,1)}, u32[]{:S(2)}, u32[]{:S(2)}) collective-permute-start(bf16[5,96,768]{2,1,0:T(8,128)(2,1)S(1)} %pad_maximum_fusion.refs_0_), channel_id=1, source_target_pairs={{0,1},{1,0},{2,3},{3,2},{4,5},{5,4},{6,7},{7,6},{8,9},{9,8},{10,11... | collective-permute-start | bytes 2211848 | tf_op jit(solution)/shard_map/ppermute | solution.py:35
  54.1 22.9 %collective-permute-start.18 = (bf16[5,96,768]{2,1,0:T(8,128)(2,1)}, bf16[5,96,768]{2,1,0:T(8,128)(2,1)}, u32[]{:S(2)}, u32[]{:S(2)}) collective-permute-start(bf16[5,96,768]{2,1,0:T(8,128)(2,1)} %collective-permute-done.10.refs_1_), channel_id=1, source_target_pairs={{0,8},{1,9},{2,10},{3,11},{4,12},{5,13},{6,14},{7,15},{8,0},{9,1},... | collective-permute-start | bytes 2211848 | tf_op jit(solution)/shard_map/ppermute | solution.py:35
  55.7 18.4 %collective-permute-start.1 = (bf16[480,768]{1,0:T(8,128)(2,1)}, bf16[480,768]{1,0:T(8,128)(2,1)}, u32[]{:S(2)}, u32[]{:S(2)}) collective-permute-start(bf16[480,768]{1,0:T(8,128)(2,1)} %collective-permute-done.refs_1_), channel_id=1, source_target_pairs={{0,2},{1,3},{2,0},{3,1},{4,6},{5,7},{6,4},{7,5},{8,12},{9,13},{10,... | collective-permute-start | bytes 2211848 | tf_op jit(solution)/shard_map/ppermute | solution.py:35
  56.2 24.7 %collective-permute-start.20 = (bf16[5,96,768]{2,1,0:T(8,128)(2,1)}, bf16[5,96,768]{2,1,0:T(8,128)(2,1)}, u32[]{:S(2)}, u32[]{:S(2)}) collective-permute-start(bf16[5,96,768]{2,1,0:T(8,128)(2,1)} %collective-permute-done.10.refs_1_), channel_id=1, source_target_pairs={{0,1},{1,0},{2,3},{3,2},{4,5},{5,4},{6,7},{7,6},{8,9},{9,8},{10,11... | collective-permute-start | bytes 2211848 | tf_op jit(solution)/shard_map/ppermute | solution.py:35
  56.2 19.2 %collective-permute-start.17 = (bf16[5,96,768]{2,1,0:T(8,128)(2,1)}, bf16[5,96,768]{2,1,0:T(8,128)(2,1)}, u32[]{:S(2)}, u32[]{:S(2)}) collective-permute-start(bf16[5,96,768]{2,1,0:T(8,128)(2,1)} %collective-permute-done.10.refs_1_), channel_id=1, source_target_pairs={{0,4},{1,5},{2,6},{3,7},{4,0},{5,1},{6,2},{7,3},{8,10},{9,11},{10,... | collective-permute-start | bytes 2211848 | tf_op jit(solution)/shard_map/ppermute | solution.py:35
  77.0 16.3 %collective-permute-start.22 = (bf16[5,96,768]{2,1,0:T(8,128)(2,1)}, bf16[5,96,768]{2,1,0:T(8,128)(2,1)S(1)}, u32[]{:S(2)}, u32[]{:S(2)}) collective-permute-start(bf16[5,96,768]{2,1,0:T(8,128)(2,1)} %collective-permute-done.18.refs_3_), channel_id=1, source_target_pairs={{0,1},{1,0},{2,3},{3,2},{4,5},{5,4},{6,7},{7,6},{8,9},{9,8},{10,11... | collective-permute-start | bytes 2211848 | tf_op jit(solution)/shard_map/ppermute | solution.py:35
  77.0 19.2 %collective-permute-start.12 = (bf16[480,768]{1,0:T(8,128)(2,1)}, bf16[480,768]{1,0:T(8,128)(2,1)}, u32[]{:S(2)}, u32[]{:S(2)}) collective-permute-start(bf16[480,768]{1,0:T(8,128)(2,1)} %collective-permute-done.refs_1_), channel_id=1, source_target_pairs={{0,8},{1,9},{2,10},{3,11},{4,12},{5,13},{6,14},{7,15},{8,0},{9,1},... | collective-permute-start | bytes 2211848 | tf_op jit(solution)/shard_map/ppermute | solution.py:35
  79.4 16.9 %collective-permute-start.21 = (bf16[5,96,768]{2,1,0:T(8,128)(2,1)}, bf16[5,96,768]{2,1,0:T(8,128)(2,1)}, u32[]{:S(2)}, u32[]{:S(2)}) collective-permute-start(bf16[5,96,768]{2,1,0:T(8,128)(2,1)} %collective-permute-done.17.refs_2_), channel_id=1, source_target_pairs={{0,1},{1,0},{2,3},{3,2},{4,5},{5,4},{6,7},{7,6},{8,9},{9,8},{10,11... | collective-permute-start | bytes 2211848 | tf_op jit(solution)/shard_map/ppermute | solution.py:35
  92.8 17.2 %collective-permute-start.13 = (bf16[480,768]{1,0:T(8,128)(2,1)S(1)}, bf16[480,768]{1,0:T(8,128)(2,1)S(1)}, u32[]{:S(2)}, u32[]{:S(2)}) collective-permute-start(bf16[480,768]{1,0:T(8,128)(2,1)S(1)} %constant_dynamic-update-slice_fusion.refs_0_), channel_id=1, source_target_pairs={{0,1},{1,0},{2,3},{3,2},{4,5},{5,4},{6,7},{7,6},{8,9},{9,8},{10,11... | collective-permute-start | bytes 2211848 | tf_op jit(solution)/shard_map/ppermute | solution.py:35
  92.8 17.1 %collective-permute-start.14 = (bf16[480,768]{1,0:T(8,128)(2,1)}, bf16[480,768]{1,0:T(8,128)(2,1)S(1)}, u32[]{:S(2)}, u32[]{:S(2)}) collective-permute-start(bf16[480,768]{1,0:T(8,128)(2,1)} %collective-permute-done.refs_1_), channel_id=1, source_target_pairs={{0,1},{1,0},{2,3},{3,2},{4,5},{5,4},{6,7},{7,6},{8,9},{9,8},{10,11... | collective-permute-start | bytes 2211848 | tf_op jit(solution)/shard_map/ppermute | solution.py:35
  93.3 16.7 %collective-permute-start.15 = (bf16[480,768]{1,0:T(8,128)(2,1)}, bf16[480,768]{1,0:T(8,128)(2,1)S(1)}, u32[]{:S(2)}, u32[]{:S(2)}) collective-permute-start(bf16[480,768]{1,0:T(8,128)(2,1)} %collective-permute-done.1.refs_2_), channel_id=1, source_target_pairs={{0,1},{1,0},{2,3},{3,2},{4,5},{5,4},{6,7},{7,6},{8,9},{9,8},{10,11... | collective-permute-start | bytes 2211848 | tf_op jit(solution)/shard_map/ppermute | solution.py:35
  127.5 19.0 %collective-permute-start.31 = (bf16[2,192,768]{2,1,0:T(8,128)(2,1)}, bf16[2,192,768]{2,1,0:T(8,128)(2,1)S(1)}, u32[]{:S(2)}, u32[]{:S(2)}) collective-permute-start(bf16[2,192,768]{2,1,0:T(8,128)(2,1)} %get-tuple-element.176), channel_id=1, source_target_pairs={{0,2},{1,3},{2,0},{3,1},{4,6},{5,7},{6,4},{7,5},{8,10},{9,11},{10,... | collective-permute-start | bytes 1769480 | tf_op jit(solution)/shard_map/ppermute | solution.py:35
  128.0 18.5 %collective-permute-start.32 = (bf16[2,192,768]{2,1,0:T(8,128)(2,1)}, bf16[2,192,768]{2,1,0:T(8,128)(2,1)S(1)}, u32[]{:S(2)}, u32[]{:S(2)}) collective-permute-start(bf16[2,192,768]{2,1,0:T(8,128)(2,1)} %get-tuple-element.177), channel_id=1, source_target_pairs={{0,4},{1,5},{2,6},{3,7},{4,0},{5,1},{6,2},{7,3},{8,12},{9,13},{10,... | collective-permute-start | bytes 1769480 | tf_op jit(solution)/shard_map/ppermute | solution.py:35
  162.5 23.3 %collective-permute-start.41 = (f32[8,3968]{1,0:T(8,128)S(1)}, f32[8,3968]{1,0:T(8,128)S(1)}, u32[]{:S(2)}, u32[]{:S(2)}) collective-permute-start(f32[8,3968]{1,0:T(8,128)S(1)} %pad_maximum_fusion.6), channel_id=1, source_target_pairs={{0,1},{1,0},{2,3},{3,2},{4,5},{5,4},{6,7},{7,6},{8,9},{9,8},{10,11... | collective-permute-start | bytes 380936 | tf_op jit(solution)/shard_map/ppermute | solution.py:35
  162.9 22.9 %collective-permute-start.42 = (bf16[192,768]{1,0:T(8,128)(2,1)S(1)}, bf16[192,768]{1,0:T(8,128)(2,1)S(1)}, u32[]{:S(2)}, u32[]{:S(2)}) collective-permute-start(bf16[192,768]{1,0:T(8,128)(2,1)S(1)} %select_convert_fusion.2), channel_id=1, source_target_pairs={{0,8},{1,9},{2,10},{3,11},{4,12},{5,13},{6,14},{7,15},{8,0},{9,1},... | collective-permute-start | bytes 884744 | tf_op jit(solution)/shard_map/ppermute | solution.py:35
  163.7 22.2 %collective-permute-start.43 = (bf16[2,240,768]{2,1,0:T(8,128)(2,1)S(1)}, bf16[2,240,768]{2,1,0:T(8,128)(2,1)S(1)}, u32[]{:S(2)}, u32[]{:S(2)}) collective-permute-start(bf16[2,240,768]{2,1,0:T(8,128)(2,1)S(1)} %copy-done.43), channel_id=1, source_target_pairs={{0,2},{1,3},{2,0},{3,1},{4,6},{5,7},{6,4},{7,5},{8,10},{9,11},{10,... | collective-permute-start | bytes 2211848 | tf_op jit(solution)/shard_map/ppermute | solution.py:35
  165.2 20.7 %collective-permute-start.44 = (bf16[2,240,768]{2,1,0:T(8,128)(2,1)S(1)}, bf16[2,240,768]{2,1,0:T(8,128)(2,1)S(1)}, u32[]{:S(2)}, u32[]{:S(2)}) collective-permute-start(bf16[2,240,768]{2,1,0:T(8,128)(2,1)S(1)} %copy-done.42), channel_id=1, source_target_pairs={{0,4},{1,5},{2,6},{3,7},{4,0},{5,1},{6,2},{7,3},{8,12},{9,13},{10,... | collective-permute-start | bytes 2211848 | tf_op jit(solution)/shard_map/ppermute | solution.py:35
  185.9 20.1 %collective-permute-start.46 = (f32[8,3968]{1,0:T(8,128)S(1)}, f32[8,3968]{1,0:T(8,128)S(1)}, u32[]{:S(2)}, u32[]{:S(2)}) collective-permute-start(f32[8,3968]{1,0:T(8,128)S(1)} %add.283), channel_id=1, source_target_pairs={{0,2},{1,3},{2,0},{3,1},{4,6},{5,7},{6,4},{7,5},{8,10},{9,11},{10,... | collective-permute-start | bytes 380936 | tf_op jit(solution)/shard_map/ppermute | solution.py:35
  187.5 18.5 %collective-permute-start.49 = (bf16[192,768]{1,0:T(8,128)(2,1)S(1)}, bf16[192,768]{1,0:T(8,128)(2,1)S(1)}, u32[]{:S(2)}, u32[]{:S(2)}) collective-permute-start(bf16[192,768]{1,0:T(8,128)(2,1)S(1)} %add_convert_fusion.3), channel_id=1, source_target_pairs={{0,24},{1,25},{2,26},{3,27},{4,28},{5,29},{6,30},{7,31},{8,16},{9,... | collective-permute-start | bytes 884744 | tf_op jit(solution)/shard_map/ppermute | solution.py:35
  220.2 19.1 %collective-permute-start.58 = (bf16[2,128,768]{2,1,0:T(8,128)(2,1)S(1)}, bf16[2,128,768]{2,1,0:T(8,128)(2,1)S(1)}, u32[]{:S(2)}, u32[]{:S(2)}) collective-permute-start(bf16[2,128,768]{2,1,0:T(8,128)(2,1)S(1)} %copy-done.48), channel_id=1, source_target_pairs={{0,4},{1,5},{2,6},{3,7},{4,0},{5,1},{6,2},{7,3},{8,12},{9,13},{10,... | collective-permute-start | bytes 1179656 | tf_op jit(solution)/shard_map/ppermute | solution.py:35
  221.0 18.3 %collective-permute-start.55 = (bf16[3,96,192]{2,1,0:T(8,128)(2,1)S(1)}, bf16[3,96,192]{2,1,0:T(8,128)(2,1)S(1)}, u32[]{:S(2)}, u32[]{:S(2)}) collective-permute-start(bf16[3,96,192]{2,1,0:T(8,128)(2,1)S(1)} %bitcast.175), channel_id=1, source_target_pairs={{0,4},{1,5},{2,6},{3,7},{4,0},{5,1},{6,2},{7,3},{8,12},{9,13},{10,... | collective-permute-start | bytes 331784 | tf_op jit(solution)/shard_map/ppermute | solution.py:35
  222.6 16.7 %collective-permute-start.56 = (bf16[3,96,192]{2,1,0:T(8,128)(2,1)S(1)}, bf16[3,96,192]{2,1,0:T(8,128)(2,1)S(1)}, u32[]{:S(2)}, u32[]{:S(2)}) collective-permute-start(bf16[3,96,192]{2,1,0:T(8,128)(2,1)S(1)} %bitcast.174), channel_id=1, source_target_pairs={{0,6},{1,7},{2,4},{3,5},{4,2},{5,3},{6,0},{7,1},{8,14},{9,15},{10,... | collective-permute-start | bytes 331784 | tf_op jit(solution)/shard_map/ppermute | solution.py:35
  255.2 20.7 %collective-permute-start.66 = (bf16[240,768]{1,0:T(8,128)(2,1)S(1)}, bf16[240,768]{1,0:T(8,128)(2,1)S(1)}, u32[]{:S(2)}, u32[]{:S(2)}) collective-permute-start(bf16[240,768]{1,0:T(8,128)(2,1)S(1)} %add_convert_fusion), channel_id=1, source_target_pairs={{0,8},{1,9},{2,10},{3,11},{4,12},{5,13},{6,14},{7,15},{8,0},{9,1},... | collective-permute-start | bytes 1105928 | tf_op jit(solution)/shard_map/ppermute | solution.py:35
  257.9 20.1 %collective-permute-start.68 = (f32[16,3968]{1,0:T(8,128)S(1)}, f32[16,3968]{1,0:T(8,128)S(1)}, u32[]{:S(2)}, u32[]{:S(2)}) collective-permute-start(f32[16,3968]{1,0:T(8,128)S(1)} %pad_maximum_fusion.5), channel_id=1, source_target_pairs={{0,16},{1,17},{2,18},{3,19},{4,20},{5,21},{6,22},{7,23},{8,24},{9,... | collective-permute-start | bytes 761864 | tf_op jit(solution)/shard_map/ppermute | solution.py:35
  264.5 19.1 %collective-permute-start.65 = (bf16[160,768]{1,0:T(8,128)(2,1)S(1)}, bf16[160,768]{1,0:T(8,128)(2,1)S(1)}, u32[]{:S(2)}, u32[]{:S(2)}) collective-permute-start(bf16[160,768]{1,0:T(8,128)(2,1)S(1)} %add_convert_fusion.4), channel_id=1, source_target_pairs={{0,8},{1,9},{2,10},{3,11},{4,12},{5,13},{6,14},{7,15},{8,0},{9,1},... | collective-permute-start | bytes 737288 | tf_op jit(solution)/shard_map/ppermute | solution.py:35
  (101 other events, 896.6 us)
